TPU v7x, 32 devices: a whole 2x2x4 slice. The times are simulated.
32 devices in a mesh: grp: 4 (over z), seq: 8 (over y, x, core).
Axes of the slice: x: 2, y: 2, z: 4, core: 2. Of those that a mesh axis runs over, the one named last changes fastest.
Arguments:
- queries: bfloat16 [4096, 1232], P(('grp', 'seq')), may hold values from -6 to 6
- key_vectors: bfloat16 [4096, 1232], P(('grp', 'seq')), may hold values from -6 to 6
- value_vectors: bfloat16 [4096, 1232], P(('grp', 'seq')), may hold values from -1 to 3
- output_grad: bfloat16 [4096, 1232], P(('grp', 'seq')), may hold values from -4096 to 4096
- state_in: float32 [11, 112, 112], replicated, may hold values from 38.4 to 64
- norm_in: float32 [11, 112], replicated, may hold values from 38.4 to 64
- grad_state: float32 [11, 112, 112], replicated, may hold values from -1 to 1
- grad_norm: float32 [11, 112], replicated, may hold values from -12 to 12
Outputs:
- query_grad: bfloat16 [4096, 1232], P(('grp', 'seq'))
- key_grad: bfloat16 [4096, 1232], P(('grp', 'seq'))
- value_grad: bfloat16 [4096, 1232], P(('grp', 'seq'))
All inputs are finite; a program needn't handle non-finite values.
Results may differ from a plain program's by a relative error of at most 0.006.
Values sent between devices are 32-bit elements; how exact they have to be, the bound alone decides.
No kernel may reach another device: no remote copies, remote signals or barrier semaphores. Data moves between devices by JAX's collectives and lax.ppermute only.
A program may use at most 128 MiB of HBM per device.

v0:
```python
import jax
import jax.numpy as jnp
from jax import lax
from jax.sharding import PartitionSpec as P


def entering(x, axis, combine, identity, reverse):
    length, index = (lax.axis_size(axis), lax.axis_index(axis))
    everything = jax.tree.map(lambda part: lax.all_gather(part, axis), x)
    start = jax.tree.map(
        lambda part, zero: jnp.broadcast_to(jnp.asarray(zero, part.dtype), part.shape), x, identity
    )

    def step(k, before):
        at = length - 1 - k if reverse else k
        reached = at > index if reverse else at < index
        new = combine(before, jax.tree.map(lambda part: part[at], everything))
        return jax.tree.map(lambda a, b: jnp.where(reached, a, b), new, before)

    return lax.fori_loop(0, length, step, start)


def combine_sums(earlier, later):
    return jax.tree.map(jnp.add, earlier, later)


def select_groups(stacked, weights):
    state_all, norm_all = stacked
    return (
        jnp.einsum("g,ghde->hde", weights, state_all, precision=lax.Precision.HIGHEST),
        jnp.einsum("g,ghd->hd", weights, norm_all, precision=lax.Precision.HIGHEST),
    )


def per_device(
    queries, key_vectors, value_vectors, output_grad, state_in, norm_in, grad_state, grad_norm
):
    highest = lax.Precision.HIGHEST
    length = queries.shape[0]
    heads = state_in.shape[0]
    width = state_in.shape[1]
    groups = lax.axis_size("grp")
    group_index = lax.axis_index("grp")
    group_ids = lax.iota(jnp.int32, groups)
    query_feat = jnp.maximum(queries, 0).reshape(length, heads, width)
    key_feat = jnp.maximum(key_vectors, 0).reshape(length, heads, width)
    value_heads = value_vectors.reshape(length, heads, width)
    query_wide = query_feat.astype(jnp.float32)
    key_wide = key_feat.astype(jnp.float32)
    value_wide = value_heads.astype(jnp.float32)
    block_state = jnp.einsum(
        "thd,the->hde", key_feat, value_heads, preferred_element_type=jnp.float32
    )
    block_norm = jnp.sum(key_wide, axis=0)
    empty = (jnp.zeros_like(block_state), jnp.zeros_like(block_norm))
    inner = entering((block_state, block_norm), "seq", combine_sums, empty, False)
    group_total = lax.psum((block_state, block_norm), "seq")
    every_group = (
        lax.all_gather(group_total[0][None], "grp", axis=0, tiled=True),
        lax.all_gather(group_total[1][None], "grp", axis=0, tiled=True),
    )
    outer = select_groups(every_group, (group_ids < group_index).astype(jnp.float32))
    prefix_state = state_in + outer[0] + inner[0]
    prefix_norm = norm_in + outer[1] + inner[1]
    positions = lax.iota(jnp.int32, length)
    causal = (positions[:, None] >= positions[None, :])[None]
    scores = jnp.einsum("thd,shd->hts", query_feat, key_feat, preferred_element_type=jnp.float32)
    masked = jnp.where(causal, scores, 0.0)
    denominator = (
        1.0
        + jnp.einsum("thd,hd->ht", query_wide, prefix_norm, precision=highest)
        + jnp.sum(masked, axis=2)
    )
    scores_low = masked.astype(jnp.bfloat16)
    numerator = jnp.einsum(
        "thd,hde->hte", query_wide, prefix_state, precision=highest
    ) + jnp.einsum("hts,she->hte", scores_low, value_heads, preferred_element_type=jnp.float32)
    output = numerator / denominator[:, :, None]
    grad_wide = output_grad.reshape(length, heads, width).astype(jnp.float32).transpose(1, 0, 2)
    num_grad = grad_wide / denominator[:, :, None]
    den_grad = -jnp.sum(grad_wide * output, axis=2) / denominator
    num_grad_low = num_grad.astype(jnp.bfloat16)
    carry_state = jnp.einsum(
        "thd,hte->hde", query_feat, num_grad_low, preferred_element_type=jnp.float32
    )
    carry_sum = jnp.einsum("thd,ht->hd", query_wide, den_grad, precision=highest)
    inner_back = entering((carry_state, carry_sum), "seq", combine_sums, empty, True)
    group_back = lax.psum((carry_state, carry_sum), "seq")
    every_back = (
        lax.all_gather(group_back[0][None], "grp", axis=0, tiled=True),
        lax.all_gather(group_back[1][None], "grp", axis=0, tiled=True),
    )
    outer_back = select_groups(every_back, (group_ids > group_index).astype(jnp.float32))
    suffix_state = grad_state + outer_back[0] + inner_back[0]
    suffix_norm = grad_norm + outer_back[1] + inner_back[1]
    mixed = (
        jnp.einsum("hte,she->hts", num_grad_low, value_heads, preferred_element_type=jnp.float32)
        + den_grad[:, :, None]
    )
    mixed_low = jnp.where(causal, mixed, 0.0).astype(jnp.bfloat16)
    query_part = (
        jnp.einsum("hte,hde->htd", num_grad, prefix_state, precision=highest)
        + den_grad[:, :, None] * prefix_norm[:, None, :]
        + jnp.einsum("hts,shd->htd", mixed_low, key_feat, preferred_element_type=jnp.float32)
    )
    key_part = (
        jnp.einsum("she,hde->hsd", value_wide, suffix_state, precision=highest)
        + suffix_norm[:, None, :]
        + jnp.einsum("hts,thd->hsd", mixed_low, query_feat, preferred_element_type=jnp.float32)
    )
    value_part = jnp.einsum("shd,hde->hse", key_wide, suffix_state, precision=highest) + jnp.einsum(
        "hts,hte->hse", scores_low, num_grad_low, preferred_element_type=jnp.float32
    )

    def to_tokens(part):
        return part.transpose(1, 0, 2).reshape(length, heads * width)

    query_grad = jnp.where(queries > 0, to_tokens(query_part), 0.0).astype(jnp.bfloat16)
    key_grad = jnp.where(key_vectors > 0, to_tokens(key_part), 0.0).astype(jnp.bfloat16)
    value_grad = to_tokens(value_part).astype(jnp.bfloat16)
    return (query_grad, key_grad, value_grad)


def solution(mesh):
    in_specs = (
        P(("grp", "seq"), None),
        P(("grp", "seq"), None),
        P(("grp", "seq"), None),
        P(("grp", "seq"), None),
        P(),
        P(),
        P(),
        P(),
    )
    out_specs = (P(("grp", "seq"), None), P(("grp", "seq"), None), P(("grp", "seq"), None))
    return jax.shard_map(
        per_device, mesh=mesh, in_specs=in_specs, out_specs=out_specs, check_vma=False
    )
```

profile of v0, /device:TPU:0, one launch (start us, length us, event | category | flops | bytes accessed | tf_op | source)
XLA Modules:
  0.0 294.5 jit_solution(12768337966284812017)
XLA Ops:
  7.2 1.1 broadcast_maximum_fusion
  8.3 1.2 fusion.56
  9.9 15.7 %psum.28 = f32[1,11,112]{2,1,0:T(8,128)S(1)} all-reduce(f32[1,11,112]{2,1,0:T(8,128)S(1)} %broadcast_in_dim.50), channel_id=1, replica_groups=mesh['grp'=4,'seq'=8] {'seq'}, use_global_device_ids=true, to_apply=%region_1.2 | all-reduce | flops 1232 | bytes 9856 | tf_op jit(solution)/shard_map/psum | solution.py:57
  25.6 13.4 %all_gather.36 = f32[4,11,112]{2,1,0:T(8,128)S(1)} all-gather(f32[1,11,112]{2,1,0:T(8,128)S(1)} %psum.28), channel_id=1, replica_groups=mesh['grp'=4,'seq'=8] {'grp'}, dimensions={0}, use_global_device_ids=true | all-gather | bytes 24640 | tf_op jit(solution)/shard_map/all_gather | solution.py:60
  38.9 8.4 %all_gather.40 = f32[8,11,112]{2,1,0:T(8,128)S(1)} all-gather(f32[1,11,112]{2,1,0:T(8,128)S(1)} %broadcast_in_dim.50), channel_id=1, replica_groups=mesh['grp'=4,'seq'=8] {'seq'}, dimensions={0}, use_global_device_ids=true | all-gather | bytes 44352 | tf_op jit(solution)/shard_map/all_gather | solution.py:9
  47.6 0.3 fusion.55
  47.9 5.2 %all-gather.13.cloned.1.call-done = f32[88,112,112]{2,1,0:T(8,128)} async-done(((f32[11,112,112]{2,1,0:T(8,128)}), f32[88,112,112]{2,1,0:T(8,128)}) %all-gather.13.cloned.1.call-update) | async-done | bytes 4415504 | tf_op jit(solution)/shard_map/all_gather | solution.py:9
  53.2 10.5 %while.34 = (s32[]{:T(128)}, f32[11,112,112]{2,1,0:T(8,128)S(1)}, f32[11,112]{1,0:T(8,128)S(1)}, s32[]{:T(128)}, f32[8,11,112,112]{3,2,1,0:T(8,128)}, /*index=5*/f32[8,11,112]{2,1,0:T(8,128)S(1)}, s32[]{:T(128)}, s32[]{:T(128)}) while((s32[]{:T(128)}, f32[11,112,112]{2,1,0:T(8,128)S(1)}, f32[11,112]{1,0:T(8,128)S(1)}, s32[]{:T(128)}, ...), condition=%wide.region_3.4_spmd.clone, body=%wide.region_2.3_spmd.clone.sunk | while | flops 417652 | bytes 1670707 | solution.py:20
  53.2 1.3 add_select_fusion.8
  54.5 1.3 add_select_fusion.8
  55.8 1.3 add_select_fusion.8
  57.1 1.3 add_select_fusion.8
  58.4 1.3 add_select_fusion.8
  59.7 1.3 add_select_fusion.8
  61.1 1.3 add_select_fusion.8
  62.4 1.3 add_select_fusion.8
  63.7 0.4 fusion.33
  64.0 1.2 fusion.52
  65.2 40.3 %all-gather.15.cloned.1.call-done = f32[88,112,112]{2,1,0:T(8,128)} async-done(((f32[11,112,112]{2,1,0:T(8,128)}), f32[88,112,112]{2,1,0:T(8,128)}) %all-gather.15.cloned.1.call-update) | async-done | bytes 4415504 | tf_op jit(solution)/shard_map/all_gather | solution.py:9
  105.6 0.7 all-reduce.3.cloned.1.call-update
  106.3 61.0 %all-reduce.3.cloned.1.call-done = (f32[1,11,112,112]{3,2,1,0:T(8,128)}, f32[1,11,112,112]{3,2,1,0:T(8,128)}) async-done(((f32[1,11,112,112]{3,2,1,0:T(8,128)}, f32[1,11,112,112]{3,2,1,0:T(8,128)}), (f32[1,11,112,112]{3,2,1,0:T(8,128)}, f32[1,11,112,112]{3,2,1,0:T(8,128)})) %all-reduce.3.cloned.1.call-update) | async-done | bytes 1103888 | tf_op jit(solution)/shard_map/psum | solution.py:57
  167.5 0.3 fusion.22
  167.8 2.2 fusion.20
  170.0 51.2 %all-gather.9.cloned.1.call-done = f32[4,11,112,112]{3,2,1,0:T(8,128)} async-done(((f32[1,11,112,112]{3,2,1,0:T(8,128)}), f32[4,11,112,112]{3,2,1,0:T(8,128)}) %all-gather.9.cloned.1.call-update) | async-done | bytes 2207760 | tf_op jit(solution)/shard_map/all_gather | solution.py:59
  221.2 4.8 %fusion.2 = f32[1,11,112,112]{3,0,2,1:T(1,128)S(1)} fusion(f32[4,11,112,112]{3,2,1,0:T(8,128)} %all-gather.9.cloned.1.call-done, s32[]{:T(128)S(6)} %axis_index.27), kind=kOutput, calls=%fused_computation.6 | convolution fusion | flops 6623236 | bytes 2759684 | tf_op jit(solution)/shard_map/g,ghde->hde/dot_general | solution.py:30
  226.0 0.9 copy-done.7
  226.9 0.8 fusion.13
  227.7 0.6 fusion.31
  228.3 9.2 %all-gather.3 = f32[8,11,112]{2,1,0:T(8,128)S(1)} all-gather(f32[1,11,112]{2,1,0:T(8,128)S(1)} %bitcast.142), channel_id=4, replica_groups=mesh['grp'=4,'seq'=8] {'seq'}, dimensions={0}, use_global_device_ids=true | all-gather | bytes 44352 | tf_op jit(solution)/shard_map/all_gather | solution.py:9
  237.5 14.2 %psum.31 = f32[1,11,112]{2,1,0:T(8,128)S(1)} all-reduce(f32[1,11,112]{2,1,0:T(8,128)S(1)} %bitcast.143), channel_id=1, replica_groups=mesh['grp'=4,'seq'=8] {'seq'}, use_global_device_ids=true, to_apply=%region_10.11 | all-reduce | flops 1232 | bytes 9856 | tf_op jit(solution)/shard_map/psum | solution.py:88
  251.7 14.1 %all_gather.47 = f32[4,11,112]{2,1,0:T(8,128)S(1)} all-gather(f32[1,11,112]{2,1,0:T(8,128)S(1)} %psum.31), channel_id=1, replica_groups=mesh['grp'=4,'seq'=8] {'grp'}, dimensions={0}, use_global_device_ids=true | all-gather | bytes 24640 | tf_op jit(solution)/shard_map/all_gather | solution.py:91
  266.0 10.6 %while.35 = (s32[]{:T(128)}, f32[11,112,112]{2,1,0:T(8,128)S(1)}, f32[11,112]{1,0:T(8,128)S(1)}, s32[]{:T(128)}, f32[8,11,112,112]{3,2,1,0:T(8,128)}, /*index=5*...) while((s32[]{:T(128)}, f32[11,112,112]{2,1,0:T(8,128)S(1)}, ...), condition=%wide.region_9.10_spmd.clone, body=%wide.region_8.9_spmd.clone.sunk | while | flops 417656 | bytes 1670769 | solution.py:20
  266.0 1.3 add_select_fusion.10
  267.4 1.3 add_select_fusion.10
  268.7 1.3 add_select_fusion.10
  270.0 1.3 add_select_fusion.10
  271.3 1.3 add_select_fusion.10
  272.6 1.3 add_select_fusion.10
  274.0 1.3 add_select_fusion.10
  275.3 1.3 add_select_fusion.10
  276.9 1.2 convolution_bitcast_fusion.1
  278.2 4.9 %fusion = f32[1,11,112,112]{3,0,2,1:T(1,128)S(1)} fusion(f32[4,11,112,112]{3,2,1,0:T(8,128)} %all-gather.11.cloned.1.call-done, s32[]{:T(128)S(6)} %axis_index.27), kind=kOutput, calls=%fused_computation.4 | convolution fusion | flops 6623236 | bytes 2759684 | tf_op jit(solution)/shard_map/g,ghde->hde/dot_general | solution.py:30
  283.1 1.5 fusion.12
  284.5 0.5 fusion.8
  285.1 0.8 fusion.14
  285.9 0.8 fusion.10
  286.8 0.3 fusion.9
  287.1 0.8 fusion.15
  (79 shorter events, 1.4 us)
Async XLA Ops:
  7.2 1.1 copy-start
  7.2 2.4 copy-start.1
  7.2 40.4 %copy-start.4 = (bf16[128,1232]{0,1:T(8,128)(2,1)S(1)}, bf16[128,1232]{0,1:T(8,128)(2,1)}, u32[]{:S(2)}) copy-start(bf16[128,1232]{0,1:T(8,128)(2,1)} %param.12) | copy-start | bytes 946180
  7.2 45.9 %all-gather.13.cloned.1.call-start = ((), (), s32[]{:S(2)}) async-start(), calls=%async_computation.2 | async-start | bytes 5677056 | tf_op jit(solution)/shard_map/all_gather | solution.py:9
  9.5 96.0 %all-gather.15.cloned.1.call-start = ((), (), s32[]{:S(2)}) async-start(), calls=%async_computation.3 | async-start | bytes 5677056 | tf_op jit(solution)/shard_map/all_gather | solution.py:9
  47.4 5.8 %copy-start.9 = (pred[128,128]{0,1:T(8,128)(4,1)}, pred[128,128]{0,1:T(8,128)(4,1)S(1)}, u32[]{:S(2)}) copy-start(pred[128,128]{0,1:T(8,128)(4,1)S(1)} %iota_compare_fusion) | copy-start | bytes 49156
  53.2 10.5 %copy-start.11 = (f32[11,112]{1,0:T(8,128)S(1)}, f32[11,112]{1,0:T(8,128)}, u32[]{:S(2)}) copy-start(f32[11,112]{1,0:T(8,128)} %param.17) | copy-start | bytes 14788
  53.2 10.9 %copy-start.15 = (bf16[128,1232]{0,1:T(8,128)(2,1)S(1)}, bf16[128,1232]{0,1:T(8,128)(2,1)}, u32[]{:S(2)}) copy-start(bf16[128,1232]{0,1:T(8,128)(2,1)} %param.15) | copy-start | bytes 946180
  105.6 61.8 %all-reduce.3.cloned.1.call-start = ((), (), s32[]{:S(2)}) async-start(), calls=%async_computation.4 | async-start | bytes 2523136 | tf_op jit(solution)/shard_map/psum | solution.py:57
  106.3 114.9 %all-gather.9.cloned.1.call-start = ((), (), s32[]{:S(2)}) async-start(), calls=%async_computation | async-start | bytes 3153920 | tf_op jit(solution)/shard_map/all_gather | solution.py:59
  167.4 110.8 %all-gather.11.cloned.1.call-start = ((), (), s32[]{:S(2)}) async-start(), calls=%async_computation.1 | async-start | bytes 3153920 | tf_op jit(solution)/shard_map/all_gather | solution.py:90
  170.0 56.9 %copy-start.16 = (bf16[128,1232]{0,1:T(8,128)(2,1)S(1)}, bf16[128,1232]{0,1:T(8,128)(2,1)}, u32[]{:S(2)}) copy-start(bf16[128,1232]{0,1:T(8,128)(2,1)} %param.15) | copy-start | bytes 946180
  221.2 5.7 %copy-start.13 = (f32[11,112,112]{2,1,0:T(8,128)S(1)}, f32[11,112,112]{2,1,0:T(8,128)}, u32[]{:S(2)}) copy-start(f32[11,112,112]{2,1,0:T(8,128)} %param.16) | copy-start | bytes 1655812
  226.0 0.9 copy-start.7
  265.9 10.6 %copy-start.12 = (f32[11,112]{1,0:T(8,128)S(1)}, f32[11,112]{1,0:T(8,128)}, u32[]{:S(2)}) copy-start(f32[11,112]{1,0:T(8,128)} %param.19) | copy-start | bytes 14788
  265.9 10.7 %copy-start.10 = (pred[128,128]{0,1:T(8,128)(4,1)S(1)}, pred[128,128]{0,1:T(8,128)(4,1)}, u32[]{:S(2)}) copy-start(pred[128,128]{0,1:T(8,128)(4,1)} %copy-done.9) | copy-start | bytes 49156
  266.0 10.7 %copy-start.17 = (bf16[128,1232]{0,1:T(8,128)(2,1)S(1)}, bf16[128,1232]{0,1:T(8,128)(2,1)}, u32[]{:S(2)}) copy-start(bf16[128,1232]{0,1:T(8,128)(2,1)} %param.15) | copy-start | bytes 946180
  276.9 6.1 %copy-start.2 = (f32[11,112,112]{2,1,0:T(8,128)S(1)}, f32[11,112,112]{2,1,0:T(8,128)}, u32[]{:S(2)}) copy-start(f32[11,112,112]{2,1,0:T(8,128)} %param.18) | copy-start | bytes 1655812
  278.2 4.9 %copy-start.6 = (f32[11,128,112]{1,2,0:T(8,128)S(1)}, f32[11,128,112]{1,2,0:T(8,128)}, u32[]{:S(2)}) copy-start(f32[11,128,112]{1,2,0:T(8,128)} %fusion.20) | copy-start | bytes 1892356
  278.2 6.3 %copy-start.3 = (f32[128,11,112]{0,2,1:T(8,128)S(1)}, f32[128,11,112]{0,2,1:T(8,128)}, u32[]{:S(2)}) copy-start(f32[128,11,112]{0,2,1:T(8,128)} %convolution_bitcast_fusion.1) | copy-start | bytes 1892356
  284.5 1.4 copy-start.8
  284.5 1.4 copy-start.14
  284.5 1.4 copy-start.18
  285.9 1.2 copy-start.5
Sparse Core Ops, SparseCore 0:
  9.9 43.2 all-gather.12
  65.4 40.1 all-gather.14
  109.6 57.6 all-reduce.2
  168.8 52.3 all-gather.8
  222.6 52.3 all-gather.10
where the time goes:
time: 295 us; the launch traced here: 294 us
  waiting for transfers between devices  159 us (54%)
  blocking collectives  75 us (25%)
  other arithmetic  23.5 us (8%)
  matrix products  21.5 us (7%)
  between operations  14.1 us (5%)
    psum x1, waiting for transfers between devices, per_device(): group_total = lax.psum((block_state, block_norm), 'seq')  61 us
    all_gather x1, waiting for transfers between devices, per_device(): lax.all_gather(group_total[0][None], 'grp', axis=0, tiled=True)  51.2 us
    all_gather x2, waiting for transfers between devices, entering(): everything = jax.tree.map(lambda part: lax.all_gather(part, axis), x)  45.5 us
    select_n x32, other arithmetic, step(): return jax.tree.map(lambda a, b: jnp.where(reached, a, b), new, before)  20.5 us
    all_gather x2, blocking collectives, entering(): everything = jax.tree.map(lambda part: lax.all_gather(part, axis), x)  17.6 us
    psum x1, blocking collectives, per_device(): group_total = lax.psum((block_state, block_norm), 'seq')  15.7 us
    psum x1, blocking collectives, per_device(): group_back = lax.psum((carry_state, carry_sum), 'seq')  14.2 us
    all_gather x1, blocking collectives, per_device(): lax.all_gather(group_back[1][None], 'grp', axis=0, tiled=True)  14.1 us
  transfers between devices with their start and end apart: 5, of which 4 were waited for; matrix products, arithmetic and copies ran while one was open for 7% of the time, Pallas kernels for 0%

commit v1 on v0

v1 whole, which is shorter than its diff:
```python
import functools

import jax
import jax.numpy as jnp
from jax import lax
from jax.experimental import pallas as pl
from jax.experimental.pallas import tpu as pltpu
from jax.sharding import PartitionSpec as P

F32 = jnp.float32
BF16 = jnp.bfloat16
LANES = 128
SUB = 8


def dot(x, y, dims):
    return lax.dot_general(x, y, (dims, ((), ())), preferred_element_type=F32)


def nn(x, y):
    return dot(x, y, ((1,), (0,)))


def nt(x, y):
    return dot(x, y, ((1,), (1,)))


def tn(x, y):
    return dot(x, y, ((0,), (0,)))


def exact(x, y):
    return lax.dot_general(
        x, y, (((1,), (0,)), ((), ())), precision=lax.Precision.HIGHEST, preferred_element_type=F32
    )


def parts(x):
    high = x.astype(BF16)
    return high, (x - high.astype(F32)).astype(BF16)


def stacked_parts(row):
    high = row.astype(BF16)
    rest = row - high.astype(F32)
    middle = rest.astype(BF16)
    low = rest - middle.astype(F32)
    zeros = jnp.zeros((SUB - 3, row.shape[1]), F32)
    return jnp.concatenate([high.astype(F32), middle.astype(F32), low, zeros], axis=0).astype(BF16)


def added(rows):
    return rows[0:1] + rows[1:2] + rows[2:3]


class Plan:
    def __init__(self, devices, length, heads, width):
        self.devices, self.length, self.heads, self.width = devices, length, heads, width
        self.half = -(-heads // 2)
        self.shift = heads - self.half
        self.rows = self.half * width
        self.per_slot = devices // SUB
        self.head_tiles = width // SUB
        self.tiles = self.half * self.head_tiles
        self.slots = -(-self.tiles // self.per_slot)
        self.span = self.slots * LANES

    def place(self, base, tile):
        slot, part = divmod(tile, self.per_slot)
        return pl.ds(part * SUB, SUB), pl.ds((base + slot) * LANES, LANES)

    def row_slot(self, head):
        return pl.ds((self.slots + head) * LANES, LANES)

    def own(self, ref, core, head):
        start = pl.multiple_of(core * (self.shift * self.width) + head * self.width, 16)
        return ref[pl.ds(start, self.width), :]

    def other(self, ref, head):
        return ref[head * self.width : (head + 1) * self.width, :]


def my_core():
    return lax.axis_index("seq") & 1


def my_device():
    return lax.axis_index("grp") * lax.axis_size("seq") + lax.axis_index("seq")


def pair_swap(x):
    size = lax.axis_size("seq")
    return lax.ppermute(x, "seq", [(i, i ^ 1) for i in range(size)])


def wide(tile):
    rows, columns = tile.shape
    if columns == LANES:
        return tile
    return jnp.concatenate([tile, jnp.zeros((rows, LANES - columns), tile.dtype)], axis=1)


def store_rows(plan, ref, base, head, block):
    block = wide(block)
    for j in range(plan.head_tiles):
        rows, columns = plan.place(base, head * plan.head_tiles + j)
        ref[rows, columns] = block[j * SUB : (j + 1) * SUB, :]


def store_padding(plan, ref, base):
    for tile in range(plan.tiles, plan.slots * plan.per_slot):
        rows, columns = plan.place(base, tile)
        ref[rows, columns] = jnp.zeros((SUB, LANES), F32)


def load_rows(plan, ref, base, head):
    tiles = []
    for j in range(plan.head_tiles):
        rows, columns = plan.place(base, head * plan.head_tiles + j)
        tiles.append(ref[rows, columns])
    return jnp.concatenate(tiles, axis=0)[:, : plan.width]


def scan_matrix(devices, later):
    row = lax.broadcasted_iota(jnp.int32, (devices, devices), 0)
    column = lax.broadcasted_iota(jnp.int32, (devices, devices), 1)
    beyond = (column // 2 > row // 2) if later else (column // 2 < row // 2)
    return jnp.where(beyond & (column % 2 == row % 2), 1.0, 0.0).astype(F32)


def scan_row(devices, core, chip, later):
    column = lax.broadcasted_iota(jnp.int32, (SUB, devices), 1)
    beyond = (column // 2 > chip) if later else (column // 2 < chip)
    return jnp.where(beyond & (column % 2 == core), 1.0, 0.0).astype(F32)


def causal_mask(length):
    row = lax.broadcasted_iota(jnp.int32, (length, length), 0)
    column = lax.broadcasted_iota(jnp.int32, (length, length), 1)
    return row <= column


def relu(x):
    return jnp.maximum(x, 0)


def chip_state(plan, ids_ref, k_ref, v_ref, k_got_ref, v_got_ref, out_ref):
    core = ids_ref[0]
    ones = jnp.ones((SUB, 2 * plan.length), BF16)
    for h in range(plan.half):
        keys = [relu(plan.own(k_ref, core, h)), relu(plan.other(k_got_ref, h)).astype(BF16)]
        values = [plan.own(v_ref, core, h), plan.other(v_got_ref, h).astype(BF16)]
        keys, values = jnp.concatenate(keys, axis=1), jnp.concatenate(values, axis=1)
        store_rows(plan, out_ref, 0, h, nt(values, keys))
        norm = wide(nt(ones, keys))
        for j in range(plan.devices // SUB):
            out_ref[j * SUB : (j + 1) * SUB, plan.row_slot(h)] = norm
    store_padding(plan, out_ref, 0)


def local_scores(
    plan, ids_ref, k_ref, v_ref, q_ref, k_got_ref, v_got_ref, q_got_ref,
    low_ref, sum_ref, inner_ref, norm_ref,
):
    core = ids_ref[0]
    causal = causal_mask(plan.length)
    ones = jnp.ones((SUB, plan.length), BF16)
    for h in range(plan.half):
        for i in range(2):
            if i == 0:
                a, b = relu(plan.own(q_ref, core, h)), relu(plan.own(k_ref, core, h))
                v = plan.own(v_ref, core, h)
            else:
                a, b = relu(plan.other(q_got_ref, h)), relu(plan.other(k_got_ref, h))
                a, b, v = a.astype(BF16), b.astype(BF16), plan.other(v_got_ref, h).astype(BF16)
            scores = jnp.where(causal, tn(b, a), 0.0)
            sum_ref[i, h : h + 1, :] = 1.0 + jnp.sum(scores, axis=0, keepdims=True)
            low = scores.astype(BF16)
            low_ref[i, h] = low
            inner_ref[i, h] = nn(v, low)
            norm_ref[i, h : h + 1, :] = wide(nt(ones, b))[0:1]


def middle(
    plan, ids_ref, in_ref, sum_ref, q_ref, g_ref, q_got_ref, g_got_ref, norm_ref, norm_in_ref,
    out_ref, den_ref, z_ref,
):
    core, chip = ids_ref[0], ids_ref[1]
    flags = (core.astype(F32), (1 - core).astype(F32))
    width = plan.width
    norms = exact(scan_row(plan.devices, core, chip, False), in_ref[:, plan.span :])
    for h in range(plan.half):
        base = norm_in_ref[pl.ds(core * plan.shift + h, 1), :]
        base = base + norms[0:1, h * LANES : h * LANES + width]
        features, grads = [], []
        for i in range(2):
            z = base + flags[i] * norm_ref[1 - i, h : h + 1, :width]
            z_ref[i, h : h + 1, :] = wide(z)
            if i == 0:
                a, g = relu(plan.own(q_ref, core, h)), plan.own(g_ref, core, h).astype(F32)
            else:
                a, g = relu(plan.other(q_got_ref, h)).astype(BF16), plan.other(g_got_ref, h)
            den = sum_ref[i, h : h + 1, :] + added(nn(stacked_parts(z), a))
            den_ref[i, h : h + 1, :] = den
            features.append(a)
            grads.append((g * (1.0 / den)).astype(BF16))
        state = nt(jnp.concatenate(features, axis=1), jnp.concatenate(grads, axis=1))
        store_rows(plan, out_ref, plan.slots, h, state)
    store_padding(plan, out_ref, plan.slots)
    out_ref[:, : plan.span] = exact(scan_matrix(plan.devices, False), in_ref[:, : plan.span])


def local_grads(
    plan, ids_ref, k_ref, v_ref, q_ref, g_ref, k_got_ref, v_got_ref, q_got_ref, g_got_ref,
    low_ref, den_ref, state_in_ref, grad_state_ref, mixed_ref, value_ref, before_ref, after_ref,
):
    core = ids_ref[0]
    own_first = core == 0
    late = (core.astype(F32), (1 - core).astype(F32))
    early = (late[1], late[0])
    for h in range(plan.half):
        own = [plan.own(ref, core, h) for ref in (k_ref, v_ref, q_ref, g_ref)]
        got = [plan.other(ref, h) for ref in (k_got_ref, v_got_ref, q_got_ref, g_got_ref)]
        us = []
        for i, (_, v, _, g) in enumerate((own, got)):
            u = (g.astype(F32) * (1.0 / den_ref[i, h : h + 1, :])).astype(BF16)
            us.append(u)
            mixed_ref[i, h] = tn(v.astype(BF16), u)
            value_ref[i, h] = nt(u, low_ref[i, h])
        k = jnp.where(own_first, own[0].astype(F32), got[0])
        v = jnp.where(own_first, own[1].astype(F32), got[1])
        first = nt(v.astype(BF16), relu(k).astype(BF16))
        q = jnp.where(own_first, got[2], own[2].astype(F32))
        u = jnp.where(own_first, us[1].astype(F32), us[0].astype(F32))
        second = nt(relu(q).astype(BF16), u.astype(BF16))
        state_in = state_in_ref[core * plan.shift + h].T
        grad_state = grad_state_ref[core * plan.shift + h]
        for i in range(2):
            before_ref[i, h] = state_in + late[i] * first
            after_ref[i, h] = grad_state + early[i] * second


def outputs_grad(
    plan, ids_ref, in_ref, before_ref, q_ref, g_ref, q_got_ref, g_got_ref, den_ref, inner_ref,
    out_ref, state_ref, c_ref, m_ref,
):
    core = ids_ref[0]
    for h in range(plan.half):
        base = load_rows(plan, in_ref, 0, h)
        total = None
        for i in range(2):
            if i == 0:
                a, g = relu(plan.own(q_ref, core, h)), plan.own(g_ref, core, h).astype(F32)
            else:
                a, g = relu(plan.other(q_got_ref, h)).astype(BF16), plan.other(g_got_ref, h)
            state = base + before_ref[i, h]
            state_ref[i, h] = state
            high, low = parts(state)
            numerator = nn(high, a) + nn(low, a) + inner_ref[i, h]
            inverse = 1.0 / den_ref[i, h : h + 1, :]
            along = jnp.sum(g * numerator, axis=0, keepdims=True)
            c = -(along * inverse) * inverse
            c_ref[i, h : h + 1, :] = c
            m = wide(added(nt(stacked_parts(c), a)))
            m_ref[i, h : h + 1, :] = m
            total = m if total is None else total + m
        out_ref[:, plan.row_slot(h)] = jnp.broadcast_to(total, (plan.devices, LANES))
    out_ref[:, : plan.span] = exact(scan_matrix(plan.devices, True), in_ref[:, plan.span :])


def query_grads(
    plan, ids_ref, k_ref, q_ref, g_ref, k_got_ref, q_got_ref, g_got_ref, den_ref, c_ref, z_ref,
    mixed_ref, state_ref, own_ref, send_ref, key_ref,
):
    core = ids_ref[0]
    causal = causal_mask(plan.length)
    width = plan.width
    for i in range(2):
        columns = z_ref[i].T
        for h in range(plan.half):
            rows = slice(h * width, (h + 1) * width)
            if i == 0:
                a, b = relu(plan.own(q_ref, core, h)), relu(plan.own(k_ref, core, h))
                g = plan.own(g_ref, core, h).astype(F32)
            else:
                a, b = relu(plan.other(q_got_ref, h)), relu(plan.other(k_got_ref, h))
                a, b, g = a.astype(BF16), b.astype(BF16), plan.other(g_got_ref, h)
            u = g * (1.0 / den_ref[i, h : h + 1, :])
            c = c_ref[i, h : h + 1, :]
            mixed = jnp.where(causal, mixed_ref[i, h] + c, 0.0).astype(BF16)
            high, low = parts(state_ref[i, h])
            u_high, u_low = parts(u)
            grad = tn(high, u_high) + (tn(low, u_high) + tn(high, u_low))
            grad = grad + columns[:width, h : h + 1] * c + nn(b, mixed)
            grad = jnp.where(a.astype(F32) > 0, grad, 0.0)
            target = own_ref if i == 0 else send_ref
            target[rows, :] = grad
            key_ref[i, h] = nt(a, mixed)


def key_value_grads(
    plan, ids_ref, in_ref, after_ref, grad_norm_ref, m_ref, key_in_ref, value_in_ref, k_ref, v_ref, k_got_ref, v_got_ref, key_ref, value_ref, key_send_ref,
    value_send_ref,
):
    core, chip = ids_ref[0], ids_ref[1]
    flags = ((1 - core).astype(F32), core.astype(F32))
    width = plan.width
    norms = exact(scan_row(plan.devices, core, chip, True), in_ref[:, plan.span :])[0:1]
    norms = jnp.concatenate(
        [norms[:, h * LANES : (h + 1) * LANES] for h in range(plan.half)]
        + [jnp.zeros((SUB - plan.half % SUB, LANES), F32)], axis=0,
    )
    own_rows = [
        grad_norm_ref[pl.ds(core * plan.shift + h, 1), :] for h in range(plan.half)
    ] + [jnp.zeros((SUB - plan.half % SUB, width), F32)]
    norms = norms + wide(jnp.concatenate(own_rows, axis=0))
    for i in range(2):
        columns = (norms + flags[i] * m_ref[1 - i]).T
        for h in range(plan.half):
            rows = slice(h * width, (h + 1) * width)
            high, low = parts(load_rows(plan, in_ref, 0, h) + after_ref[i, h])
            if i == 0:
                b, v = relu(plan.own(k_ref, core, h)), plan.own(v_ref, core, h)
            else:
                b, v = relu(plan.other(k_got_ref, h)).astype(BF16), plan.other(v_got_ref, h).astype(BF16)
            key = nn(high, v) + nn(low, v) + columns[:width, h : h + 1] + key_in_ref[i, h]
            key = jnp.where(b.astype(F32) > 0, key, 0.0)
            value = tn(high, b) + tn(low, b) + value_in_ref[i, h]
            if i == 0:
                key_ref[rows, :] = key
                value_ref[rows, :] = value
            else:
                key_send_ref[rows, :] = key
                value_send_ref[rows, :] = value


def assemble(plan, ids_ref, *refs):
    core = ids_ref[0]
    count = len(refs) // 3
    start = pl.multiple_of(core * (plan.shift * plan.width), 16)
    rest = plan.shift * plan.width
    skip = plan.rows - rest
    other = pl.multiple_of((1 - core) * plan.rows, 16)
    source = pl.multiple_of((1 - core) * skip, 16)
    for own_ref, got_ref, out_ref in zip(refs[:count], refs[count : 2 * count], refs[2 * count :]):
        out_ref[pl.ds(start, plan.rows), :] = own_ref[...].astype(BF16)
        out_ref[pl.ds(other, rest), :] = got_ref[pl.ds(source, rest), :].astype(BF16)


def call(body, outs, args, flops=10_000_000, scratch=()):
    smem = pl.BlockSpec(memory_space=pltpu.SMEM)
    vmem = pl.BlockSpec(memory_space=pltpu.VMEM)
    in_specs = [smem if x.ndim == 1 else vmem for x in args]
    moved = sum(x.size * x.dtype.itemsize for x in (*args, *outs))
    return pl.pallas_call(
        body,
        out_shape=outs,
        in_specs=in_specs,
        out_specs=[vmem] * len(outs),
        scratch_shapes=list(scratch),
        cost_estimate=pl.CostEstimate(flops=flops, bytes_accessed=moved, transcendentals=0),
    )(*args)


def shape(dims, dtype=F32):
    return jax.ShapeDtypeStruct(dims, dtype)


def per_device(
    queries, key_vectors, value_vectors, output_grad, state_in, norm_in, grad_state, grad_norm
):
    both = ("grp", "seq")
    length = queries.shape[0]
    heads, width = norm_in.shape
    devices = lax.axis_size("grp") * lax.axis_size("seq")
    plan = Plan(devices, length, heads, width)
    half = plan.half
    core = my_core()
    who = jnp.stack([core, my_device() >> 1]).astype(jnp.int32)
    q, k, v, g = queries.T, key_vectors.T, value_vectors.T, output_grad.T

    def bind(body):
        return functools.partial(body, plan)

    def exchange(x):
        return lax.all_to_all(x, both, 0, 0, tiled=True)

    def swap_columns(x):
        start = (1 - core) * (plan.shift * width)
        return pair_swap(lax.dynamic_slice_in_dim(x, start, plan.rows, 0).astype(F32))

    tokens = shape((plan.rows, length))
    pair = shape((2, half, width, length))
    square = (2, half, length, length)
    states = shape((2, half, width, width))
    rows = shape((2, SUB * -(-half // SUB), LANES))
    wide_sent = shape((devices, plan.span + half * LANES))

    k_got, v_got = swap_columns(k), swap_columns(v)
    (sent,) = call(bind(chip_state), (wide_sent,), (who, k, v, k_got, v_got))
    got = exchange(sent)
    q_got, g_got = swap_columns(q), swap_columns(g)
    low, sums, inner, norm = call(
        bind(local_scores),
        (shape(square, BF16), rows, pair, rows),
        (who, k, v, q, k_got, v_got, q_got),
    )
    sent, den, z = call(
        bind(middle),
        (shape((devices, 2 * plan.span)), rows, rows),
        (who, got, sums, q, g, q_got, g_got, norm, norm_in),
    )
    got = exchange(sent)
    mixed, value, before, after = call(
        bind(local_grads),
        (shape(square), pair, states, states),
        (who, k, v, q, g, k_got, v_got, q_got, g_got, low, den, state_in, grad_state),
    )
    sent, state, c, m = call(
        bind(outputs_grad),
        (wide_sent, states, rows, rows),
        (who, got, before, q, g, q_got, g_got, den, inner),
    )
    got = exchange(sent)
    query, query_send, key = call(
        bind(query_grads),
        (tokens, tokens, pair),
        (who, k, q, g, k_got, q_got, g_got, den, c, z, mixed, state),
    )
    final = shape((heads * width, length), BF16)
    (query_grad,) = call(bind(assemble), (final,), (who, query, pair_swap(query_send)))
    key, value, key_send, value_send = call(
        bind(key_value_grads),
        (tokens,) * 4,
        (who, got, after, grad_norm, m, key, value, k, v, k_got, v_got),
    )
    key_grad, value_grad = call(
        bind(assemble),
        (final, final),
        (who, key, value, pair_swap(key_send), pair_swap(value_send)),
    )
    return query_grad.T, key_grad.T, value_grad.T


def solution(mesh):
    rows = P(("grp", "seq"), None)
    return jax.shard_map(
        per_device,
        mesh=mesh,
        in_specs=(rows, rows, rows, rows, P(), P(), P(), P()),
        out_specs=(rows, rows, rows),
        check_vma=False,
    )
```

time: 295 us -> 96.9 us (0.33)
  waiting for transfers between devices: 159 us -> 32.5 us
  blocking collectives: 75 us -> 0 us
  Pallas kernels: 0 us -> 31.8 us
  other arithmetic: 23.5 us -> 1.69 us
  matrix products: 21.5 us -> 0 us
  starting transfers between devices: 0.16 us -> 15.5 us
  between operations: 14.1 us -> 0.74 us
  local copies, waits for them, and re-layouts: 1.04 us -> 14 us
    all_gather x4 -> x0, waiting for transfers between devices: 96.7 us -> none  [the longest x1 51.2 us: per_device(): lax.all_gather(group_total[0][None], 'grp', axis=0, tiled=True)]
    psum x1 -> x0, waiting for transfers between devices: 61 us -> none  [per_device(): group_total = lax.psum((block_state, block_norm), 'seq')]
    all_gather x4 -> x0, blocking collectives: 45.1 us -> none  [the longest x2 17.6 us: entering(): everything = jax.tree.map(lambda part: lax.all_gather(part, axis), x)]
    pallas_call x0 -> x9, Pallas kernels: none -> 31.8 us  [call(): pl.pallas_call(body, out_shape=outs, in_specs=in_specs, out_specs=[vmem]...]
    all_to_all x0 -> x3, waiting for transfers between devices: none -> 31 us  [exchange(): return lax.all_to_all(x, both, 0, 0, tiled=True)]
    psum x2 -> x0, blocking collectives: 29.9 us -> none  [the longest x1 15.7 us: per_device(): group_total = lax.psum((block_state, block_norm), 'seq')]
    dot_general x18 -> x0, matrix products: 21.5 us -> none  [the longest x2 9.68 us: select_groups(): jnp.einsum('g,ghde->hde', weights, state_all, precision=lax.Precision.HIG...]
    select_n x32 -> x0, other arithmetic: 20.5 us -> none  [step(): return jax.tree.map(lambda a, b: jnp.where(reached, a, b), new, before)]
  transfers between devices with their start and end apart: 5 -> 10, of which waited for: 4 -> 6; matrix products, arithmetic and copies ran while one was open for 7% -> 2% of each run, Pallas kernels for 0% -> 19%
where the time goes in v1:
time: 96.9 us; the launch traced here: 96.2 us
  waiting for transfers between devices  32.5 us (34%)
  Pallas kernels  31.8 us (33%)
  starting transfers between devices  15.5 us (16%)
  local copies, waits for them, and re-layouts  14 us (14%)
  other arithmetic  1.69 us (2%)
    pallas_call x9, Pallas kernels, call(): pl.pallas_call(body, out_shape=outs, in_specs=in_specs, out_specs=[vmem]...  31.8 us
    all_to_all x3, waiting for transfers between devices, exchange(): return lax.all_to_all(x, both, 0, 0, tiled=True)  31 us
    all_to_all x3, starting transfers between devices, exchange(): return lax.all_to_all(x, both, 0, 0, tiled=True)  13.4 us
    all_to_all x3, local copies, waits for them, and re-layouts, exchange(): return lax.all_to_all(x, both, 0, 0, tiled=True)  7.13 us
    unnamed x23, local copies, waits for them, and re-layouts  6.9 us
    ppermute x7, starting transfers between devices, pair_swap(): return lax.ppermute(x, 'seq', [(i, i ^ 1) for i in range(size)])  2.06 us
  transfers between devices with their start and end apart: 10, of which 6 were waited for; matrix products, arithmetic and copies ran while one was open for 2% of the time, Pallas kernels for 19%

profile of v1, /device:TPU:0, one launch (start us, length us, event | category | flops | bytes accessed | tf_op | source)
XLA Modules:
  0.0 96.2 jit_solution(15958057751377659932)
XLA Ops:
  0.6 0.0 copy-start.1
  0.6 1.0 %convert_bitcast_fusion = f32[672,128]{1,0:T(8,128)S(1)} fusion(bf16[128,1232]{0,1:T(8,128)(2,1)} %param.10, s32[]{:T(128)S(6)} %select_n.2), kind=kLoop, calls=%fused_computation.3 | loop fusion | flops 86016 | bytes 516100 | tf_op jit(solution)/shard_map/convert_element_type | solution.py:390
  1.6 0.6 collective-permute-start.3
  2.2 0.0 copy-done.1
  2.2 0.1 collective-permute-start
  2.3 0.6 pad_add_fusion.ids_ref
  2.9 0.5 collective-permute-done.3.v_got_ref
  3.5 0.5 collective-permute-done.k_got_ref
  4.0 0.2 copy-done.6
  4.2 0.5 copy-done.3
  4.7 2.4 %shard_map.103 = f32[32,3456]{1,0:T(8,128)} custom-call(s32[2]{0:T(128)} %pad_add_fusion.ids_ref, bf16[1232,128]{1,0:T(8,128)(2,1)} %bitcast.34, bf16[1232,128]{1,0:T(8,128)(2,1)} %bitcast.43, f32[672,128]{1,0:T(8,128)} %copy-done.3, f32[672,128]{1,0:T(8,128)} %copy-done.6), custom_call_target="tpu_custom_call" | custom-call | flops 10000000 | bytes 1761288 | tf_op jit(solution)/shard_map/pallas_call | solution.py:355
  7.1 2.2 %copy.11 = f32[32,1,3456]{2,1,0:T(1,128)} copy(f32[32,1,3456]{2,0,1:T(8,128)} %bitcast.49) | data formatting | bytes 884736 | tf_op jit(solution)/shard_map/all_to_all | solution.py:386
  9.3 7.2 %all-to-all-start = ((f32[32,1,3456]{2,1,0:T(1,128)}), f32[32,1,3456]{2,1,0:T(1,128)S(1)}, u32[]{:S(2)}, u32[]{:S(2)}) async-start(f32[32,1,3456]{2,1,0:T(1,128)} %copy.11), calls=%async_computation | async-start | bytes 884736 | tf_op jit(solution)/shard_map/all_to_all | solution.py:386
  16.6 0.0 copy-start.4
  16.6 0.3 collective-permute-start.1
  16.9 0.6 copy-done.4
  17.6 0.3 collective-permute-start.2
  17.9 0.5 collective-permute-done.1.q_got_ref
  18.3 0.7 copy-done.2
  19.1 4.5 %shard_map.104 = (bf16[2,6,128,128]{3,2,1,0:T(8,128)(2,1)}, f32[2,8,128]{2,1,0:T(8,128)}, f32[2,6,112,128]{3,2,1,0:T(8,128)}, f32[2,8,128]{2,1,0:T(8,128)}) custom-call(s32[2]{0:T(128)} %pad_add_fusion.ids_ref, bf16[1232,128]{1,0:T(8,128)(2,1)} %bitcast.35, bf16[1232,128]{1,0:T(8,128)(2,1)} %bitcast.44, bf16[1232,128]{1,0:T(8,128)(2,1)} %bitcast.29, ...), custom_call_target="tpu_custom_call" | custom-call | flops 10000000 | bytes 3076104 | tf_op jit(solution)/shard_map/pallas_call | solution.py:355
  23.6 7.1 %all-to-all-done = f32[32,1,3456]{2,1,0:T(1,128)S(1)} async-done(((f32[32,1,3456]{2,1,0:T(1,128)}), f32[32,1,3456]{2,1,0:T(1,128)S(1)}, u32[]{:S(2)}, u32[]{:S(2)}) %all-to-all-start) | async-done | bytes 442400 | tf_op jit(solution)/shard_map/all_to_all | solution.py:386
  30.7 0.8 copy.22
  31.5 0.0 collective-permute-done.2.g_got_ref
  31.5 0.7 copy-done.5
  32.2 3.2 %shard_map.105 = (f32[32,5376]{1,0:T(8,128)}, f32[2,8,128]{2,1,0:T(8,128)}, f32[2,8,128]{2,1,0:T(8,128)}) custom-call(s32[2]{0:T(128)} %pad_add_fusion.ids_ref, f32[32,3456]{1,0:T(8,128)} %bitcast.48, f32[2,8,128]{2,1,0:T(8,128)} %get-tuple-element.27.sum_ref, bf16[1232,128]{1,0:T(8,128)(2,1)} %bitcast.30, bf16[1232,128]{1,0:T(8,128)(2,1)} %bitcast.39, ...), custom_call_target="tpu_custom_call" | custom-call | flops 10000000 | bytes 2487112 | tf_op jit(solution)/shard_map/pallas_call | solution.py:355
  35.4 2.6 %copy.12 = f32[32,1,5376]{2,1,0:T(1,128)} copy(f32[32,1,5376]{2,0,1:T(8,128)} %bitcast.51) | data formatting | bytes 1376256 | tf_op jit(solution)/shard_map/all_to_all | solution.py:386
  38.0 2.7 %all-to-all-start.1 = ((f32[32,1,5376]{2,1,0:T(1,128)}), f32[32,1,5376]{2,1,0:T(1,128)S(1)}, u32[]{:S(2)}, u32[]{:S(2)}) async-start(f32[32,1,5376]{2,1,0:T(1,128)} %copy.12), calls=%async_computation.1 | async-start | bytes 1376256 | tf_op jit(solution)/shard_map/all_to_all | solution.py:386
  40.7 4.5 %shard_map.106 = (f32[2,6,128,128]{3,2,1,0:T(8,128)}, f32[2,6,112,128]{3,2,1,0:T(8,128)}, f32[2,6,112,112]{3,2,1,0:T(8,128)}, f32[2,6,112,112]{3,2,1,0:T(8,128)}) custom-call(s32[2]{0:T(128)} %pad_add_fusion.ids_ref, bf16[1232,128]{1,0:T(8,128)(2,1)} %bitcast.36, bf16[1232,128]{1,0:T(8,128)(2,1)} %bitcast.45, bf16[1232,128]{1,0:T(8,128)(2,1)} %bitcast.31, ...), custom_call_target="tpu_custom_call" | custom-call | flops 10000000 | bytes 6821896 | tf_op jit(solution)/shard_map/pallas_call | solution.py:355
  45.3 14.0 %all-to-all-done.1 = f32[32,1,5376]{2,1,0:T(1,128)S(1)} async-done(((f32[32,1,5376]{2,1,0:T(1,128)}), f32[32,1,5376]{2,1,0:T(1,128)S(1)}, u32[]{:S(2)}, u32[]{:S(2)}) %all-to-all-start.1) | async-done | bytes 688160 | tf_op jit(solution)/shard_map/all_to_all | solution.py:386
  59.3 0.9 copy.20
  60.2 5.3 %shard_map.107 = (f32[32,3456]{1,0:T(8,128)}, f32[2,6,112,112]{3,2,1,0:T(8,128)}, f32[2,8,128]{2,1,0:T(8,128)}, f32[2,8,128]{2,1,0:T(8,128)}) custom-call(s32[2]{0:T(128)} %pad_add_fusion.ids_ref, f32[32,5376]{1,0:T(8,128)} %bitcast.47, f32[2,6,112,112]{3,2,1,0:T(8,128)} %get-tuple-element.32.before_ref, bf16[1232,128]{1,0:T(8,128)(2,1)} %bitcast.32, ...), custom_call_target="tpu_custom_call" | custom-call | flops 10000000 | bytes 4366344 | tf_op jit(solution)/shard_map/pallas_call | solution.py:355
  65.5 2.2 %copy.13 = f32[32,1,3456]{2,1,0:T(1,128)} copy(f32[32,1,3456]{2,0,1:T(8,128)} %bitcast.52) | data formatting | bytes 884736 | tf_op jit(solution)/shard_map/all_to_all | solution.py:386
  67.8 3.5 %all-to-all-start.2 = ((f32[32,1,3456]{2,1,0:T(1,128)}), f32[32,1,3456]{2,1,0:T(1,128)S(1)}, u32[]{:S(2)}, u32[]{:S(2)}) async-start(f32[32,1,3456]{2,1,0:T(1,128)} %copy.13), calls=%async_computation.2 | async-start | bytes 884736 | tf_op jit(solution)/shard_map/all_to_all | solution.py:386
  71.3 4.0 %shard_map.108 = (f32[672,128]{1,0:T(8,128)}, f32[672,128]{1,0:T(8,128)}, f32[2,6,112,128]{3,2,1,0:T(8,128)}) custom-call(s32[2]{0:T(128)} %pad_add_fusion.ids_ref, bf16[1232,128]{1,0:T(8,128)(2,1)} %bitcast.37, bf16[1232,128]{1,0:T(8,128)(2,1)} %bitcast.33, bf16[1232,128]{1,0:T(8,128)(2,1)} %bitcast.42, f32[672,128]{1,0:T(8,128)} %copy-done.3, ...), custom_call_target="tpu_custom_call" | custom-call | flops 10000000 | bytes 4767752 | tf_op jit(solution)/shard_map/pallas_call | solution.py:355
  75.3 0.3 collective-permute-start.4
  75.6 9.8 %all-to-all-done.2 = f32[32,1,3456]{2,1,0:T(1,128)S(1)} async-done(((f32[32,1,3456]{2,1,0:T(1,128)}), f32[32,1,3456]{2,1,0:T(1,128)S(1)}, u32[]{:S(2)}, u32[]{:S(2)}) %all-to-all-start.2) | async-done | bytes 442400 | tf_op jit(solution)/shard_map/all_to_all | solution.py:386
  85.4 0.8 copy.21
  86.2 3.9 %shard_map.110 = (f32[672,128]{1,0:T(8,128)}, f32[672,128]{1,0:T(8,128)}, f32[672,128]{1,0:T(8,128)}, f32[672,128]{1,0:T(8,128)}) custom-call(s32[2]{0:T(128)} %pad_add_fusion.ids_ref, f32[32,3456]{1,0:T(8,128)} %bitcast.50, f32[2,6,112,112]{3,2,1,0:T(8,128)} %get-tuple-element.41.after_ref, f32[11,112]{1,0:T(8,128)} %grad_norm_ref.1, ...), custom_call_target="tpu_custom_call" | custom-call | flops 10000000 | bytes 5129032 | tf_op jit(solution)/shard_map/pallas_call | solution.py:355
  90.1 0.0 collective-permute-start.5
  90.1 0.5 collective-permute-start.6
  90.6 0.0 collective-permute-done.4.refs_1_
  90.6 0.7 copy-done.7
  91.3 1.8 %shard_map.109 = bf16[1232,128]{1,0:T(8,128)(2,1)} custom-call(s32[2]{0:T(128)} %pad_add_fusion.ids_ref, f32[672,128]{1,0:T(8,128)} %get-tuple-element.38.refs_0_, f32[672,128]{1,0:T(8,128)} %copy-done.7), custom_call_target="tpu_custom_call" | custom-call | flops 10000000 | bytes 1003528 | tf_op jit(solution)/shard_map/pallas_call | solution.py:355
  93.2 0.0 collective-permute-done.5.refs_2_
  93.2 0.0 collective-permute-done.6.refs_3_
  93.2 0.7 copy-done.8
  93.9 0.1 copy-done.9
  94.0 2.2 %shard_map.111 = (bf16[1232,128]{1,0:T(8,128)(2,1)}, bf16[1232,128]{1,0:T(8,128)(2,1)}) custom-call(s32[2]{0:T(128)} %pad_add_fusion.ids_ref, f32[672,128]{1,0:T(8,128)} %get-tuple-element.45.refs_0_, f32[672,128]{1,0:T(8,128)} %get-tuple-element.46.refs_1_, f32[672,128]{1,0:T(8,128)} %copy-done.8, f32[672,128]{1,0:T(8,128)} %copy-done.9), custom_call_target="tpu_custom_call" | custom-call | flops 10000000 | bytes 2007048 | tf_op jit(solution)/shard_map/pallas_call | solution.py:355
  (12 shorter events, 0.1 us)
Async XLA Ops:
  0.6 1.6 %copy-start.1 = (bf16[128,1232]{0,1:T(8,128)(2,1)S(1)}, bf16[128,1232]{0,1:T(8,128)(2,1)}, u32[]{:S(2)}) copy-start(bf16[128,1232]{0,1:T(8,128)(2,1)} %param.9) | copy-start | bytes 946180
  1.6 1.8 %collective-permute-start.3 = (f32[672,128]{1,0:T(8,128)S(1)}, f32[672,128]{1,0:T(8,128)S(1)}, u32[]{:S(2)}, u32[]{:S(2)}) collective-permute-start(f32[672,128]{1,0:T(8,128)S(1)} %convert_bitcast_fusion), channel_id=1, source_target_pairs={{0,1},{1,0},{2,3},{3,2},{4,5},{5,4},{6,7},{7,6},{8,9},{9,8},{10,11... | collective-permute-start | bytes 1032200 | tf_op jit(solution)/shard_map/ppermute | solution.py:93
  2.2 1.7 %collective-permute-start = (f32[672,128]{1,0:T(8,128)S(1)}, f32[672,128]{1,0:T(8,128)S(1)}, u32[]{:S(2)}, u32[]{:S(2)}) collective-permute-start(f32[672,128]{1,0:T(8,128)S(1)} %convert_bitcast_fusion.3), channel_id=1, source_target_pairs={{0,1},{1,0},{2,3},{3,2},{4,5},{5,4},{6,7},{7,6},{8,9},{9,8},{10,11... | collective-permute-start | bytes 1032200 | tf_op jit(solution)/shard_map/ppermute | solution.py:93
  3.5 0.7 copy-start.6
  4.0 0.7 copy-start.3
  9.3 7.2 %copy-start = (bf16[128,1232]{0,1:T(8,128)(2,1)S(1)}, bf16[128,1232]{0,1:T(8,128)(2,1)}, u32[]{:S(2)}) copy-start(bf16[128,1232]{0,1:T(8,128)(2,1)} %param.8) | copy-start | bytes 946180
  9.3 21.3 %all-to-all-start = ((f32[32,1,3456]{2,1,0:T(1,128)}), f32[32,1,3456]{2,1,0:T(1,128)S(1)}, u32[]{:S(2)}, u32[]{:S(2)}) async-start(f32[32,1,3456]{2,1,0:T(1,128)} %copy.11), calls=%async_computation | async-start | bytes 884736 | tf_op jit(solution)/shard_map/all_to_all | solution.py:386
  16.6 1.0 %copy-start.4 = (bf16[128,1232]{0,1:T(8,128)(2,1)S(1)}, bf16[128,1232]{0,1:T(8,128)(2,1)}, u32[]{:S(2)}) copy-start(bf16[128,1232]{0,1:T(8,128)(2,1)} %param.11) | copy-start | bytes 946180
  16.6 1.7 %collective-permute-start.1 = (f32[672,128]{1,0:T(8,128)S(1)}, f32[672,128]{1,0:T(8,128)S(1)}, u32[]{:S(2)}, u32[]{:S(2)}) collective-permute-start(f32[672,128]{1,0:T(8,128)S(1)} %convert_bitcast_fusion.2), channel_id=1, source_target_pairs={{0,1},{1,0},{2,3},{3,2},{4,5},{5,4},{6,7},{7,6},{8,9},{9,8},{10,11... | collective-permute-start | bytes 1032200 | tf_op jit(solution)/shard_map/ppermute | solution.py:93
  17.6 13.9 %collective-permute-start.2 = (f32[672,128]{1,0:T(8,128)S(1)}, f32[672,128]{1,0:T(8,128)S(1)}, u32[]{:S(2)}, u32[]{:S(2)}) collective-permute-start(f32[672,128]{1,0:T(8,128)S(1)} %convert_bitcast_fusion.1), channel_id=1, source_target_pairs={{0,1},{1,0},{2,3},{3,2},{4,5},{5,4},{6,7},{7,6},{8,9},{9,8},{10,11... | collective-permute-start | bytes 1032200 | tf_op jit(solution)/shard_map/ppermute | solution.py:93
  18.3 0.7 copy-start.2
  31.5 0.7 copy-start.5
  38.0 21.3 %all-to-all-start.1 = ((f32[32,1,5376]{2,1,0:T(1,128)}), f32[32,1,5376]{2,1,0:T(1,128)S(1)}, u32[]{:S(2)}, u32[]{:S(2)}) async-start(f32[32,1,5376]{2,1,0:T(1,128)} %copy.12), calls=%async_computation.1 | async-start | bytes 1376256 | tf_op jit(solution)/shard_map/all_to_all | solution.py:386
  67.8 17.7 %all-to-all-start.2 = ((f32[32,1,3456]{2,1,0:T(1,128)}), f32[32,1,3456]{2,1,0:T(1,128)S(1)}, u32[]{:S(2)}, u32[]{:S(2)}) async-start(f32[32,1,3456]{2,1,0:T(1,128)} %copy.13), calls=%async_computation.2 | async-start | bytes 884736 | tf_op jit(solution)/shard_map/all_to_all | solution.py:386
  75.3 15.3 %collective-permute-start.4 = (f32[672,128]{1,0:T(8,128)}, f32[672,128]{1,0:T(8,128)S(1)}, u32[]{:S(2)}, u32[]{:S(2)}) collective-permute-start(f32[672,128]{1,0:T(8,128)} %get-tuple-element.39), channel_id=1, source_target_pairs={{0,1},{1,0},{2,3},{3,2},{4,5},{5,4},{6,7},{7,6},{8,9},{9,8},{10,11... | collective-permute-start | bytes 1032200 | tf_op jit(solution)/shard_map/ppermute | solution.py:93
  90.1 3.1 %collective-permute-start.5 = (f32[672,128]{1,0:T(8,128)}, f32[672,128]{1,0:T(8,128)S(1)}, u32[]{:S(2)}, u32[]{:S(2)}) collective-permute-start(f32[672,128]{1,0:T(8,128)} %get-tuple-element.47), channel_id=1, source_target_pairs={{0,1},{1,0},{2,3},{3,2},{4,5},{5,4},{6,7},{7,6},{8,9},{9,8},{10,11... | collective-permute-start | bytes 1032200 | tf_op jit(solution)/shard_map/ppermute | solution.py:93
  90.1 3.1 %collective-permute-start.6 = (f32[672,128]{1,0:T(8,128)}, f32[672,128]{1,0:T(8,128)S(1)}, u32[]{:S(2)}, u32[]{:S(2)}) collective-permute-start(f32[672,128]{1,0:T(8,128)} %get-tuple-element.48), channel_id=1, source_target_pairs={{0,1},{1,0},{2,3},{3,2},{4,5},{5,4},{6,7},{7,6},{8,9},{9,8},{10,11... | collective-permute-start | bytes 1032200 | tf_op jit(solution)/shard_map/ppermute | solution.py:93
  90.6 0.7 copy-start.7
  93.2 0.7 copy-start.8
  93.2 0.9 copy-start.9

commit v2 on v1

v2 whole, which is shorter than its diff:
```python
import functools

import jax
import jax.numpy as jnp
from jax import lax
from jax.experimental import pallas as pl
from jax.experimental.pallas import tpu as pltpu
from jax.sharding import PartitionSpec as P

F32 = jnp.float32
BF16 = jnp.bfloat16
LANES = 128
SUB = 8
VMEM_BYTES = 67_043_328
FREE = 48 * 2**20


def dot(x, y, dims):
    return lax.dot_general(x, y, (dims, ((), ())), preferred_element_type=F32)


def nn(x, y):
    return dot(x, y, ((1,), (0,)))


def nt(x, y):
    return dot(x, y, ((1,), (1,)))


def tn(x, y):
    return dot(x, y, ((0,), (0,)))


def parts(x):
    high = x.astype(BF16)
    return high, (x - high.astype(F32)).astype(BF16)


def stacked_parts(row):
    high = row.astype(BF16)
    rest = row - high.astype(F32)
    middle = rest.astype(BF16)
    low = rest - middle.astype(F32)
    zeros = jnp.zeros((SUB - 3, row.shape[1]), F32)
    return jnp.concatenate([high.astype(F32), middle.astype(F32), low, zeros], axis=0).astype(BF16)


def added(rows):
    return rows[0:1] + rows[1:2] + rows[2:3]


class Plan:
    def __init__(self, devices, length, heads, width):
        self.devices, self.length, self.heads, self.width = devices, length, heads, width
        self.half = -(-heads // 2)
        self.shift = heads - self.half
        self.rows = self.half * width
        self.extra = SUB * -(-self.half // SUB)
        self.per_slot = devices // SUB
        self.head_tiles = width // SUB
        self.tiles = self.half * self.head_tiles
        self.slots = -(-self.tiles // self.per_slot)
        self.span = self.slots * LANES

    def place(self, base, tile):
        slot, part = divmod(tile, self.per_slot)
        return pl.ds(part * SUB, SUB), 0, pl.ds((base + slot) * LANES, LANES)

    def columns(self, start, count):
        return slice(None), slice(None), pl.ds(start, count)

    def row_slot(self, head):
        return pl.ds((self.slots + head) * LANES, LANES)

    def own(self, ref, core, head):
        start = pl.multiple_of(core * (self.shift * self.width) + head * self.width, 16)
        return ref[pl.ds(start, self.width), :]

    def other(self, ref, head):
        return ref[head * self.width : (head + 1) * self.width, :]


def my_core():
    return lax.axis_index("seq") & 1


def my_device():
    return lax.axis_index("grp") * lax.axis_size("seq") + lax.axis_index("seq")


def pair_swap(x):
    size = lax.axis_size("seq")
    return lax.ppermute(x, "seq", [(i, i ^ 1) for i in range(size)])


def wide(tile):
    rows, columns = tile.shape
    if columns == LANES:
        return tile
    return jnp.concatenate([tile, jnp.zeros((rows, LANES - columns), tile.dtype)], axis=1)


def store_rows(plan, ref, base, head, block):
    block = wide(block)
    for j in range(plan.head_tiles):
        ref[plan.place(base, head * plan.head_tiles + j)] = block[j * SUB : (j + 1) * SUB, :]


def store_padding(plan, ref, base):
    for tile in range(plan.tiles, plan.slots * plan.per_slot):
        ref[plan.place(base, tile)] = jnp.zeros((SUB, LANES), F32)


def load_rows(plan, ref, base, head):
    tiles = []
    for j in range(plan.head_tiles):
        tiles.append(ref[plan.place(base, head * plan.head_tiles + j)])
    return jnp.concatenate(tiles, axis=0)[:, : plan.width]


def each(count, step, carry):
    if count > 16:
        return lax.fori_loop(0, count, step, carry)
    for i in range(count):
        carry = step(i, carry)
    return carry


def scan_rows(plan, in_ref, start, out_ref, later):
    chips = plan.devices // 2
    columns = pl.ds(start, plan.span)

    def step(i, sums):
        chip = chips - 1 - i if later else i
        grown = []
        for core in range(2):
            row = 2 * chip + core
            out_ref[row, :, : plan.span] = sums[core]
            grown.append(sums[core] + in_ref[row, :, columns])
        return tuple(grown)

    zero = jnp.zeros((1, plan.span), F32)
    each(chips, step, (zero, zero))


def scan_norms(plan, in_ref, core, chip, later):
    columns = pl.ds(plan.span, plan.half * LANES)

    def step(i, total):
        take = (i > chip) if later else (i < chip)
        return total + jnp.where(take, in_ref[2 * i + core, :, columns], 0.0)

    return each(plan.devices // 2, step, jnp.zeros((1, plan.half * LANES), F32))


def causal_mask(length):
    row = lax.broadcasted_iota(jnp.int32, (length, length), 0)
    column = lax.broadcasted_iota(jnp.int32, (length, length), 1)
    return row <= column


def relu(x):
    return jnp.maximum(x, 0)


def block_state(plan, partner, ids_ref, k_ref, v_ref, out_ref):
    core = ids_ref[0]
    if partner:
        core = 1 - core
    ones = jnp.ones((SUB, plan.length), BF16)
    out_ref[plan.rows :, :] = jnp.zeros((plan.extra, LANES), F32)
    for h in range(plan.half):
        b, v = relu(plan.own(k_ref, core, h)), plan.own(v_ref, core, h)
        out_ref[h * plan.width : (h + 1) * plan.width, :] = wide(nt(b, v))
        out_ref[plan.rows + h : plan.rows + h + 1, :] = wide(nt(ones, b))[0:1]


def chip_state(plan, own_ref, got_ref, out_ref):
    for h in range(plan.half):
        rows = slice(h * plan.width, (h + 1) * plan.width)
        store_rows(plan, out_ref, 0, h, own_ref[rows, :] + got_ref[rows, :])
        row = slice(plan.rows + h, plan.rows + h + 1)
        norm = jnp.broadcast_to(own_ref[row, :] + got_ref[row, :], (plan.devices, LANES))
        out_ref[:, 0, plan.row_slot(h)] = norm
    store_padding(plan, out_ref, 0)


def pack_tokens(
    plan, ids_ref, q_ref, k_ref, v_ref, g_ref, q_got_ref, k_got_ref, v_got_ref, g_got_ref,
    a_ref, b_ref, vb_ref, gb_ref, low_ref, sum_ref, norm_ref,
):
    core = ids_ref[0]
    causal = causal_mask(plan.length)
    ones = jnp.ones((SUB, plan.length), BF16)
    sources = ((q_ref, q_got_ref), (k_ref, k_got_ref), (v_ref, v_got_ref), (g_ref, g_got_ref))
    for h in range(plan.half):
        for i in range(2):
            for n, (pair, ref) in enumerate(zip(sources, (a_ref, b_ref, vb_ref, gb_ref))):
                x = plan.other(pair[1], h).astype(BF16) if i else plan.own(pair[0], core, h)
                ref[i, h] = relu(x) if n < 2 else x
            a, b = a_ref[i, h], b_ref[i, h]
            scores = jnp.where(causal, tn(b, a), 0.0)
            sum_ref[i, h : h + 1, :] = 1.0 + jnp.sum(scores, axis=0, keepdims=True)
            low_ref[i, h] = scores.astype(BF16)
            norm_ref[i, h : h + 1, :] = wide(nt(ones, b))[0:1]


def middle(
    plan, ids_ref, in_ref, sum_ref, a_ref, g_ref, norm_ref, norm_in_ref,
    out_ref, inverse_ref, z_ref,
):
    core, chip = ids_ref[0], ids_ref[1]
    flags = (core.astype(F32), (1 - core).astype(F32))
    width = plan.width
    norms = scan_norms(plan, in_ref, core, chip, False)
    scan_rows(plan, in_ref, 0, out_ref, False)
    for h in range(plan.half):
        base = norm_in_ref[pl.ds(core * plan.shift + h, 1), :]
        base = base + norms[0:1, h * LANES : h * LANES + width]
        features, grads = [], []
        for i in range(2):
            z = base + flags[i] * norm_ref[1 - i, h : h + 1, :width]
            z_ref[i, h : h + 1, :] = wide(z)
            a = a_ref[i, h]
            den = sum_ref[i, h : h + 1, :] + added(nn(stacked_parts(z), a))
            inverse = 1.0 / den
            inverse_ref[i, h : h + 1, :] = inverse
            features.append(a)
            grads.append((g_ref[i, h].astype(F32) * inverse).astype(BF16))
        state = nt(jnp.concatenate(features, axis=1), jnp.concatenate(grads, axis=1))
        store_rows(plan, out_ref, plan.slots, h, state)
    store_padding(plan, out_ref, plan.slots)


def before_states(
    plan, ids_ref, a_ref, b_ref, v_ref, g_ref, low_ref, state_in_ref, before_ref, inner_ref
):
    core = ids_ref[0]
    own_first = core == 0
    late = (core.astype(F32), (1 - core).astype(F32))
    for h in range(plan.half):
        for i in range(2):
            inner = nn(v_ref[i, h], low_ref[i, h])
            inner_ref[i, h : h + 1, :] = jnp.sum(
                g_ref[i, h].astype(F32) * inner, axis=0, keepdims=True
            )
        b = jnp.where(own_first, b_ref[0, h].astype(F32), b_ref[1, h].astype(F32)).astype(BF16)
        v = jnp.where(own_first, v_ref[0, h].astype(F32), v_ref[1, h].astype(F32)).astype(BF16)
        first = nt(b, v)
        for i in range(2):
            before_ref[i, h] = state_in_ref[core * plan.shift + h] + late[i] * first


def outputs_grad(
    plan, ids_ref, in_ref, before_ref, a_ref, g_ref, inverse_ref, inner_ref,
    out_ref, product_ref, c_ref, m_ref,
):
    scan_rows(plan, in_ref, plan.span, out_ref, True)
    for h in range(plan.half):
        base = load_rows(plan, in_ref, 0, h)
        total = None
        for i in range(2):
            high, low = parts(base + before_ref[i, h])
            g, a = g_ref[i, h], a_ref[i, h]
            product = nn(jnp.concatenate([high, low], axis=0), g)
            product = product[: plan.width] + product[plan.width :]
            product_ref[i, h] = product
            inverse = inverse_ref[i, h : h + 1, :]
            along = jnp.sum(a.astype(F32) * product, axis=0, keepdims=True)
            c = -((along + inner_ref[i, h : h + 1, :]) * inverse) * inverse
            c_ref[i, h : h + 1, :] = c
            m = wide(added(nt(stacked_parts(c), a)))
            m_ref[i, h : h + 1, :] = m
            total = m if total is None else total + m
        out_ref[:, 0, plan.row_slot(h)] = jnp.broadcast_to(total, (plan.devices, LANES))


def query_grads(
    plan, ids_ref, a_ref, b_ref, v_ref, g_ref, inverse_ref, c_ref, z_ref, product_ref,
    own_ref, send_ref, mixed_ref,
):
    causal = causal_mask(plan.length)
    width = plan.width
    for i in (1, 0):
        columns = z_ref[i].T
        for h in range(plan.half):
            rows = slice(h * width, (h + 1) * width)
            inverse, c = inverse_ref[i, h : h + 1, :], c_ref[i, h : h + 1, :]
            u = (g_ref[i, h].astype(F32) * inverse).astype(BF16)
            mixed = jnp.where(causal, tn(v_ref[i, h], u) + c, 0.0).astype(BF16)
            mixed_ref[i, h] = mixed
            grad = product_ref[i, h] * inverse + columns[:width, h : h + 1] * c
            grad = jnp.where(a_ref[i, h].astype(F32) > 0, grad + nn(b_ref[i, h], mixed), 0.0)
            target = send_ref if i else own_ref
            target[rows, :] = grad


def after_states(
    plan, ids_ref, a_ref, g_ref, inverse_ref, low_ref, mixed_ref, grad_state_ref,
    final_0_ref, final_1_ref,
):
    core = ids_ref[0]
    own_first = core == 0
    early = ((1 - core).astype(F32), core.astype(F32))
    for h in range(plan.half):
        us = []
        for i, ref in enumerate((final_0_ref, final_1_ref)):
            u = (g_ref[i, h].astype(F32) * inverse_ref[i, h : h + 1, :]).astype(BF16)
            us.append(u)
            ref[1, h] = nt(a_ref[i, h], mixed_ref[i, h])
            ref[2, h] = nt(u, low_ref[i, h])
        a = jnp.where(own_first, a_ref[1, h].astype(F32), a_ref[0, h].astype(F32)).astype(BF16)
        u = jnp.where(own_first, us[1].astype(F32), us[0].astype(F32)).astype(BF16)
        second = nt(a, u)
        for i, ref in enumerate((final_0_ref, final_1_ref)):
            ref[0, h] = wide(grad_state_ref[core * plan.shift + h] + early[i] * second)


def key_value_grads(
    plan, i, ids_ref, in_ref, final_ref, grad_norm_ref, m_ref, b_ref, v_ref, key_ref, value_ref
):
    core, chip = ids_ref[0], ids_ref[1]
    flag = (core if i else 1 - core).astype(F32)
    width = plan.width
    norms = scan_norms(plan, in_ref, core, chip, True)
    zeros = plan.extra - plan.half
    norms = jnp.concatenate(
        [norms[:, h * LANES : (h + 1) * LANES] for h in range(plan.half)]
        + [jnp.zeros((zeros, LANES), F32)] * (zeros > 0), axis=0,
    )
    own_rows = [
        grad_norm_ref[pl.ds(core * plan.shift + h, 1), :] for h in range(plan.half)
    ] + [jnp.zeros((zeros, width), F32)] * (zeros > 0)
    norms = norms + wide(jnp.concatenate(own_rows, axis=0))
    columns = (norms + flag * m_ref[1 - i]).T
    for h in range(plan.half):
        rows = slice(h * width, (h + 1) * width)
        high, low = parts(load_rows(plan, in_ref, 0, h) + final_ref[0, h, :, :width])
        b, v = b_ref[i, h], v_ref[i, h]
        both = nn(jnp.concatenate([high, low], axis=0), v)
        key = both[:width] + both[width:] + columns[:width, h : h + 1] + final_ref[1, h]
        key = jnp.where(b.astype(F32) > 0, key, 0.0)
        value = tn(high, b) + tn(low, b) + final_ref[2, h]
        key_ref[rows, :] = key.astype(key_ref.dtype)
        value_ref[rows, :] = value.astype(value_ref.dtype)


def assemble(plan, ids_ref, *refs):
    core = ids_ref[0]
    count = len(refs) // 3
    start = pl.multiple_of(core * (plan.shift * plan.width), 16)
    rest = plan.shift * plan.width
    skip = plan.rows - rest
    other = pl.multiple_of((1 - core) * plan.rows, 16)
    source = pl.multiple_of((1 - core) * skip, 16)
    for own_ref, got_ref, out_ref in zip(refs[:count], refs[count : 2 * count], refs[2 * count :]):
        out_ref[pl.ds(start, plan.rows), :] = own_ref[...].astype(BF16)
        out_ref[pl.ds(other, rest), :] = got_ref[pl.ds(source, rest), :].astype(BF16)


def call(body, outs, args, room=FREE, flops=10_000_000, scratch=()):
    smem = pl.BlockSpec(memory_space=pltpu.SMEM)
    vmem = pl.BlockSpec(memory_space=pltpu.VMEM)
    in_specs = [smem if x.ndim == 1 else vmem for x in args]
    moved = sum(x.size * x.dtype.itemsize for x in (*args, *outs))
    return pl.pallas_call(
        body,
        out_shape=outs,
        in_specs=in_specs,
        out_specs=[vmem] * len(outs),
        scratch_shapes=list(scratch),
        compiler_params=pltpu.CompilerParams(vmem_limit_bytes=VMEM_BYTES - room),
        cost_estimate=pl.CostEstimate(flops=flops, bytes_accessed=moved, transcendentals=0),
    )(*args)


def shape(dims, dtype=F32):
    return jax.ShapeDtypeStruct(dims, dtype)


def per_device(
    queries, key_vectors, value_vectors, output_grad, state_in, norm_in, grad_state, grad_norm
):
    both = ("grp", "seq")
    length = queries.shape[0]
    heads, width = norm_in.shape
    devices = lax.axis_size("grp") * lax.axis_size("seq")
    plan = Plan(devices, length, heads, width)
    half = plan.half
    core = my_core()
    who = jnp.stack([core, my_device() >> 1]).astype(jnp.int32)
    q, k, v, g = queries.T, key_vectors.T, value_vectors.T, output_grad.T

    def bind(body):
        return functools.partial(body, plan)

    def exchange(x):
        return lax.all_to_all(x, both, 0, 0, tiled=True)

    def swap_columns(x):
        start = (1 - core) * (plan.shift * width)
        return pair_swap(lax.dynamic_slice_in_dim(x, start, plan.rows, 0).astype(F32))

    tokens = shape((plan.rows, length))
    packed = shape((2, half, width, length), BF16)
    products = shape((2, half, width, length))
    square = shape((2, half, length, length), BF16)
    states = shape((2, half, width, width))
    rows = shape((2, plan.extra, LANES))
    final = shape((3, half, width, LANES))
    block = shape((plan.rows + plan.extra, LANES))
    sent_single = shape((devices, 1, plan.span + half * LANES))
    sent_double = shape((devices, 1, 2 * plan.span))

    (send,) = call(functools.partial(block_state, plan, True), (block,), (who, k, v))
    block_got = pair_swap(send)
    (block_own,) = call(functools.partial(block_state, plan, False), (block,), (who, k, v))
    (sent,) = call(bind(chip_state), (sent_single,), (block_own, block_got))
    sent, k, v, q, g = lax.optimization_barrier((sent, k, v, q, g))
    got = exchange(sent)
    a, b, v, g, low, sums, norm = call(
        bind(pack_tokens),
        (packed, packed, packed, packed, square, rows, rows),
        (who, q, k, v, g, *(swap_columns(x) for x in (q, k, v, g))),
    )
    sent, inverse, z = call(
        bind(middle),
        (sent_double, rows, rows),
        (who, got, sums, a, g, norm, norm_in),
    )
    got = exchange(sent)
    before, inner = call(
        bind(before_states), (states, rows), (who, a, b, v, g, low, state_in)
    )
    sent, product, c, m = call(
        bind(outputs_grad),
        (sent_single, products, rows, rows),
        (who, got, before, a, g, inverse, inner),
    )
    got = exchange(sent)
    query, query_send, mixed = call(
        bind(query_grads), (tokens, tokens, square), (who, a, b, v, g, inverse, c, z, product)
    )
    query_got = pair_swap(query_send)
    final_0, final_1 = call(
        bind(after_states), (final, final), (who, a, g, inverse, low, mixed, grad_state)
    )
    whole = shape((heads * width, length), BF16)
    (query_grad,) = call(bind(assemble), (whole,), (who, query, query_got))
    got, query_grad = lax.optimization_barrier((got, query_grad))
    key_send, value_send = call(
        functools.partial(key_value_grads, plan, 1),
        (tokens, tokens),
        (who, got, final_1, grad_norm, m, b, v),
    )
    key_got, value_got = pair_swap(key_send), pair_swap(value_send)
    half_tokens = shape((plan.rows, length), BF16)
    key, value = call(
        functools.partial(key_value_grads, plan, 0),
        (half_tokens, half_tokens),
        (who, got, final_0, grad_norm, m, b, v),
    )
    key_grad, value_grad = call(
        bind(assemble), (whole, whole), (who, key, value, key_got, value_got)
    )
    return query_grad.T, key_grad.T, value_grad.T


def solution(mesh):
    rows = P(("grp", "seq"), None)
    return jax.shard_map(
        per_device,
        mesh=mesh,
        in_specs=(rows, rows, rows, rows, P(), P(), P(), P()),
        out_specs=(rows, rows, rows),
        check_vma=False,
    )
```

time: 96.9 us -> 78.2 us (0.81)
  Pallas kernels: 31.8 us -> 15.9 us
  local copies, waits for them, and re-layouts: 14 us -> 10.6 us
  waiting for transfers between devices: 32.5 us -> 34.1 us
  other arithmetic: 1.69 us -> 0.18 us
    pallas_call x9 -> x13, Pallas kernels: 31.8 us -> 15.9 us  [call(): pl.pallas_call(body, out_shape=outs, in_specs=in_specs, out_specs=[vmem]...]
    all_to_all x3 -> x0, local copies, waits for them, and re-layouts: 7.13 us -> none  [exchange(): return lax.all_to_all(x, both, 0, 0, tiled=True)]
    unnamed x23 -> x34, local copies, waits for them, and re-layouts: 6.9 us -> 10.6 us
    ppermute x7 -> x8, waiting for transfers between devices: 1.49 us -> 3.06 us  [pair_swap(): return lax.ppermute(x, 'seq', [(i, i ^ 1) for i in range(size)])]
    ppermute x7 -> x8, starting transfers between devices: 2.06 us -> 2.53 us  [pair_swap(): return lax.ppermute(x, 'seq', [(i, i ^ 1) for i in range(size)])]
  transfers between devices with their start and end apart: 10 -> 11, of which waited for: 6 -> 9; matrix products, arithmetic and copies ran while one was open for 2% -> 0% of each run, Pallas kernels for 19% -> 11%
where the time goes in v2:
time: 78.2 us; the launch traced here: 77.7 us
  waiting for transfers between devices  34.1 us (44%)
  starting transfers between devices  16 us (20%)
  Pallas kernels  15.9 us (20%)
  local copies, waits for them, and re-layouts  10.6 us (14%)
  between operations  0.81 us (1%)
    all_to_all x3, waiting for transfers between devices, exchange(): return lax.all_to_all(x, both, 0, 0, tiled=True)  31.1 us
    pallas_call x13, Pallas kernels, call(): pl.pallas_call(body, out_shape=outs, in_specs=in_specs, out_specs=[vmem]...  15.9 us
    all_to_all x3, starting transfers between devices, exchange(): return lax.all_to_all(x, both, 0, 0, tiled=True)  13.4 us
    unnamed x34, local copies, waits for them, and re-layouts  10.6 us
    ppermute x8, waiting for transfers between devices, pair_swap(): return lax.ppermute(x, 'seq', [(i, i ^ 1) for i in range(size)])  3.06 us
    ppermute x8, starting transfers between devices, pair_swap(): return lax.ppermute(x, 'seq', [(i, i ^ 1) for i in range(size)])  2.53 us
  transfers between devices with their start and end apart: 11, of which 9 were waited for; matrix products, arithmetic and copies ran while one was open for 0% of the time, Pallas kernels for 11%

profile of v2, /device:TPU:0, one launch (start us, length us, event | category | flops | bytes accessed | tf_op | source)
XLA Modules:
  0.0 77.7 jit_solution(8900245186380061216)
XLA Ops:
  0.6 0.1 pad_add_fusion.ids_ref
  0.7 1.0 %copy-done = bf16[128,1232]{0,1:T(8,128)(2,1)S(1)} copy-done((bf16[128,1232]{0,1:T(8,128)(2,1)S(1)}, bf16[128,1232]{0,1:T(8,128)(2,1)}, u32[]{:S(2)}) %copy-start) | copy-done | bytes 315416
  1.7 1.0 %copy-done.2 = bf16[128,1232]{0,1:T(8,128)(2,1)S(1)} copy-done((bf16[128,1232]{0,1:T(8,128)(2,1)S(1)}, bf16[128,1232]{0,1:T(8,128)(2,1)}, u32[]{:S(2)}) %copy-start.2) | copy-done | bytes 315416
  2.6 0.9 %shard_map.104 = f32[680,128]{1,0:T(8,128)S(1)} custom-call(s32[2]{0:T(128)S(1)} %pad_add_fusion.ids_ref, bf16[1232,128]{1,0:T(8,128)(2,1)S(1)} %bitcast.9, bf16[1232,128]{1,0:T(8,128)(2,1)S(1)} %bitcast.13), custom_call_target="tpu_custom_call" | custom-call | flops 10000000 | bytes 978952 | tf_op jit(solution)/shard_map/pallas_call | solution.py:366
  3.5 0.6 collective-permute-start
  4.1 0.9 %shard_map.103.own_ref = f32[680,128]{1,0:T(8,128)S(1)} custom-call(s32[2]{0:T(128)S(1)} %pad_add_fusion.ids_ref, bf16[1232,128]{1,0:T(8,128)(2,1)S(1)} %bitcast.10, bf16[1232,128]{1,0:T(8,128)(2,1)S(1)} %bitcast.14), custom_call_target="tpu_custom_call" | custom-call | flops 10000000 | bytes 978952 | tf_op jit(solution)/shard_map/pallas_call | solution.py:366
  4.9 0.4 collective-permute-done.got_ref
  5.4 1.0 %shard_map.105 = f32[32,1,3456]{2,1,0:T(1,128)} custom-call(f32[680,128]{1,0:T(8,128)S(1)} %shard_map.103.own_ref, f32[680,128]{1,0:T(8,128)S(1)} %collective-permute-done.got_ref), custom_call_target="tpu_custom_call" | custom-call | flops 10000000 | bytes 1138688 | tf_op jit(solution)/shard_map/pallas_call | solution.py:366
  6.4 7.2 %all-to-all-start = ((f32[32,1,3456]{2,1,0:T(1,128)}), f32[32,1,3456]{2,1,0:T(1,128)S(1)}, u32[]{:S(2)}, u32[]{:S(2)}) async-start(f32[32,1,3456]{2,1,0:T(1,128)} %shard_map.105), calls=%async_computation | async-start | bytes 884736 | tf_op jit(solution)/shard_map/all_to_all | solution.py:398
  13.6 0.0 copy-start.1
  13.6 0.9 %copy-done.1 = bf16[128,1232]{0,1:T(8,128)(2,1)S(1)} copy-done((bf16[128,1232]{0,1:T(8,128)(2,1)S(1)}, bf16[128,1232]{0,1:T(8,128)(2,1)}, u32[]{:S(2)}) %copy-start.1) | copy-done | bytes 315416
  14.6 0.9 %copy-done.3 = bf16[128,1232]{0,1:T(8,128)(2,1)S(1)} copy-done((bf16[128,1232]{0,1:T(8,128)(2,1)S(1)}, bf16[128,1232]{0,1:T(8,128)(2,1)}, u32[]{:S(2)}) %copy-start.3) | copy-done | bytes 315416
  15.6 0.9 %copy-done.9 = bf16[128,1232]{0,1:T(8,128)(2,1)S(1)} copy-done((bf16[128,1232]{0,1:T(8,128)(2,1)S(1)}, bf16[128,1232]{0,1:T(8,128)(2,1)}, u32[]{:S(2)}) %copy-start.9) | copy-done | bytes 315416
  16.5 0.3 collective-permute-start.4
  16.8 0.3 collective-permute-start.3
  17.1 0.3 collective-permute-start.2
  17.3 0.3 collective-permute-start.1
  17.6 0.6 collective-permute-done.4.g_got_ref
  18.2 0.5 collective-permute-done.3.v_got_ref
  18.7 0.5 collective-permute-done.2.k_got_ref
  19.2 0.5 collective-permute-done.1.q_got_ref
  19.7 1.1 %shard_map.106 = (bf16[2,6,112,128]{3,2,1,0:T(8,128)(2,1)S(1)}, bf16[2,6,112,128]{3,2,1,0:T(8,128)(2,1)S(1)}, bf16[2,6,112,128]{3,2,1,0:T(8,128)(2,1)S(1)}, bf16...) custom-call(s32[2]{0:T(128)S(1)} %pad_add_fusion.ids_ref, ...), custom_call_target="tpu_custom_call" | custom-call | flops 10000000 | bytes 4423688 | tf_op jit(solution)/shard_map/pallas_call | solution.py:366
  20.8 6.9 %all-to-all-done.in_ref = f32[32,1,3456]{2,1,0:T(1,128)S(1)} async-done(((f32[32,1,3456]{2,1,0:T(1,128)}), f32[32,1,3456]{2,1,0:T(1,128)S(1)}, u32[]{:S(2)}, u32[]{:S(2)}) %all-to-all-start) | async-done | bytes 442400 | tf_op jit(solution)/shard_map/all_to_all | solution.py:398
  27.7 1.9 %shard_map.107 = (f32[32,1,5376]{2,1,0:T(1,128)}, f32[2,8,128]{2,1,0:T(8,128)S(1)}, f32[2,8,128]{2,1,0:T(8,128)S(1)}) custom-call(s32[2]{0:T(128)S(1)} %pad_add_fusion.ids_ref, f32[32,1,3456]{2,1,0:T(1,128)S(1)} %all-to-all-done.in_ref, f32[2,8,128]{2,1,0:T(8,128)S(1)} %get-tuple-element.42.sum_ref, bf16[2,6,112,128]{3,2,1,0:T(8,128)(2,1)S(1)} %get-tuple-element.43.a_ref, ...), custom_call_target="tpu_custom_call" | custom-call | flops 10000000 | bytes 1856328 | tf_op jit(solution)/shard_map/pallas_call | solution.py:366
  29.7 2.7 %all-to-all-start.1 = ((f32[32,1,5376]{2,1,0:T(1,128)}), f32[32,1,5376]{2,1,0:T(1,128)S(1)}, u32[]{:S(2)}, u32[]{:S(2)}) async-start(f32[32,1,5376]{2,1,0:T(1,128)} %get-tuple-element.46), calls=%async_computation.1 | async-start | bytes 1376256 | tf_op jit(solution)/shard_map/all_to_all | solution.py:398
  32.4 1.0 %shard_map.108 = (f32[2,6,112,112]{3,2,1,0:T(8,128)S(1)}, f32[2,8,128]{2,1,0:T(8,128)S(1)}) custom-call(s32[2]{0:T(128)S(1)} %pad_add_fusion.ids_ref, bf16[2,6,112,128]{3,2,1,0:T(8,128)(2,1)S(1)} %get-tuple-element.43.a_ref, bf16[2,6,112,128]{3,2,1,0:T(8,128)(2,1)S(1)} %get-tuple-element.47.b_ref, bf16[2,6,112,128]{3,2,1,0:T(8,128)(2,1)S(1)} %get-tuple-element.48.v_ref, ...), custom_call_target="tpu_custom_call" | custom-call | flops 10000000 | bytes 2931720 | tf_op jit(solution)/shard_map/pallas_call | solution.py:366
  33.4 0.9 %copy-done.10 = f32[2,6,112,112]{3,2,1,0:T(8,128)} copy-done((f32[2,6,112,112]{3,2,1,0:T(8,128)}, f32[2,6,112,112]{3,2,1,0:T(8,128)S(1)}, u32[]{:S(2)}) %copy-start.10) | copy-done | bytes 602136
  34.3 16.7 %all-to-all-done.1.in_ref = f32[32,1,5376]{2,1,0:T(1,128)S(1)} async-done(((f32[32,1,5376]{2,1,0:T(1,128)}), f32[32,1,5376]{2,1,0:T(1,128)S(1)}, u32[]{:S(2)}, u32[]{:S(2)}) %all-to-all-start.1) | async-done | bytes 688160 | tf_op jit(solution)/shard_map/all_to_all | solution.py:398
  51.0 1.1 %copy-done.11 = f32[2,6,112,112]{3,2,1,0:T(8,128)S(1)} copy-done((f32[2,6,112,112]{3,2,1,0:T(8,128)S(1)}, f32[2,6,112,112]{3,2,1,0:T(8,128)}, u32[]{:S(2)}) %copy-start.11) | copy-done | bytes 602136
  52.1 1.2 %shard_map.109 = (f32[32,1,3456]{2,1,0:T(1,128)S(1)}, f32[2,6,112,128]{3,2,1,0:T(8,128)S(1)}, f32[2,8,128]{2,1,0:T(8,128)S(1)}, f32[2,8,128]{2,1,0:T(8,128)S(1)}) custom-call(s32[2]{0:T(128)S(1)} %pad_add_fusion.ids_ref, f32[32,1,5376]{2,1,0:T(1,128)S(1)} %all-to-all-done.1.in_ref, f32[2,6,112,112]{3,2,1,0:T(8,128)S(1)} %copy-done.11, ...), custom_call_target="tpu_custom_call" | custom-call | flops 10000000 | bytes 3141640 | tf_op jit(solution)/shard_map/pallas_call | solution.py:366
  53.3 0.8 copy-done.14
  54.1 3.5 %all-to-all-start.2 = ((f32[32,1,3456]{2,1,0:T(1,128)}), f32[32,1,3456]{2,1,0:T(1,128)S(1)}, u32[]{:S(2)}, u32[]{:S(2)}) async-start(f32[32,1,3456]{2,1,0:T(1,128)} %copy-done.14), calls=%async_computation.2 | async-start | bytes 884736 | tf_op jit(solution)/shard_map/all_to_all | solution.py:398
  57.6 0.0 copy-start.13
  57.6 1.9 %shard_map.110 = (f32[672,128]{1,0:T(8,128)S(1)}, f32[672,128]{1,0:T(8,128)S(1)}, bf16[2,6,128,128]{3,2,1,0:T(8,128)(2,1)S(1)}) custom-call(s32[2]{0:T(128)S(1)} %pad_add_fusion.ids_ref, bf16[2,6,112,128]{3,2,1,0:T(8,128)(2,1)S(1)} %get-tuple-element.43.a_ref, bf16[2,6,112,128]{3,2,1,0:T(8,128)(2,1)S(1)} %get-tuple-element.47.b_ref, ...), custom_call_target="tpu_custom_call" | custom-call | flops 10000000 | bytes 3170312 | tf_op jit(solution)/shard_map/pallas_call | solution.py:366
  59.5 0.3 collective-permute-start.5
  59.8 1.2 %shard_map.112 = (f32[3,6,112,128]{3,2,1,0:T(8,128)S(1)}, f32[3,6,112,128]{3,2,1,0:T(8,128)S(1)}) custom-call(s32[2]{0:T(128)S(1)} %pad_add_fusion.ids_ref, bf16[2,6,112,128]{3,2,1,0:T(8,128)(2,1)S(1)} %get-tuple-element.43.a_ref, bf16[2,6,112,128]{3,2,1,0:T(8,128)(2,1)S(1)} %get-tuple-element.44.g_ref, f32[2,8,128]{2,1,0:T(8,128)S(1)} %get-tuple-element.51.inverse_ref, ...), custom_call_target="tpu_custom_call" | custom-call | flops 10000000 | bytes 4099080 | tf_op jit(solution)/shard_map/pallas_call | solution.py:366
  61.0 1.0 %copy-done.4 = f32[3,6,112,128]{3,2,1,0:T(8,128)} copy-done((f32[3,6,112,128]{3,2,1,0:T(8,128)}, f32[3,6,112,128]{3,2,1,0:T(8,128)S(1)}, u32[]{:S(2)}) %copy-start.4) | copy-done | bytes 1032216
  62.0 1.0 %copy-done.6 = f32[3,6,112,128]{3,2,1,0:T(8,128)} copy-done((f32[3,6,112,128]{3,2,1,0:T(8,128)}, f32[3,6,112,128]{3,2,1,0:T(8,128)S(1)}, u32[]{:S(2)}) %copy-start.6) | copy-done | bytes 1032216
  63.0 1.3 %shard_map.111 = bf16[1232,128]{1,0:T(8,128)(2,1)} custom-call(s32[2]{0:T(128)S(1)} %pad_add_fusion.ids_ref, f32[672,128]{1,0:T(8,128)S(1)} %get-tuple-element.57.refs_0_, f32[672,128]{1,0:T(8,128)S(1)} %collective-permute-done.5.refs_1_), custom_call_target="tpu_custom_call" | custom-call | flops 10000000 | bytes 1003528 | tf_op jit(solution)/shard_map/pallas_call | solution.py:366
  64.3 7.5 %all-to-all-done.2.in_ref = f32[32,1,3456]{2,1,0:T(1,128)S(1)} async-done(((f32[32,1,3456]{2,1,0:T(1,128)}), f32[32,1,3456]{2,1,0:T(1,128)S(1)}, u32[]{:S(2)}, u32[]{:S(2)}) %all-to-all-start.2) | async-done | bytes 442400 | tf_op jit(solution)/shard_map/all_to_all | solution.py:398
  71.7 1.2 %copy-done.7 = f32[3,6,112,128]{3,2,1,0:T(8,128)S(1)} copy-done((f32[3,6,112,128]{3,2,1,0:T(8,128)S(1)}, f32[3,6,112,128]{3,2,1,0:T(8,128)}, u32[]{:S(2)}) %copy-start.7) | copy-done | bytes 1032216
  72.9 1.1 %shard_map.114 = (f32[672,128]{1,0:T(8,128)S(1)}, f32[672,128]{1,0:T(8,128)S(1)}) custom-call(s32[2]{0:T(128)S(1)} %pad_add_fusion.ids_ref, f32[32,1,3456]{2,1,0:T(1,128)S(1)} %all-to-all-done.2.in_ref, f32[3,6,112,128]{3,2,1,0:T(8,128)S(1)} %copy-done.7, f32[11,112]{1,0:T(8,128)S(1)} %copy-done.15, f32[2,8,128]{2,1,0:T(8,128)S(1)} %get-tuple-element.63.m_ref, ...), custom_call_target="tpu_custom_call" | custom-call | flops 10000000 | bytes 2863944 | tf_op jit(solution)/shard_map/pallas_call | solution.py:366
  74.0 0.1 collective-permute-start.6
  74.1 0.5 collective-permute-start.7
  74.6 1.1 %shard_map.113 = (bf16[672,128]{1,0:T(8,128)(2,1)S(1)}, bf16[672,128]{1,0:T(8,128)(2,1)S(1)}) custom-call(s32[2]{0:T(128)S(1)} %pad_add_fusion.ids_ref, f32[32,1,3456]{2,1,0:T(1,128)S(1)} %all-to-all-done.2.in_ref, f32[3,6,112,128]{3,2,1,0:T(8,128)S(1)} %copy-done.5, f32[11,112]{1,0:T(8,128)S(1)} %copy-done.15, f32[2,8,128]{2,1,0:T(8,128)S(1)} %get-tuple-element.63.m_ref, ...), custom_call_target="tpu_custom_call" | custom-call | flops 10000000 | bytes 2519880 | tf_op jit(solution)/shard_map/pallas_call | solution.py:366
  75.7 0.0 collective-permute-done.6.refs_2_
  75.8 0.5 collective-permute-done.7.refs_3_
  76.3 1.4 %shard_map.115 = (bf16[1232,128]{1,0:T(8,128)(2,1)}, bf16[1232,128]{1,0:T(8,128)(2,1)}) custom-call(s32[2]{0:T(128)S(1)} %pad_add_fusion.ids_ref, bf16[672,128]{1,0:T(8,128)(2,1)S(1)} %get-tuple-element.64.refs_0_, bf16[672,128]{1,0:T(8,128)(2,1)S(1)} %get-tuple-element.65.refs_1_, f32[672,128]{1,0:T(8,128)S(1)} %collective-permute-done.6.refs_2_, ...), custom_call_target="tpu_custom_call" | custom-call | flops 10000000 | bytes 1662984 | tf_op jit(solution)/shard_map/pallas_call | solution.py:366
  (26 shorter events, 0.1 us)
Async XLA Ops:
  0.7 1.0 %copy-start = (bf16[128,1232]{0,1:T(8,128)(2,1)S(1)}, bf16[128,1232]{0,1:T(8,128)(2,1)}, u32[]{:S(2)}) copy-start(bf16[128,1232]{0,1:T(8,128)(2,1)} %param.9) | copy-start | bytes 946180
  1.7 1.0 %copy-start.2 = (bf16[128,1232]{0,1:T(8,128)(2,1)S(1)}, bf16[128,1232]{0,1:T(8,128)(2,1)}, u32[]{:S(2)}) copy-start(bf16[128,1232]{0,1:T(8,128)(2,1)} %param.10) | copy-start | bytes 946180
  3.5 1.8 %collective-permute-start = (f32[680,128]{1,0:T(8,128)S(1)}, f32[680,128]{1,0:T(8,128)S(1)}, u32[]{:S(2)}, u32[]{:S(2)}) collective-permute-start(f32[680,128]{1,0:T(8,128)S(1)} %shard_map.104), channel_id=1, source_target_pairs={{0,1},{1,0},{2,3},{3,2},{4,5},{5,4},{6,7},{7,6},{8,9},{9,8},{10,11... | collective-permute-start | bytes 1044488 | tf_op jit(solution)/shard_map/ppermute | solution.py:93
  6.4 7.2 %copy-start.8 = (bf16[128,1232]{0,1:T(8,128)(2,1)S(1)}, bf16[128,1232]{0,1:T(8,128)(2,1)}, u32[]{:S(2)}) copy-start(bf16[128,1232]{0,1:T(8,128)(2,1)} %param.8) | copy-start | bytes 946180
  6.4 21.3 %all-to-all-start = ((f32[32,1,3456]{2,1,0:T(1,128)}), f32[32,1,3456]{2,1,0:T(1,128)S(1)}, u32[]{:S(2)}, u32[]{:S(2)}) async-start(f32[32,1,3456]{2,1,0:T(1,128)} %shard_map.105), calls=%async_computation | async-start | bytes 884736 | tf_op jit(solution)/shard_map/all_to_all | solution.py:398
  13.6 1.0 %copy-start.1 = (bf16[128,1232]{0,1:T(8,128)(2,1)S(1)}, bf16[128,1232]{0,1:T(8,128)(2,1)}, u32[]{:S(2)}) copy-start(bf16[128,1232]{0,1:T(8,128)(2,1)} %param.9) | copy-start | bytes 946180
  14.6 1.0 %copy-start.3 = (bf16[128,1232]{0,1:T(8,128)(2,1)S(1)}, bf16[128,1232]{0,1:T(8,128)(2,1)}, u32[]{:S(2)}) copy-start(bf16[128,1232]{0,1:T(8,128)(2,1)} %param.10) | copy-start | bytes 946180
  15.5 1.0 %copy-start.9 = (bf16[128,1232]{0,1:T(8,128)(2,1)S(1)}, bf16[128,1232]{0,1:T(8,128)(2,1)}, u32[]{:S(2)}) copy-start(bf16[128,1232]{0,1:T(8,128)(2,1)} %param.11) | copy-start | bytes 946180
  16.5 1.7 %collective-permute-start.4 = (f32[672,128]{1,0:T(8,128)S(1)}, f32[672,128]{1,0:T(8,128)S(1)}, u32[]{:S(2)}, u32[]{:S(2)}) collective-permute-start(f32[672,128]{1,0:T(8,128)S(1)} %dynamic-slice_convert_fusion), channel_id=1, source_target_pairs={{0,1},{1,0},{2,3},{3,2},{4,5},{5,4},{6,7},{7,6},{8,9},{9,8},{10,11... | collective-permute-start | bytes 1032200 | tf_op jit(solution)/shard_map/ppermute | solution.py:93
  16.8 1.9 %collective-permute-start.3 = (f32[672,128]{1,0:T(8,128)S(1)}, f32[672,128]{1,0:T(8,128)S(1)}, u32[]{:S(2)}, u32[]{:S(2)}) collective-permute-start(f32[672,128]{1,0:T(8,128)S(1)} %dynamic-slice_convert_fusion.1), channel_id=1, source_target_pairs={{0,1},{1,0},{2,3},{3,2},{4,5},{5,4},{6,7},{7,6},{8,9},{9,8},{10,11... | collective-permute-start | bytes 1032200 | tf_op jit(solution)/shard_map/ppermute | solution.py:93
  17.1 2.1 %collective-permute-start.2 = (f32[672,128]{1,0:T(8,128)S(1)}, f32[672,128]{1,0:T(8,128)S(1)}, u32[]{:S(2)}, u32[]{:S(2)}) collective-permute-start(f32[672,128]{1,0:T(8,128)S(1)} %dynamic-slice_convert_fusion.2), channel_id=1, source_target_pairs={{0,1},{1,0},{2,3},{3,2},{4,5},{5,4},{6,7},{7,6},{8,9},{9,8},{10,11... | collective-permute-start | bytes 1032200 | tf_op jit(solution)/shard_map/ppermute | solution.py:93
  17.3 2.4 %collective-permute-start.1 = (f32[672,128]{1,0:T(8,128)S(1)}, f32[672,128]{1,0:T(8,128)S(1)}, u32[]{:S(2)}, u32[]{:S(2)}) collective-permute-start(f32[672,128]{1,0:T(8,128)S(1)} %dynamic-slice_convert_fusion.3), channel_id=1, source_target_pairs={{0,1},{1,0},{2,3},{3,2},{4,5},{5,4},{6,7},{7,6},{8,9},{9,8},{10,11... | collective-permute-start | bytes 1032200 | tf_op jit(solution)/shard_map/ppermute | solution.py:93
  19.7 8.0 %copy-start.16 = (f32[11,112]{1,0:T(8,128)S(1)}, f32[11,112]{1,0:T(8,128)}, u32[]{:S(2)}) copy-start(f32[11,112]{1,0:T(8,128)} %norm_in_ref.1) | copy-start | bytes 14788
  29.7 2.8 %copy-start.12 = (f32[11,112,112]{2,1,0:T(8,128)S(1)}, f32[11,112,112]{2,1,0:T(8,128)}, u32[]{:S(2)}) copy-start(f32[11,112,112]{2,1,0:T(8,128)} %state_in_ref.1) | copy-start | bytes 1655812
  29.7 21.3 %all-to-all-start.1 = ((f32[32,1,5376]{2,1,0:T(1,128)}), f32[32,1,5376]{2,1,0:T(1,128)S(1)}, u32[]{:S(2)}, u32[]{:S(2)}) async-start(f32[32,1,5376]{2,1,0:T(1,128)} %get-tuple-element.46), calls=%async_computation.1 | async-start | bytes 1376256 | tf_op jit(solution)/shard_map/all_to_all | solution.py:398
  33.4 0.9 %copy-start.10 = (f32[2,6,112,112]{3,2,1,0:T(8,128)}, f32[2,6,112,112]{3,2,1,0:T(8,128)S(1)}, u32[]{:S(2)}) copy-start(f32[2,6,112,112]{3,2,1,0:T(8,128)S(1)} %get-tuple-element.50.before_ref) | copy-start | bytes 1806340
  51.0 1.1 %copy-start.11 = (f32[2,6,112,112]{3,2,1,0:T(8,128)S(1)}, f32[2,6,112,112]{3,2,1,0:T(8,128)}, u32[]{:S(2)}) copy-start(f32[2,6,112,112]{3,2,1,0:T(8,128)} %copy-done.10) | copy-start | bytes 1806340
  53.3 0.8 %copy-start.14 = (f32[32,1,3456]{2,1,0:T(1,128)}, f32[32,1,3456]{2,1,0:T(1,128)S(1)}, u32[]{:S(2)}) copy-start(f32[32,1,3456]{2,1,0:T(1,128)S(1)} %get-tuple-element.53) | copy-start | bytes 1327108
  54.1 17.6 %all-to-all-start.2 = ((f32[32,1,3456]{2,1,0:T(1,128)}), f32[32,1,3456]{2,1,0:T(1,128)S(1)}, u32[]{:S(2)}, u32[]{:S(2)}) async-start(f32[32,1,3456]{2,1,0:T(1,128)} %copy-done.14), calls=%async_computation.2 | async-start | bytes 884736 | tf_op jit(solution)/shard_map/all_to_all | solution.py:398
  57.6 2.2 %copy-start.13 = (f32[11,112,112]{2,1,0:T(8,128)S(1)}, f32[11,112,112]{2,1,0:T(8,128)}, u32[]{:S(2)}) copy-start(f32[11,112,112]{2,1,0:T(8,128)} %grad_state_ref.1) | copy-start | bytes 1655812
  59.5 3.4 %collective-permute-start.5 = (f32[672,128]{1,0:T(8,128)S(1)}, f32[672,128]{1,0:T(8,128)S(1)}, u32[]{:S(2)}, u32[]{:S(2)}) collective-permute-start(f32[672,128]{1,0:T(8,128)S(1)} %get-tuple-element.58), channel_id=1, source_target_pairs={{0,1},{1,0},{2,3},{3,2},{4,5},{5,4},{6,7},{7,6},{8,9},{9,8},{10,11... | collective-permute-start | bytes 1032200 | tf_op jit(solution)/shard_map/ppermute | solution.py:93
  61.0 1.0 %copy-start.4 = (f32[3,6,112,128]{3,2,1,0:T(8,128)}, f32[3,6,112,128]{3,2,1,0:T(8,128)S(1)}, u32[]{:S(2)}) copy-start(f32[3,6,112,128]{3,2,1,0:T(8,128)S(1)} %get-tuple-element.62.final_ref) | copy-start | bytes 3096580
  62.0 1.0 %copy-start.6 = (f32[3,6,112,128]{3,2,1,0:T(8,128)}, f32[3,6,112,128]{3,2,1,0:T(8,128)S(1)}, u32[]{:S(2)}) copy-start(f32[3,6,112,128]{3,2,1,0:T(8,128)S(1)} %get-tuple-element.66.final_ref) | copy-start | bytes 3096580
  63.0 8.8 %copy-start.15 = (f32[11,112]{1,0:T(8,128)S(1)}, f32[11,112]{1,0:T(8,128)}, u32[]{:S(2)}) copy-start(f32[11,112]{1,0:T(8,128)} %grad_norm_ref.3) | copy-start | bytes 14788
  71.7 1.2 %copy-start.7 = (f32[3,6,112,128]{3,2,1,0:T(8,128)S(1)}, f32[3,6,112,128]{3,2,1,0:T(8,128)}, u32[]{:S(2)}) copy-start(f32[3,6,112,128]{3,2,1,0:T(8,128)} %copy-done.6) | copy-start | bytes 3096580
  72.9 1.7 %copy-start.5 = (f32[3,6,112,128]{3,2,1,0:T(8,128)S(1)}, f32[3,6,112,128]{3,2,1,0:T(8,128)}, u32[]{:S(2)}) copy-start(f32[3,6,112,128]{3,2,1,0:T(8,128)} %copy-done.4) | copy-start | bytes 3096580
  74.0 1.7 %collective-permute-start.6 = (f32[672,128]{1,0:T(8,128)S(1)}, f32[672,128]{1,0:T(8,128)S(1)}, u32[]{:S(2)}, u32[]{:S(2)}) collective-permute-start(f32[672,128]{1,0:T(8,128)S(1)} %get-tuple-element.67), channel_id=1, source_target_pairs={{0,1},{1,0},{2,3},{3,2},{4,5},{5,4},{6,7},{7,6},{8,9},{9,8},{10,11... | collective-permute-start | bytes 1032200 | tf_op jit(solution)/shard_map/ppermute | solution.py:93
  74.1 2.1 %collective-permute-start.7 = (f32[672,128]{1,0:T(8,128)S(1)}, f32[672,128]{1,0:T(8,128)S(1)}, u32[]{:S(2)}, u32[]{:S(2)}) collective-permute-start(f32[672,128]{1,0:T(8,128)S(1)} %get-tuple-element.68), channel_id=1, source_target_pairs={{0,1},{1,0},{2,3},{3,2},{4,5},{5,4},{6,7},{7,6},{8,9},{9,8},{10,11... | collective-permute-start | bytes 1032200 | tf_op jit(solution)/shard_map/ppermute | solution.py:93

commit v3 on v2

--- a/solution.py
+++ b/solution.py
@@ -59,7 +59,11 @@
         self.per_slot = devices // SUB
         self.head_tiles = width // SUB
         self.tiles = self.half * self.head_tiles
-        self.slots = -(-self.tiles // self.per_slot)
+        self.spare = LANES - width
+        self.pieces = width // self.spare if self.spare and width % self.spare == 0 else 0
+        self.donors = self.tiles // (self.pieces + 1) if self.pieces else 0
+        self.stored = self.tiles - self.donors
+        self.slots = -(-self.stored // self.per_slot)
         self.span = self.slots * LANES
 
     def place(self, base, tile):
@@ -100,21 +104,41 @@
     return jnp.concatenate([tile, jnp.zeros((rows, LANES - columns), tile.dtype)], axis=1)
 
 
-def store_rows(plan, ref, base, head, block):
+def store_rows(plan, ref, base, head, block, held):
     block = wide(block)
+    lane = lax.broadcasted_iota(jnp.int32, (SUB, LANES), 1)
     for j in range(plan.head_tiles):
-        ref[plan.place(base, head * plan.head_tiles + j)] = block[j * SUB : (j + 1) * SUB, :]
+        at = head * plan.head_tiles + j
+        tile = block[j * SUB : (j + 1) * SUB, :]
+        if at >= plan.stored:
+            held[at - plan.stored] = tile
+            continue
+        if at < plan.donors * plan.pieces:
+            donor, piece = divmod(at, plan.pieces)
+            moved = pltpu.roll(held[donor], plan.width - piece * plan.spare, 1)
+            tile = jnp.where(lane >= plan.width, moved, tile)
+        ref[plan.place(base, at)] = tile
 
 
 def store_padding(plan, ref, base):
-    for tile in range(plan.tiles, plan.slots * plan.per_slot):
+    for tile in range(plan.stored, plan.slots * plan.per_slot):
         ref[plan.place(base, tile)] = jnp.zeros((SUB, LANES), F32)
 
 
 def load_rows(plan, ref, base, head):
+    lane = lax.broadcasted_iota(jnp.int32, (SUB, LANES), 1)
     tiles = []
     for j in range(plan.head_tiles):
-        tiles.append(ref[plan.place(base, head * plan.head_tiles + j)])
+        at = head * plan.head_tiles + j
+        if at < plan.stored:
+            tiles.append(ref[plan.place(base, at)])
+            continue
+        tile = None
+        for piece in range(plan.pieces):
+            part = ref[plan.place(base, (at - plan.stored) * plan.pieces + piece)]
+            part = pltpu.roll(part, (LANES - plan.width + piece * plan.spare) % LANES, 1)
+            tile = part if tile is None else jnp.where(lane >= piece * plan.spare, part, tile)
+        tiles.append(tile)
     return jnp.concatenate(tiles, axis=0)[:, : plan.width]
 
 
@@ -157,6 +181,10 @@
     row = lax.broadcasted_iota(jnp.int32, (length, length), 0)
     column = lax.broadcasted_iota(jnp.int32, (length, length), 1)
     return row <= column
+
+
+def scores_of(a, b, causal):
+    return jnp.where(causal, tn(b, a), 0.0)
 
 
 def relu(x):
@@ -176,9 +204,10 @@
 
 
 def chip_state(plan, own_ref, got_ref, out_ref):
-    for h in range(plan.half):
+    held = {}
+    for h in reversed(range(plan.half)):
         rows = slice(h * plan.width, (h + 1) * plan.width)
-        store_rows(plan, out_ref, 0, h, own_ref[rows, :] + got_ref[rows, :])
+        store_rows(plan, out_ref, 0, h, own_ref[rows, :] + got_ref[rows, :], held)
         row = slice(plan.rows + h, plan.rows + h + 1)
         norm = jnp.broadcast_to(own_ref[row, :] + got_ref[row, :], (plan.devices, LANES))
         out_ref[:, 0, plan.row_slot(h)] = norm
@@ -187,7 +216,7 @@
 
 def pack_tokens(
     plan, ids_ref, q_ref, k_ref, v_ref, g_ref, q_got_ref, k_got_ref, v_got_ref, g_got_ref,
-    a_ref, b_ref, vb_ref, gb_ref, low_ref, sum_ref, norm_ref,
+    a_ref, b_ref, vb_ref, gb_ref, sum_ref, norm_ref,
 ):
     core = ids_ref[0]
     causal = causal_mask(plan.length)
@@ -199,9 +228,8 @@
                 x = plan.other(pair[1], h).astype(BF16) if i else plan.own(pair[0], core, h)
                 ref[i, h] = relu(x) if n < 2 else x
             a, b = a_ref[i, h], b_ref[i, h]
-            scores = jnp.where(causal, tn(b, a), 0.0)
+            scores = scores_of(a, b, causal)
             sum_ref[i, h : h + 1, :] = 1.0 + jnp.sum(scores, axis=0, keepdims=True)
-            low_ref[i, h] = scores.astype(BF16)
             norm_ref[i, h : h + 1, :] = wide(nt(ones, b))[0:1]
 
 
@@ -214,7 +242,8 @@
     width = plan.width
     norms = scan_norms(plan, in_ref, core, chip, False)
     scan_rows(plan, in_ref, 0, out_ref, False)
-    for h in range(plan.half):
+    held = {}
+    for h in reversed(range(plan.half)):
         base = norm_in_ref[pl.ds(core * plan.shift + h, 1), :]
         base = base + norms[0:1, h * LANES : h * LANES + width]
         features, grads = [], []
@@ -228,19 +257,21 @@
             features.append(a)
             grads.append((g_ref[i, h].astype(F32) * inverse).astype(BF16))
         state = nt(jnp.concatenate(features, axis=1), jnp.concatenate(grads, axis=1))
-        store_rows(plan, out_ref, plan.slots, h, state)
+        store_rows(plan, out_ref, plan.slots, h, state, held)
     store_padding(plan, out_ref, plan.slots)
 
 
 def before_states(
-    plan, ids_ref, a_ref, b_ref, v_ref, g_ref, low_ref, state_in_ref, before_ref, inner_ref
+    plan, ids_ref, a_ref, b_ref, v_ref, g_ref, state_in_ref, before_ref, inner_ref
 ):
     core = ids_ref[0]
+    causal = causal_mask(plan.length)
     own_first = core == 0
     late = (core.astype(F32), (1 - core).astype(F32))
     for h in range(plan.half):
         for i in range(2):
-            inner = nn(v_ref[i, h], low_ref[i, h])
+            low = scores_of(a_ref[i, h], b_ref[i, h], causal).astype(BF16)
+            inner = nn(v_ref[i, h], low)
             inner_ref[i, h : h + 1, :] = jnp.sum(
                 g_ref[i, h].astype(F32) * inner, axis=0, keepdims=True
             )
@@ -296,28 +327,30 @@
 
 
 def after_states(
-    plan, ids_ref, a_ref, g_ref, inverse_ref, low_ref, mixed_ref, grad_state_ref,
-    final_0_ref, final_1_ref,
+    plan, ids_ref, a_ref, b_ref, g_ref, inverse_ref, mixed_ref, grad_state_ref, *refs
 ):
     core = ids_ref[0]
+    causal = causal_mask(plan.length)
     own_first = core == 0
     early = ((1 - core).astype(F32), core.astype(F32))
     for h in range(plan.half):
         us = []
-        for i, ref in enumerate((final_0_ref, final_1_ref)):
+        for i in range(2):
             u = (g_ref[i, h].astype(F32) * inverse_ref[i, h : h + 1, :]).astype(BF16)
             us.append(u)
-            ref[1, h] = nt(a_ref[i, h], mixed_ref[i, h])
-            ref[2, h] = nt(u, low_ref[i, h])
+            low = scores_of(a_ref[i, h], b_ref[i, h], causal).astype(BF16)
+            refs[3 * i + 1][h] = nt(a_ref[i, h], mixed_ref[i, h])
+            refs[3 * i + 2][h] = nt(u, low)
         a = jnp.where(own_first, a_ref[1, h].astype(F32), a_ref[0, h].astype(F32)).astype(BF16)
         u = jnp.where(own_first, us[1].astype(F32), us[0].astype(F32)).astype(BF16)
         second = nt(a, u)
-        for i, ref in enumerate((final_0_ref, final_1_ref)):
-            ref[0, h] = wide(grad_state_ref[core * plan.shift + h] + early[i] * second)
+        for i in range(2):
+            refs[3 * i][h] = grad_state_ref[core * plan.shift + h] + early[i] * second
 
 
 def key_value_grads(
-    plan, i, ids_ref, in_ref, final_ref, grad_norm_ref, m_ref, b_ref, v_ref, key_ref, value_ref
+    plan, i, ids_ref, in_ref, after_ref, key_in_ref, value_in_ref, grad_norm_ref, m_ref, b_ref,
+    v_ref, key_ref, value_ref,
 ):
     core, chip = ids_ref[0], ids_ref[1]
     flag = (core if i else 1 - core).astype(F32)
@@ -335,12 +368,12 @@
     columns = (norms + flag * m_ref[1 - i]).T
     for h in range(plan.half):
         rows = slice(h * width, (h + 1) * width)
-        high, low = parts(load_rows(plan, in_ref, 0, h) + final_ref[0, h, :, :width])
+        high, low = parts(load_rows(plan, in_ref, 0, h) + after_ref[h])
         b, v = b_ref[i, h], v_ref[i, h]
         both = nn(jnp.concatenate([high, low], axis=0), v)
-        key = both[:width] + both[width:] + columns[:width, h : h + 1] + final_ref[1, h]
+        key = both[:width] + both[width:] + columns[:width, h : h + 1] + key_in_ref[h]
         key = jnp.where(b.astype(F32) > 0, key, 0.0)
-        value = tn(high, b) + tn(low, b) + final_ref[2, h]
+        value = tn(high, b) + tn(low, b) + value_in_ref[h]
         key_ref[rows, :] = key.astype(key_ref.dtype)
         value_ref[rows, :] = value.astype(value_ref.dtype)
 
@@ -407,7 +440,8 @@
     square = shape((2, half, length, length), BF16)
     states = shape((2, half, width, width))
     rows = shape((2, plan.extra, LANES))
-    final = shape((3, half, width, LANES))
+    after = shape((half, width, width))
+    part = shape((half, width, length))
     block = shape((plan.rows + plan.extra, LANES))
     sent_single = shape((devices, 1, plan.span + half * LANES))
     sent_double = shape((devices, 1, 2 * plan.span))
@@ -418,9 +452,9 @@
     (sent,) = call(bind(chip_state), (sent_single,), (block_own, block_got))
     sent, k, v, q, g = lax.optimization_barrier((sent, k, v, q, g))
     got = exchange(sent)
-    a, b, v, g, low, sums, norm = call(
+    a, b, v, g, sums, norm = call(
         bind(pack_tokens),
-        (packed, packed, packed, packed, square, rows, rows),
+        (packed, packed, packed, packed, rows, rows),
         (who, q, k, v, g, *(swap_columns(x) for x in (q, k, v, g))),
     )
     sent, inverse, z = call(
@@ -430,7 +464,7 @@
     )
     got = exchange(sent)
     before, inner = call(
-        bind(before_states), (states, rows), (who, a, b, v, g, low, state_in)
+        bind(before_states), (states, rows), (who, a, b, v, g, state_in)
     )
     sent, product, c, m = call(
         bind(outputs_grad),
@@ -442,8 +476,8 @@
         bind(query_grads), (tokens, tokens, square), (who, a, b, v, g, inverse, c, z, product)
     )
     query_got = pair_swap(query_send)
-    final_0, final_1 = call(
-        bind(after_states), (final, final), (who, a, g, inverse, low, mixed, grad_state)
+    finals = call(
+        bind(after_states), (after, part, part) * 2, (who, a, b, g, inverse, mixed, grad_state)
     )
     whole = shape((heads * width, length), BF16)
     (query_grad,) = call(bind(assemble), (whole,), (who, query, query_got))
@@ -451,14 +485,14 @@
     key_send, value_send = call(
         functools.partial(key_value_grads, plan, 1),
         (tokens, tokens),
-        (who, got, final_1, grad_norm, m, b, v),
+        (who, got, *finals[3:], grad_norm, m, b, v),
     )
     key_got, value_got = pair_swap(key_send), pair_swap(value_send)
     half_tokens = shape((plan.rows, length), BF16)
     key, value = call(
         functools.partial(key_value_grads, plan, 0),
         (half_tokens, half_tokens),
-        (who, got, final_0, grad_norm, m, b, v),
+        (who, got, *finals[:3], grad_norm, m, b, v),
     )
     key_grad, value_grad = call(
         bind(assemble), (whole, whole), (who, key, value, key_got, value_got)

time: 78.2 us -> 73.4 us (0.939)
  local copies, waits for them, and re-layouts: 10.6 us -> 4.38 us
  Pallas kernels: 15.9 us -> 18.2 us
    unnamed x34 -> x26, local copies, waits for them, and re-layouts: 10.6 us -> 4.38 us
    pallas_call x13, Pallas kernels: 15.9 us -> 18.2 us  [call(): pl.pallas_call(body, out_shape=outs, in_specs=in_specs, out_specs=[vmem]...]
  transfers between devices with their start and end apart: 11 -> 11, of which waited for: 9 -> 9; matrix products, arithmetic and copies ran while one was open for 0% -> 0% of each run, Pallas kernels for 11% -> 14%
where the time goes in v3:
time: 73.4 us; the launch traced here: 73 us
  waiting for transfers between devices  33.7 us (46%)
  Pallas kernels  18.2 us (25%)
  starting transfers between devices  15.7 us (21%)
  local copies, waits for them, and re-layouts  4.38 us (6%)
  between operations  0.82 us (1%)
    all_to_all x3, waiting for transfers between devices, exchange(): return lax.all_to_all(x, both, 0, 0, tiled=True)  30.8 us
    pallas_call x13, Pallas kernels, call(): pl.pallas_call(body, out_shape=outs, in_specs=in_specs, out_specs=[vmem]...  18.2 us
    all_to_all x3, starting transfers between devices, exchange(): return lax.all_to_all(x, both, 0, 0, tiled=True)  13.2 us
    unnamed x26, local copies, waits for them, and re-layouts  4.38 us
    ppermute x8, waiting for transfers between devices, pair_swap(): return lax.ppermute(x, 'seq', [(i, i ^ 1) for i in range(size)])  2.91 us
    ppermute x8, starting transfers between devices, pair_swap(): return lax.ppermute(x, 'seq', [(i, i ^ 1) for i in range(size)])  2.53 us
  transfers between devices with their start and end apart: 11, of which 9 were waited for; matrix products, arithmetic and copies ran while one was open for 0% of the time, Pallas kernels for 14%

profile of v3, /device:TPU:0, one launch (start us, length us, event | category | flops | bytes accessed | tf_op | source)
XLA Modules:
  0.0 73.0 jit_solution(4745564843477070982)
XLA Ops:
  0.6 0.1 pad_add_fusion.ids_ref
  0.7 1.0 %copy-done = bf16[128,1232]{0,1:T(8,128)(2,1)S(1)} copy-done((bf16[128,1232]{0,1:T(8,128)(2,1)S(1)}, bf16[128,1232]{0,1:T(8,128)(2,1)}, u32[]{:S(2)}) %copy-start) | copy-done | bytes 315416
  1.7 1.0 %copy-done.2 = bf16[128,1232]{0,1:T(8,128)(2,1)S(1)} copy-done((bf16[128,1232]{0,1:T(8,128)(2,1)S(1)}, bf16[128,1232]{0,1:T(8,128)(2,1)}, u32[]{:S(2)}) %copy-start.2) | copy-done | bytes 315416
  2.7 0.9 %shard_map.104 = f32[680,128]{1,0:T(8,128)S(1)} custom-call(s32[2]{0:T(128)S(1)} %pad_add_fusion.ids_ref, bf16[1232,128]{1,0:T(8,128)(2,1)S(1)} %bitcast.9, bf16[1232,128]{1,0:T(8,128)(2,1)S(1)} %bitcast.13), custom_call_target="tpu_custom_call" | custom-call | flops 10000000 | bytes 978952 | tf_op jit(solution)/shard_map/pallas_call | solution.py:399
  3.5 0.6 collective-permute-start
  4.1 0.0 copy-done.1
  4.1 0.0 copy-done.3
  4.1 0.9 %shard_map.103.own_ref = f32[680,128]{1,0:T(8,128)S(1)} custom-call(s32[2]{0:T(128)S(1)} %pad_add_fusion.ids_ref, bf16[1232,128]{1,0:T(8,128)(2,1)S(1)} %bitcast.10, bf16[1232,128]{1,0:T(8,128)(2,1)S(1)} %bitcast.14), custom_call_target="tpu_custom_call" | custom-call | flops 10000000 | bytes 978952 | tf_op jit(solution)/shard_map/pallas_call | solution.py:399
  5.0 0.4 collective-permute-done.got_ref
  5.4 1.1 %shard_map.105 = f32[32,1,3200]{2,1,0:T(1,128)} custom-call(f32[680,128]{1,0:T(8,128)S(1)} %shard_map.103.own_ref, f32[680,128]{1,0:T(8,128)S(1)} %collective-permute-done.got_ref), custom_call_target="tpu_custom_call" | custom-call | flops 10000000 | bytes 1105920 | tf_op jit(solution)/shard_map/pallas_call | solution.py:399
  6.4 7.2 %all-to-all-start = ((f32[32,1,3200]{2,1,0:T(1,128)}), f32[32,1,3200]{2,1,0:T(1,128)S(1)}, u32[]{:S(2)}, u32[]{:S(2)}) async-start(f32[32,1,3200]{2,1,0:T(1,128)} %shard_map.105), calls=%async_computation | async-start | bytes 819200 | tf_op jit(solution)/shard_map/all_to_all | solution.py:431
  13.6 0.0 copy-done.4
  13.7 0.0 copy-start.5
  13.8 0.9 %copy-done.5 = bf16[128,1232]{0,1:T(8,128)(2,1)S(1)} copy-done((bf16[128,1232]{0,1:T(8,128)(2,1)S(1)}, bf16[128,1232]{0,1:T(8,128)(2,1)}, u32[]{:S(2)}) %copy-start.5) | copy-done | bytes 315416
  14.7 0.3 collective-permute-start.4
  15.1 0.3 collective-permute-start.3
  15.3 0.3 collective-permute-start.2
  15.6 0.3 collective-permute-start.1
  15.8 0.6 collective-permute-done.4.g_got_ref
  16.5 0.5 collective-permute-done.3.v_got_ref
  16.9 0.5 collective-permute-done.2.k_got_ref
  17.4 0.5 collective-permute-done.1.q_got_ref
  17.9 1.1 %shard_map.106 = (bf16[2,6,112,128]{3,2,1,0:T(8,128)(2,1)S(1)}, bf16[2,6,112,128]{3,2,1,0:T(8,128)(2,1)S(1)}, bf16[2,6,112,128]{3,2,1,0:T(8,128)(2,1)S(1)}, bf16...) custom-call(s32[2]{0:T(128)S(1)} %pad_add_fusion.ids_ref, ...), custom_call_target="tpu_custom_call" | custom-call | flops 10000000 | bytes 4030472 | tf_op jit(solution)/shard_map/pallas_call | solution.py:399
  19.0 8.2 %all-to-all-done.in_ref = f32[32,1,3200]{2,1,0:T(1,128)S(1)} async-done(((f32[32,1,3200]{2,1,0:T(1,128)}), f32[32,1,3200]{2,1,0:T(1,128)S(1)}, u32[]{:S(2)}, u32[]{:S(2)}) %all-to-all-start) | async-done | bytes 409632 | tf_op jit(solution)/shard_map/all_to_all | solution.py:431
  27.2 0.0 copy-done.12
  27.2 2.0 %shard_map.107 = (f32[32,1,4864]{2,1,0:T(1,128)}, f32[2,8,128]{2,1,0:T(8,128)S(1)}, f32[2,8,128]{2,1,0:T(8,128)S(1)}) custom-call(s32[2]{0:T(128)S(1)} %pad_add_fusion.ids_ref, f32[32,1,3200]{2,1,0:T(1,128)S(1)} %all-to-all-done.in_ref, f32[2,8,128]{2,1,0:T(8,128)S(1)} %get-tuple-element.45.sum_ref, bf16[2,6,112,128]{3,2,1,0:T(8,128)(2,1)S(1)} %get-tuple-element.46.a_ref, ...), custom_call_target="tpu_custom_call" | custom-call | flops 10000000 | bytes 1758024 | tf_op jit(solution)/shard_map/pallas_call | solution.py:399
  29.2 2.7 %all-to-all-start.1 = ((f32[32,1,4864]{2,1,0:T(1,128)}), f32[32,1,4864]{2,1,0:T(1,128)S(1)}, u32[]{:S(2)}, u32[]{:S(2)}) async-start(f32[32,1,4864]{2,1,0:T(1,128)} %get-tuple-element.49), calls=%async_computation.1 | async-start | bytes 1245184 | tf_op jit(solution)/shard_map/all_to_all | solution.py:431
  31.9 1.9 %shard_map.108 = (f32[2,6,112,112]{3,2,1,0:T(8,128)S(1)}, f32[2,8,128]{2,1,0:T(8,128)S(1)}) custom-call(s32[2]{0:T(128)S(1)} %pad_add_fusion.ids_ref, bf16[2,6,112,128]{3,2,1,0:T(8,128)(2,1)S(1)} %get-tuple-element.46.a_ref, bf16[2,6,112,128]{3,2,1,0:T(8,128)(2,1)S(1)} %get-tuple-element.50.b_ref, bf16[2,6,112,128]{3,2,1,0:T(8,128)(2,1)S(1)} %get-tuple-element.51.v_ref, ...), custom_call_target="tpu_custom_call" | custom-call | flops 10000000 | bytes 2538504 | tf_op jit(solution)/shard_map/pallas_call | solution.py:399
  33.8 15.5 %all-to-all-done.1.in_ref = f32[32,1,4864]{2,1,0:T(1,128)S(1)} async-done(((f32[32,1,4864]{2,1,0:T(1,128)}), f32[32,1,4864]{2,1,0:T(1,128)S(1)}, u32[]{:S(2)}, u32[]{:S(2)}) %all-to-all-start.1) | async-done | bytes 622624 | tf_op jit(solution)/shard_map/all_to_all | solution.py:431
  49.3 1.3 %shard_map.109 = (f32[32,1,3200]{2,1,0:T(1,128)S(1)}, f32[2,6,112,128]{3,2,1,0:T(8,128)S(1)}, f32[2,8,128]{2,1,0:T(8,128)S(1)}, f32[2,8,128]{2,1,0:T(8,128)S(1)}) custom-call(s32[2]{0:T(128)S(1)} %pad_add_fusion.ids_ref, f32[32,1,4864]{2,1,0:T(1,128)S(1)} %all-to-all-done.1.in_ref, f32[2,6,112,112]{3,2,1,0:T(8,128)S(1)} %get-tuple-element.52.before_ref, ...), custom_call_target="tpu_custom_call" | custom-call | flops 10000000 | bytes 3043336 | tf_op jit(solution)/shard_map/pallas_call | solution.py:399
  50.6 0.7 %copy-done.8 = f32[32,1,3200]{2,1,0:T(1,128)} copy-done((f32[32,1,3200]{2,1,0:T(1,128)}, f32[32,1,3200]{2,1,0:T(1,128)S(1)}, u32[]{:S(2)}) %copy-start.8) | copy-done | bytes 409624
  51.3 3.2 %all-to-all-start.2 = ((f32[32,1,3200]{2,1,0:T(1,128)}), f32[32,1,3200]{2,1,0:T(1,128)S(1)}, u32[]{:S(2)}, u32[]{:S(2)}) async-start(f32[32,1,3200]{2,1,0:T(1,128)} %copy-done.8), calls=%async_computation.2 | async-start | bytes 819200 | tf_op jit(solution)/shard_map/all_to_all | solution.py:431
  54.6 0.0 copy-start.6
  54.6 1.9 %shard_map.110 = (f32[672,128]{1,0:T(8,128)S(1)}, f32[672,128]{1,0:T(8,128)S(1)}, bf16[2,6,128,128]{3,2,1,0:T(8,128)(2,1)S(1)}) custom-call(s32[2]{0:T(128)S(1)} %pad_add_fusion.ids_ref, bf16[2,6,112,128]{3,2,1,0:T(8,128)(2,1)S(1)} %get-tuple-element.46.a_ref, bf16[2,6,112,128]{3,2,1,0:T(8,128)(2,1)S(1)} %get-tuple-element.50.b_ref, ...), custom_call_target="tpu_custom_call" | custom-call | flops 10000000 | bytes 3170312 | tf_op jit(solution)/shard_map/pallas_call | solution.py:399
  56.5 0.3 collective-permute-start.5
  56.8 2.1 %shard_map.112 = (f32[6,112,112]{2,1,0:T(8,128)S(1)}, f32[6,112,128]{2,1,0:T(8,128)S(1)}, f32[6,112,128]{2,1,0:T(8,128)S(1)}, f32[6,112,112]{2,1,0:T(8,128)S(1)}...) custom-call(s32[2]{0:T(128)S(1)} %pad_add_fusion.ids_ref, bf16[2,6,112,128]{3,2,1,0:T(8,128)(2,1)S(1)} %get-tuple-element.46.a_ref, ...), custom_call_target="tpu_custom_call" | custom-call | flops 10000000 | bytes 3963912 | tf_op jit(solution)/shard_map/pallas_call | solution.py:399
  59.0 0.0 copy-start.9
  59.0 0.7 %copy-done.9 = f32[6,112,128]{2,1,0:T(8,128)} copy-done((f32[6,112,128]{2,1,0:T(8,128)}, f32[6,112,128]{2,1,0:T(8,128)S(1)}, u32[]{:S(2)}) %copy-start.9) | copy-done | bytes 344088
  59.7 0.0 collective-permute-done.5.refs_1_
  59.7 1.3 %shard_map.111 = bf16[1232,128]{1,0:T(8,128)(2,1)} custom-call(s32[2]{0:T(128)S(1)} %pad_add_fusion.ids_ref, f32[672,128]{1,0:T(8,128)S(1)} %get-tuple-element.59.refs_0_, f32[672,128]{1,0:T(8,128)S(1)} %collective-permute-done.5.refs_1_), custom_call_target="tpu_custom_call" | custom-call | flops 10000000 | bytes 1003528 | tf_op jit(solution)/shard_map/pallas_call | solution.py:399
  61.0 7.1 %all-to-all-done.2.in_ref = f32[32,1,3200]{2,1,0:T(1,128)S(1)} async-done(((f32[32,1,3200]{2,1,0:T(1,128)}), f32[32,1,3200]{2,1,0:T(1,128)S(1)}, u32[]{:S(2)}, u32[]{:S(2)}) %all-to-all-start.2) | async-done | bytes 409632 | tf_op jit(solution)/shard_map/all_to_all | solution.py:431
  68.1 1.2 %shard_map.114 = (f32[672,128]{1,0:T(8,128)S(1)}, f32[672,128]{1,0:T(8,128)S(1)}) custom-call(s32[2]{0:T(128)S(1)} %pad_add_fusion.ids_ref, f32[32,1,3200]{2,1,0:T(1,128)S(1)} %all-to-all-done.2.in_ref, f32[6,112,112]{2,1,0:T(8,128)S(1)} %get-tuple-element.70.after_ref, f32[6,112,128]{2,1,0:T(8,128)S(1)} %get-tuple-element.71.key_in_ref, ...), custom_call_target="tpu_custom_call" | custom-call | flops 10000000 | bytes 2788168 | tf_op jit(solution)/shard_map/pallas_call | solution.py:399
  69.3 0.1 collective-permute-start.6
  69.4 0.5 collective-permute-start.7
  69.9 1.2 %shard_map.113 = (bf16[672,128]{1,0:T(8,128)(2,1)S(1)}, bf16[672,128]{1,0:T(8,128)(2,1)S(1)}) custom-call(s32[2]{0:T(128)S(1)} %pad_add_fusion.ids_ref, f32[32,1,3200]{2,1,0:T(1,128)S(1)} %all-to-all-done.2.in_ref, f32[6,112,112]{2,1,0:T(8,128)S(1)} %get-tuple-element.64.after_ref, f32[6,112,128]{2,1,0:T(8,128)S(1)} %get-tuple-element.65.key_in_ref, ...), custom_call_target="tpu_custom_call" | custom-call | flops 10000000 | bytes 2444104 | tf_op jit(solution)/shard_map/pallas_call | solution.py:399
  71.1 0.0 collective-permute-done.6.refs_2_
  71.1 0.4 collective-permute-done.7.refs_3_
  71.5 1.4 %shard_map.115 = (bf16[1232,128]{1,0:T(8,128)(2,1)}, bf16[1232,128]{1,0:T(8,128)(2,1)}) custom-call(s32[2]{0:T(128)S(1)} %pad_add_fusion.ids_ref, bf16[672,128]{1,0:T(8,128)(2,1)S(1)} %get-tuple-element.68.refs_0_, bf16[672,128]{1,0:T(8,128)(2,1)S(1)} %get-tuple-element.69.refs_1_, f32[672,128]{1,0:T(8,128)S(1)} %collective-permute-done.6.refs_2_, ...), custom_call_target="tpu_custom_call" | custom-call | flops 10000000 | bytes 1662984 | tf_op jit(solution)/shard_map/pallas_call | solution.py:399
  (18 shorter events, 0.1 us)
Async XLA Ops:
  0.7 1.0 %copy-start = (bf16[128,1232]{0,1:T(8,128)(2,1)S(1)}, bf16[128,1232]{0,1:T(8,128)(2,1)}, u32[]{:S(2)}) copy-start(bf16[128,1232]{0,1:T(8,128)(2,1)} %param.9) | copy-start | bytes 946180
  1.7 1.0 %copy-start.2 = (bf16[128,1232]{0,1:T(8,128)(2,1)S(1)}, bf16[128,1232]{0,1:T(8,128)(2,1)}, u32[]{:S(2)}) copy-start(bf16[128,1232]{0,1:T(8,128)(2,1)} %param.10) | copy-start | bytes 946180
  2.6 1.4 %copy-start.1 = (bf16[128,1232]{0,1:T(8,128)(2,1)S(1)}, bf16[128,1232]{0,1:T(8,128)(2,1)}, u32[]{:S(2)}) copy-start(bf16[128,1232]{0,1:T(8,128)(2,1)} %param.9) | copy-start | bytes 946180
  2.7 1.4 %copy-start.3 = (bf16[128,1232]{0,1:T(8,128)(2,1)S(1)}, bf16[128,1232]{0,1:T(8,128)(2,1)}, u32[]{:S(2)}) copy-start(bf16[128,1232]{0,1:T(8,128)(2,1)} %param.10) | copy-start | bytes 946180
  3.5 1.8 %collective-permute-start = (f32[680,128]{1,0:T(8,128)S(1)}, f32[680,128]{1,0:T(8,128)S(1)}, u32[]{:S(2)}, u32[]{:S(2)}) collective-permute-start(f32[680,128]{1,0:T(8,128)S(1)} %shard_map.104), channel_id=1, source_target_pairs={{0,1},{1,0},{2,3},{3,2},{4,5},{5,4},{6,7},{7,6},{8,9},{9,8},{10,11... | collective-permute-start | bytes 1044488 | tf_op jit(solution)/shard_map/ppermute | solution.py:97
  6.4 7.2 %copy-start.4 = (bf16[128,1232]{0,1:T(8,128)(2,1)S(1)}, bf16[128,1232]{0,1:T(8,128)(2,1)}, u32[]{:S(2)}) copy-start(bf16[128,1232]{0,1:T(8,128)(2,1)} %param.8) | copy-start | bytes 946180
  6.4 20.8 %all-to-all-start = ((f32[32,1,3200]{2,1,0:T(1,128)}), f32[32,1,3200]{2,1,0:T(1,128)S(1)}, u32[]{:S(2)}, u32[]{:S(2)}) async-start(f32[32,1,3200]{2,1,0:T(1,128)} %shard_map.105), calls=%async_computation | async-start | bytes 819200 | tf_op jit(solution)/shard_map/all_to_all | solution.py:431
  13.7 1.0 %copy-start.5 = (bf16[128,1232]{0,1:T(8,128)(2,1)S(1)}, bf16[128,1232]{0,1:T(8,128)(2,1)}, u32[]{:S(2)}) copy-start(bf16[128,1232]{0,1:T(8,128)(2,1)} %param.11) | copy-start | bytes 946180
  14.7 1.7 %collective-permute-start.4 = (f32[672,128]{1,0:T(8,128)S(1)}, f32[672,128]{1,0:T(8,128)S(1)}, u32[]{:S(2)}, u32[]{:S(2)}) collective-permute-start(f32[672,128]{1,0:T(8,128)S(1)} %dynamic-slice_convert_fusion), channel_id=1, source_target_pairs={{0,1},{1,0},{2,3},{3,2},{4,5},{5,4},{6,7},{7,6},{8,9},{9,8},{10,11... | collective-permute-start | bytes 1032200 | tf_op jit(solution)/shard_map/ppermute | solution.py:97
  15.1 1.9 %collective-permute-start.3 = (f32[672,128]{1,0:T(8,128)S(1)}, f32[672,128]{1,0:T(8,128)S(1)}, u32[]{:S(2)}, u32[]{:S(2)}) collective-permute-start(f32[672,128]{1,0:T(8,128)S(1)} %dynamic-slice_convert_fusion.1), channel_id=1, source_target_pairs={{0,1},{1,0},{2,3},{3,2},{4,5},{5,4},{6,7},{7,6},{8,9},{9,8},{10,11... | collective-permute-start | bytes 1032200 | tf_op jit(solution)/shard_map/ppermute | solution.py:97
  15.3 2.1 %collective-permute-start.2 = (f32[672,128]{1,0:T(8,128)S(1)}, f32[672,128]{1,0:T(8,128)S(1)}, u32[]{:S(2)}, u32[]{:S(2)}) collective-permute-start(f32[672,128]{1,0:T(8,128)S(1)} %dynamic-slice_convert_fusion.2), channel_id=1, source_target_pairs={{0,1},{1,0},{2,3},{3,2},{4,5},{5,4},{6,7},{7,6},{8,9},{9,8},{10,11... | collective-permute-start | bytes 1032200 | tf_op jit(solution)/shard_map/ppermute | solution.py:97
  15.6 2.4 %collective-permute-start.1 = (f32[672,128]{1,0:T(8,128)S(1)}, f32[672,128]{1,0:T(8,128)S(1)}, u32[]{:S(2)}, u32[]{:S(2)}) collective-permute-start(f32[672,128]{1,0:T(8,128)S(1)} %dynamic-slice_convert_fusion.3), channel_id=1, source_target_pairs={{0,1},{1,0},{2,3},{3,2},{4,5},{5,4},{6,7},{7,6},{8,9},{9,8},{10,11... | collective-permute-start | bytes 1032200 | tf_op jit(solution)/shard_map/ppermute | solution.py:97
  17.9 9.3 %copy-start.12 = (f32[11,112]{1,0:T(8,128)S(1)}, f32[11,112]{1,0:T(8,128)}, u32[]{:S(2)}) copy-start(f32[11,112]{1,0:T(8,128)} %norm_in_ref.1) | copy-start | bytes 14788
  29.2 2.8 %copy-start.7 = (f32[11,112,112]{2,1,0:T(8,128)S(1)}, f32[11,112,112]{2,1,0:T(8,128)}, u32[]{:S(2)}) copy-start(f32[11,112,112]{2,1,0:T(8,128)} %state_in_ref.1) | copy-start | bytes 1655812
  29.2 20.1 %all-to-all-start.1 = ((f32[32,1,4864]{2,1,0:T(1,128)}), f32[32,1,4864]{2,1,0:T(1,128)S(1)}, u32[]{:S(2)}, u32[]{:S(2)}) async-start(f32[32,1,4864]{2,1,0:T(1,128)} %get-tuple-element.49), calls=%async_computation.1 | async-start | bytes 1245184 | tf_op jit(solution)/shard_map/all_to_all | solution.py:431
  50.6 0.7 %copy-start.8 = (f32[32,1,3200]{2,1,0:T(1,128)}, f32[32,1,3200]{2,1,0:T(1,128)S(1)}, u32[]{:S(2)}) copy-start(f32[32,1,3200]{2,1,0:T(1,128)S(1)} %get-tuple-element.55) | copy-start | bytes 1228804
  51.3 16.8 %all-to-all-start.2 = ((f32[32,1,3200]{2,1,0:T(1,128)}), f32[32,1,3200]{2,1,0:T(1,128)S(1)}, u32[]{:S(2)}, u32[]{:S(2)}) async-start(f32[32,1,3200]{2,1,0:T(1,128)} %copy-done.8), calls=%async_computation.2 | async-start | bytes 819200 | tf_op jit(solution)/shard_map/all_to_all | solution.py:431
  54.6 2.2 %copy-start.6 = (f32[11,112,112]{2,1,0:T(8,128)S(1)}, f32[11,112,112]{2,1,0:T(8,128)}, u32[]{:S(2)}) copy-start(f32[11,112,112]{2,1,0:T(8,128)} %grad_state_ref.1) | copy-start | bytes 1655812
  56.5 3.2 %collective-permute-start.5 = (f32[672,128]{1,0:T(8,128)S(1)}, f32[672,128]{1,0:T(8,128)S(1)}, u32[]{:S(2)}, u32[]{:S(2)}) collective-permute-start(f32[672,128]{1,0:T(8,128)S(1)} %get-tuple-element.60), channel_id=1, source_target_pairs={{0,1},{1,0},{2,3},{3,2},{4,5},{5,4},{6,7},{7,6},{8,9},{9,8},{10,11... | collective-permute-start | bytes 1032200 | tf_op jit(solution)/shard_map/ppermute | solution.py:97
  59.0 0.8 %copy-start.9 = (f32[6,112,128]{2,1,0:T(8,128)}, f32[6,112,128]{2,1,0:T(8,128)S(1)}, u32[]{:S(2)}) copy-start(f32[6,112,128]{2,1,0:T(8,128)S(1)} %get-tuple-element.72.value_in_ref) | copy-start | bytes 1032196
  59.7 8.4 %copy-start.10 = (f32[6,112,128]{2,1,0:T(8,128)S(1)}, f32[6,112,128]{2,1,0:T(8,128)}, u32[]{:S(2)}) copy-start(f32[6,112,128]{2,1,0:T(8,128)} %copy-done.9) | copy-start | bytes 1032196
  59.7 8.4 %copy-start.11 = (f32[11,112]{1,0:T(8,128)S(1)}, f32[11,112]{1,0:T(8,128)}, u32[]{:S(2)}) copy-start(f32[11,112]{1,0:T(8,128)} %grad_norm_ref.3) | copy-start | bytes 14788
  69.3 1.8 %collective-permute-start.6 = (f32[672,128]{1,0:T(8,128)S(1)}, f32[672,128]{1,0:T(8,128)S(1)}, u32[]{:S(2)}, u32[]{:S(2)}) collective-permute-start(f32[672,128]{1,0:T(8,128)S(1)} %get-tuple-element.73), channel_id=1, source_target_pairs={{0,1},{1,0},{2,3},{3,2},{4,5},{5,4},{6,7},{7,6},{8,9},{9,8},{10,11... | collective-permute-start | bytes 1032200 | tf_op jit(solution)/shard_map/ppermute | solution.py:97
  69.4 2.1 %collective-permute-start.7 = (f32[672,128]{1,0:T(8,128)S(1)}, f32[672,128]{1,0:T(8,128)S(1)}, u32[]{:S(2)}, u32[]{:S(2)}) collective-permute-start(f32[672,128]{1,0:T(8,128)S(1)} %get-tuple-element.74), channel_id=1, source_target_pairs={{0,1},{1,0},{2,3},{3,2},{4,5},{5,4},{6,7},{7,6},{8,9},{9,8},{10,11... | collective-permute-start | bytes 1032200 | tf_op jit(solution)/shard_map/ppermute | solution.py:97

commit v4 on v3

--- a/solution.py
+++ b/solution.py
@@ -63,18 +63,29 @@
         self.pieces = width // self.spare if self.spare and width % self.spare == 0 else 0
         self.donors = self.tiles // (self.pieces + 1) if self.pieces else 0
         self.stored = self.tiles - self.donors
-        self.slots = -(-self.stored // self.per_slot)
+        self.whole = self.stored // devices
+        self.slots = self.whole * SUB + -(-(self.stored - self.whole * devices) // self.per_slot)
         self.span = self.slots * LANES
 
+    def put(self, ref, base, tile, value):
+        if tile < self.whole * self.devices:
+            slot, piece = divmod(tile, self.devices)
+            columns = pl.ds((base + slot * SUB) * LANES, SUB * LANES)
+            ref[piece, :, columns] = value.reshape(1, SUB * LANES)
+        else:
+            ref[self.place(base, tile)] = value
+
+    def get(self, ref, base, tile):
+        if tile < self.whole * self.devices:
+            slot, piece = divmod(tile, self.devices)
+            columns = pl.ds((base + slot * SUB) * LANES, SUB * LANES)
+            return ref[piece, :, columns].reshape(SUB, LANES)
+        return ref[self.place(base, tile)]
+
     def place(self, base, tile):
-        slot, part = divmod(tile, self.per_slot)
+        slot, part = divmod(tile - self.whole * self.devices, self.per_slot)
+        slot += self.whole * SUB
         return pl.ds(part * SUB, SUB), 0, pl.ds((base + slot) * LANES, LANES)
-
-    def columns(self, start, count):
-        return slice(None), slice(None), pl.ds(start, count)
-
-    def row_slot(self, head):
-        return pl.ds((self.slots + head) * LANES, LANES)
 
     def own(self, ref, core, head):
         start = pl.multiple_of(core * (self.shift * self.width) + head * self.width, 16)
@@ -117,12 +128,19 @@
             donor, piece = divmod(at, plan.pieces)
             moved = pltpu.roll(held[donor], plan.width - piece * plan.spare, 1)
             tile = jnp.where(lane >= plan.width, moved, tile)
-        ref[plan.place(base, at)] = tile
+        plan.put(ref, base, at, tile)
 
 
 def store_padding(plan, ref, base):
-    for tile in range(plan.stored, plan.slots * plan.per_slot):
+    rest = (plan.slots - plan.whole * SUB) * plan.per_slot + plan.whole * plan.devices
+    for tile in range(plan.stored, rest):
         ref[plan.place(base, tile)] = jnp.zeros((SUB, LANES), F32)
+
+
+def store_norms(plan, ref, rows):
+    rows = rows.reshape(1, plan.extra * LANES)[:, : plan.half * LANES]
+    for piece in range(plan.devices):
+        ref[piece, :, pl.ds(plan.span, plan.half * LANES)] = rows
 
 
 def load_rows(plan, ref, base, head):
@@ -131,11 +149,11 @@
     for j in range(plan.head_tiles):
         at = head * plan.head_tiles + j
         if at < plan.stored:
-            tiles.append(ref[plan.place(base, at)])
+            tiles.append(plan.get(ref, base, at))
             continue
         tile = None
         for piece in range(plan.pieces):
-            part = ref[plan.place(base, (at - plan.stored) * plan.pieces + piece)]
+            part = plan.get(ref, base, (at - plan.stored) * plan.pieces + piece)
             part = pltpu.roll(part, (LANES - plan.width + piece * plan.spare) % LANES, 1)
             tile = part if tile is None else jnp.where(lane >= piece * plan.spare, part, tile)
         tiles.append(tile)
@@ -191,16 +209,15 @@
     return jnp.maximum(x, 0)
 
 
-def block_state(plan, partner, ids_ref, k_ref, v_ref, out_ref):
-    core = ids_ref[0]
-    if partner:
-        core = 1 - core
+def block_states(plan, k_ref, v_ref, send_ref, own_ref):
+    core = my_core()
     ones = jnp.ones((SUB, plan.length), BF16)
-    out_ref[plan.rows :, :] = jnp.zeros((plan.extra, LANES), F32)
-    for h in range(plan.half):
-        b, v = relu(plan.own(k_ref, core, h)), plan.own(v_ref, core, h)
-        out_ref[h * plan.width : (h + 1) * plan.width, :] = wide(nt(b, v))
-        out_ref[plan.rows + h : plan.rows + h + 1, :] = wide(nt(ones, b))[0:1]
+    for side, out_ref in ((1 - core, send_ref), (core, own_ref)):
+        out_ref[plan.rows :, :] = jnp.zeros((plan.extra, LANES), F32)
+        for h in range(plan.half):
+            b, v = relu(plan.own(k_ref, side, h)), plan.own(v_ref, side, h)
+            out_ref[h * plan.width : (h + 1) * plan.width, :] = wide(nt(b, v))
+            out_ref[plan.rows + h : plan.rows + h + 1, :] = wide(nt(ones, b))[0:1]
 
 
 def chip_state(plan, own_ref, got_ref, out_ref):
@@ -208,17 +225,15 @@
     for h in reversed(range(plan.half)):
         rows = slice(h * plan.width, (h + 1) * plan.width)
         store_rows(plan, out_ref, 0, h, own_ref[rows, :] + got_ref[rows, :], held)
-        row = slice(plan.rows + h, plan.rows + h + 1)
-        norm = jnp.broadcast_to(own_ref[row, :] + got_ref[row, :], (plan.devices, LANES))
-        out_ref[:, 0, plan.row_slot(h)] = norm
     store_padding(plan, out_ref, 0)
+    store_norms(plan, out_ref, own_ref[plan.rows :, :] + got_ref[plan.rows :, :])
 
 
 def pack_tokens(
-    plan, ids_ref, q_ref, k_ref, v_ref, g_ref, q_got_ref, k_got_ref, v_got_ref, g_got_ref,
+    plan, q_ref, k_ref, v_ref, g_ref, q_got_ref, k_got_ref, v_got_ref, g_got_ref,
     a_ref, b_ref, vb_ref, gb_ref, sum_ref, norm_ref,
 ):
-    core = ids_ref[0]
+    core = my_core()
     causal = causal_mask(plan.length)
     ones = jnp.ones((SUB, plan.length), BF16)
     sources = ((q_ref, q_got_ref), (k_ref, k_got_ref), (v_ref, v_got_ref), (g_ref, g_got_ref))
@@ -234,10 +249,10 @@
 
 
 def middle(
-    plan, ids_ref, in_ref, sum_ref, a_ref, g_ref, norm_ref, norm_in_ref,
+    plan, in_ref, sum_ref, a_ref, g_ref, norm_ref, norm_in_ref,
     out_ref, inverse_ref, z_ref,
 ):
-    core, chip = ids_ref[0], ids_ref[1]
+    core, chip = my_core(), my_device() >> 1
     flags = (core.astype(F32), (1 - core).astype(F32))
     width = plan.width
     norms = scan_norms(plan, in_ref, core, chip, False)
@@ -262,9 +277,9 @@
 
 
 def before_states(
-    plan, ids_ref, a_ref, b_ref, v_ref, g_ref, state_in_ref, before_ref, inner_ref
-):
-    core = ids_ref[0]
+    plan, a_ref, b_ref, v_ref, g_ref, state_in_ref, before_ref, inner_ref
+):
+    core = my_core()
     causal = causal_mask(plan.length)
     own_first = core == 0
     late = (core.astype(F32), (1 - core).astype(F32))
@@ -283,10 +298,11 @@
 
 
 def outputs_grad(
-    plan, ids_ref, in_ref, before_ref, a_ref, g_ref, inverse_ref, inner_ref,
+    plan, in_ref, before_ref, a_ref, g_ref, inverse_ref, inner_ref,
     out_ref, product_ref, c_ref, m_ref,
 ):
     scan_rows(plan, in_ref, plan.span, out_ref, True)
+    totals = []
     for h in range(plan.half):
         base = load_rows(plan, in_ref, 0, h)
         total = None
@@ -303,11 +319,13 @@
             m = wide(added(nt(stacked_parts(c), a)))
             m_ref[i, h : h + 1, :] = m
             total = m if total is None else total + m
-        out_ref[:, 0, plan.row_slot(h)] = jnp.broadcast_to(total, (plan.devices, LANES))
+        totals.append(total)
+    totals += [jnp.zeros((1, LANES), F32)] * (plan.extra - plan.half)
+    store_norms(plan, out_ref, jnp.concatenate(totals, axis=0))
 
 
 def query_grads(
-    plan, ids_ref, a_ref, b_ref, v_ref, g_ref, inverse_ref, c_ref, z_ref, product_ref,
+    plan, a_ref, b_ref, v_ref, g_ref, inverse_ref, c_ref, z_ref, product_ref,
     own_ref, send_ref, mixed_ref,
 ):
     causal = causal_mask(plan.length)
@@ -327,9 +345,9 @@
 
 
 def after_states(
-    plan, ids_ref, a_ref, b_ref, g_ref, inverse_ref, mixed_ref, grad_state_ref, *refs
-):
-    core = ids_ref[0]
+    plan, a_ref, b_ref, g_ref, inverse_ref, mixed_ref, grad_state_ref, *refs
+):
+    core = my_core()
     causal = causal_mask(plan.length)
     own_first = core == 0
     early = ((1 - core).astype(F32), core.astype(F32))
@@ -349,10 +367,10 @@
 
 
 def key_value_grads(
-    plan, i, ids_ref, in_ref, after_ref, key_in_ref, value_in_ref, grad_norm_ref, m_ref, b_ref,
+    plan, i, in_ref, after_ref, key_in_ref, value_in_ref, grad_norm_ref, m_ref, b_ref,
     v_ref, key_ref, value_ref,
 ):
-    core, chip = ids_ref[0], ids_ref[1]
+    core, chip = my_core(), my_device() >> 1
     flag = (core if i else 1 - core).astype(F32)
     width = plan.width
     norms = scan_norms(plan, in_ref, core, chip, True)
@@ -378,8 +396,8 @@
         value_ref[rows, :] = value.astype(value_ref.dtype)
 
 
-def assemble(plan, ids_ref, *refs):
-    core = ids_ref[0]
+def assemble(plan, *refs):
+    core = my_core()
     count = len(refs) // 3
     start = pl.multiple_of(core * (plan.shift * plan.width), 16)
     rest = plan.shift * plan.width
@@ -421,7 +439,6 @@
     plan = Plan(devices, length, heads, width)
     half = plan.half
     core = my_core()
-    who = jnp.stack([core, my_device() >> 1]).astype(jnp.int32)
     q, k, v, g = queries.T, key_vectors.T, value_vectors.T, output_grad.T
 
     def bind(body):
@@ -446,56 +463,55 @@
     sent_single = shape((devices, 1, plan.span + half * LANES))
     sent_double = shape((devices, 1, 2 * plan.span))
 
-    (send,) = call(functools.partial(block_state, plan, True), (block,), (who, k, v))
+    send, block_own = call(bind(block_states), (block, block), (k, v))
     block_got = pair_swap(send)
-    (block_own,) = call(functools.partial(block_state, plan, False), (block,), (who, k, v))
     (sent,) = call(bind(chip_state), (sent_single,), (block_own, block_got))
     sent, k, v, q, g = lax.optimization_barrier((sent, k, v, q, g))
     got = exchange(sent)
     a, b, v, g, sums, norm = call(
         bind(pack_tokens),
         (packed, packed, packed, packed, rows, rows),
-        (who, q, k, v, g, *(swap_columns(x) for x in (q, k, v, g))),
+        (q, k, v, g, *(swap_columns(x) for x in (q, k, v, g))),
     )
     sent, inverse, z = call(
         bind(middle),
         (sent_double, rows, rows),
-        (who, got, sums, a, g, norm, norm_in),
+        (got, sums, a, g, norm, norm_in),
     )
     got = exchange(sent)
     before, inner = call(
-        bind(before_states), (states, rows), (who, a, b, v, g, state_in)
+        bind(before_states), (states, rows), (a, b, v, g, state_in)
     )
     sent, product, c, m = call(
         bind(outputs_grad),
         (sent_single, products, rows, rows),
-        (who, got, before, a, g, inverse, inner),
+        (got, before, a, g, inverse, inner),
     )
     got = exchange(sent)
     query, query_send, mixed = call(
-        bind(query_grads), (tokens, tokens, square), (who, a, b, v, g, inverse, c, z, product)
+        bind(query_grads), (tokens, tokens, square), (a, b, v, g, inverse, c, z, product)
     )
     query_got = pair_swap(query_send)
     finals = call(
-        bind(after_states), (after, part, part) * 2, (who, a, b, g, inverse, mixed, grad_state)
+        bind(after_states), (after, part, part) * 2, (a, b, g, inverse, mixed, grad_state)
     )
     whole = shape((heads * width, length), BF16)
-    (query_grad,) = call(bind(assemble), (whole,), (who, query, query_got))
+    (query_grad,) = call(bind(assemble), (whole,), (query, query_got))
     got, query_grad = lax.optimization_barrier((got, query_grad))
     key_send, value_send = call(
         functools.partial(key_value_grads, plan, 1),
         (tokens, tokens),
-        (who, got, *finals[3:], grad_norm, m, b, v),
+        (got, *finals[3:], grad_norm, m, b, v),
     )
     key_got, value_got = pair_swap(key_send), pair_swap(value_send)
     half_tokens = shape((plan.rows, length), BF16)
     key, value = call(
         functools.partial(key_value_grads, plan, 0),
         (half_tokens, half_tokens),
-        (who, got, *finals[:3], grad_norm, m, b, v),
+        (got, *finals[:3], grad_norm, m, b, v),
     )
     key_grad, value_grad = call(
-        bind(assemble), (whole, whole), (who, key, value, key_got, value_got)
+        bind(assemble), (whole, whole), (key, value, key_got, value_got)
     )
     return query_grad.T, key_grad.T, value_grad.T
 

time: 73.4 us -> 70.4 us (0.959)
  Pallas kernels: 18.2 us -> 11 us
  waiting for transfers between devices: 33.7 us -> 36.1 us
  local copies, waits for them, and re-layouts: 4.38 us -> 6.25 us
    pallas_call x13 -> x12, Pallas kernels: 18.2 us -> 11 us  [call(): pl.pallas_call(body, out_shape=outs, in_specs=in_specs, out_specs=[vmem]...]
    unnamed x26, local copies, waits for them, and re-layouts: 4.38 us -> 6.25 us
    ppermute x8, waiting for transfers between devices: 2.91 us -> 4.47 us  [pair_swap(): return lax.ppermute(x, 'seq', [(i, i ^ 1) for i in range(size)])]
    all_to_all x3, waiting for transfers between devices: 30.8 us -> 31.6 us  [exchange(): return lax.all_to_all(x, both, 0, 0, tiled=True)]
  transfers between devices with their start and end apart: 11 -> 11, of which waited for: 9 -> 10; matrix products, arithmetic and copies ran while one was open for 0% -> 0% of each run, Pallas kernels for 14% -> 9%
where the time goes in v4:
time: 70.4 us; the launch traced here: 69.9 us
  waiting for transfers between devices  36.1 us (51%)
  starting transfers between devices  15.7 us (22%)
  Pallas kernels  11 us (16%)
  local copies, waits for them, and re-layouts  6.25 us (9%)
  between operations  0.8 us (1%)
    all_to_all x3, waiting for transfers between devices, exchange(): return lax.all_to_all(x, both, 0, 0, tiled=True)  31.6 us
    all_to_all x3, starting transfers between devices, exchange(): return lax.all_to_all(x, both, 0, 0, tiled=True)  13.2 us
    pallas_call x12, Pallas kernels, call(): pl.pallas_call(body, out_shape=outs, in_specs=in_specs, out_specs=[vmem]...  11 us
    unnamed x26, local copies, waits for them, and re-layouts  6.25 us
    ppermute x8, waiting for transfers between devices, pair_swap(): return lax.ppermute(x, 'seq', [(i, i ^ 1) for i in range(size)])  4.47 us
    ppermute x8, starting transfers between devices, pair_swap(): return lax.ppermute(x, 'seq', [(i, i ^ 1) for i in range(size)])  2.53 us
  transfers between devices with their start and end apart: 11, of which 10 were waited for; matrix products, arithmetic and copies ran while one was open for 0% of the time, Pallas kernels for 9%

profile of v4, /device:TPU:0, one launch (start us, length us, event | category | flops | bytes accessed | tf_op | source)
XLA Modules:
  0.0 69.9 jit_solution(434703618975356119)
XLA Ops:
  0.6 0.0 copy-start
  0.6 1.0 %copy-done = bf16[128,1232]{0,1:T(8,128)(2,1)S(1)} copy-done((bf16[128,1232]{0,1:T(8,128)(2,1)S(1)}, bf16[128,1232]{0,1:T(8,128)(2,1)}, u32[]{:S(2)}) %copy-start) | copy-done | bytes 315416
  1.6 1.0 %copy-done.2 = bf16[128,1232]{0,1:T(8,128)(2,1)S(1)} copy-done((bf16[128,1232]{0,1:T(8,128)(2,1)S(1)}, bf16[128,1232]{0,1:T(8,128)(2,1)}, u32[]{:S(2)}) %copy-start.2) | copy-done | bytes 315416
  2.6 0.5 shard_map.103
  3.1 0.6 collective-permute-start
  3.6 1.3 %collective-permute-done.got_ref = f32[680,128]{1,0:T(8,128)S(1)} collective-permute-done((f32[680,128]{1,0:T(8,128)S(1)}, f32[680,128]{1,0:T(8,128)S(1)}, u32[]{:S(2)}, u32[]{:S(2)}) %collective-permute-start) | collective-permute-done | bytes 348192 | tf_op jit(solution)/shard_map/ppermute | solution.py:108
  4.9 0.9 %shard_map.104 = f32[32,1,3200]{2,1,0:T(1,128)} custom-call(f32[680,128]{1,0:T(8,128)S(1)} %get-tuple-element.42.own_ref, f32[680,128]{1,0:T(8,128)S(1)} %collective-permute-done.got_ref), custom_call_target="tpu_custom_call" | custom-call | flops 10000000 | bytes 1105920 | tf_op jit(solution)/shard_map/pallas_call | solution.py:417
  5.8 7.2 %all-to-all-start = ((f32[32,1,3200]{2,1,0:T(1,128)}), f32[32,1,3200]{2,1,0:T(1,128)S(1)}, u32[]{:S(2)}, u32[]{:S(2)}) async-start(f32[32,1,3200]{2,1,0:T(1,128)} %shard_map.104), calls=%async_computation | async-start | bytes 819200 | tf_op jit(solution)/shard_map/all_to_all | solution.py:448
  13.0 0.0 copy-start.1
  13.1 0.9 %copy-done.1 = bf16[128,1232]{0,1:T(8,128)(2,1)S(1)} copy-done((bf16[128,1232]{0,1:T(8,128)(2,1)S(1)}, bf16[128,1232]{0,1:T(8,128)(2,1)}, u32[]{:S(2)}) %copy-start.1) | copy-done | bytes 315416
  14.0 0.9 %copy-done.3 = bf16[128,1232]{0,1:T(8,128)(2,1)S(1)} copy-done((bf16[128,1232]{0,1:T(8,128)(2,1)S(1)}, bf16[128,1232]{0,1:T(8,128)(2,1)}, u32[]{:S(2)}) %copy-start.3) | copy-done | bytes 315416
  15.0 0.9 %copy-done.5 = bf16[128,1232]{0,1:T(8,128)(2,1)S(1)} copy-done((bf16[128,1232]{0,1:T(8,128)(2,1)S(1)}, bf16[128,1232]{0,1:T(8,128)(2,1)}, u32[]{:S(2)}) %copy-start.5) | copy-done | bytes 315416
  16.0 0.3 collective-permute-start.4
  16.3 0.3 collective-permute-start.3
  16.6 0.3 collective-permute-start.2
  16.8 0.3 collective-permute-start.1
  17.1 0.6 collective-permute-done.4.g_got_ref
  17.7 0.5 collective-permute-done.3.v_got_ref
  18.2 0.5 collective-permute-done.2.k_got_ref
  18.7 0.5 collective-permute-done.1.q_got_ref
  19.2 0.5 shard_map.105
  19.7 6.8 %all-to-all-done.in_ref = f32[32,1,3200]{2,1,0:T(1,128)S(1)} async-done(((f32[32,1,3200]{2,1,0:T(1,128)}), f32[32,1,3200]{2,1,0:T(1,128)S(1)}, u32[]{:S(2)}, u32[]{:S(2)}) %all-to-all-start) | async-done | bytes 409632 | tf_op jit(solution)/shard_map/all_to_all | solution.py:448
  26.6 0.0 copy-done.12
  26.6 1.3 %shard_map.106 = (f32[32,1,4864]{2,1,0:T(1,128)}, f32[2,8,128]{2,1,0:T(8,128)S(1)}, f32[2,8,128]{2,1,0:T(8,128)S(1)}) custom-call(f32[32,1,3200]{2,1,0:T(1,128)S(1)} %all-to-all-done.in_ref, f32[2,8,128]{2,1,0:T(8,128)S(1)} %get-tuple-element.49.sum_ref, bf16[2,6,112,128]{3,2,1,0:T(8,128)(2,1)S(1)} %get-tuple-element.50.a_ref, ...), custom_call_target="tpu_custom_call" | custom-call | flops 10000000 | bytes 1758016 | tf_op jit(solution)/shard_map/pallas_call | solution.py:417
  27.9 2.7 %all-to-all-start.1 = ((f32[32,1,4864]{2,1,0:T(1,128)}), f32[32,1,4864]{2,1,0:T(1,128)S(1)}, u32[]{:S(2)}, u32[]{:S(2)}) async-start(f32[32,1,4864]{2,1,0:T(1,128)} %get-tuple-element.53), calls=%async_computation.1 | async-start | bytes 1245184 | tf_op jit(solution)/shard_map/all_to_all | solution.py:448
  30.7 1.3 %shard_map.107 = (f32[2,6,112,112]{3,2,1,0:T(8,128)S(1)}, f32[2,8,128]{2,1,0:T(8,128)S(1)}) custom-call(bf16[2,6,112,128]{3,2,1,0:T(8,128)(2,1)S(1)} %get-tuple-element.50.a_ref, bf16[2,6,112,128]{3,2,1,0:T(8,128)(2,1)S(1)} %get-tuple-element.54.b_ref, bf16[2,6,112,128]{3,2,1,0:T(8,128)(2,1)S(1)} %get-tuple-element.55.v_ref, ...), custom_call_target="tpu_custom_call" | custom-call | flops 10000000 | bytes 2538496 | tf_op jit(solution)/shard_map/pallas_call | solution.py:417
  32.0 16.1 %all-to-all-done.1.in_ref = f32[32,1,4864]{2,1,0:T(1,128)S(1)} async-done(((f32[32,1,4864]{2,1,0:T(1,128)}), f32[32,1,4864]{2,1,0:T(1,128)S(1)}, u32[]{:S(2)}, u32[]{:S(2)}) %all-to-all-start.1) | async-done | bytes 622624 | tf_op jit(solution)/shard_map/all_to_all | solution.py:448
  48.1 0.7 shard_map.108
  48.7 0.0 copy-start.8
  48.7 0.7 %copy-done.8 = f32[32,1,3200]{2,1,0:T(1,128)} copy-done((f32[32,1,3200]{2,1,0:T(1,128)}, f32[32,1,3200]{2,1,0:T(1,128)S(1)}, u32[]{:S(2)}) %copy-start.8) | copy-done | bytes 409624
  49.5 3.2 %all-to-all-start.2 = ((f32[32,1,3200]{2,1,0:T(1,128)}), f32[32,1,3200]{2,1,0:T(1,128)S(1)}, u32[]{:S(2)}, u32[]{:S(2)}) async-start(f32[32,1,3200]{2,1,0:T(1,128)} %copy-done.8), calls=%async_computation.2 | async-start | bytes 819200 | tf_op jit(solution)/shard_map/all_to_all | solution.py:448
  52.7 0.0 copy-start.7
  52.7 1.4 %shard_map.109 = (f32[672,128]{1,0:T(8,128)S(1)}, f32[672,128]{1,0:T(8,128)S(1)}, bf16[2,6,128,128]{3,2,1,0:T(8,128)(2,1)S(1)}) custom-call(bf16[2,6,112,128]{3,2,1,0:T(8,128)(2,1)S(1)} %get-tuple-element.50.a_ref, bf16[2,6,112,128]{3,2,1,0:T(8,128)(2,1)S(1)} %get-tuple-element.54.b_ref, bf16[2,6,112,128]{3,2,1,0:T(8,128)(2,1)S(1)} %get-tuple-element.55.v_ref, ...), custom_call_target="tpu_custom_call" | custom-call | flops 10000000 | bytes 3170304 | tf_op jit(solution)/shard_map/pallas_call | solution.py:417
  54.1 0.3 collective-permute-start.5
  54.4 0.0 copy-done.7
  54.4 1.6 %shard_map.111 = (f32[6,112,112]{2,1,0:T(8,128)S(1)}, f32[6,112,128]{2,1,0:T(8,128)S(1)}, f32[6,112,128]{2,1,0:T(8,128)S(1)}, f32[6,112,112]{2,1,0:T(8,128)S(1)}...) custom-call(bf16[2,6,112,128]{3,2,1,0:T(8,128)(2,1)S(1)} %get-tuple-element.50.a_ref, ...), custom_call_target="tpu_custom_call" | custom-call | flops 10000000 | bytes 3963904 | tf_op jit(solution)/shard_map/pallas_call | solution.py:417
  56.0 0.0 copy-start.9
  56.0 0.7 %copy-done.9 = f32[6,112,128]{2,1,0:T(8,128)} copy-done((f32[6,112,128]{2,1,0:T(8,128)}, f32[6,112,128]{2,1,0:T(8,128)S(1)}, u32[]{:S(2)}) %copy-start.9) | copy-done | bytes 344088
  56.8 0.0 collective-permute-done.5.refs_1_
  56.8 0.8 %shard_map.110 = bf16[1232,128]{1,0:T(8,128)(2,1)} custom-call(f32[672,128]{1,0:T(8,128)S(1)} %get-tuple-element.63.refs_0_, f32[672,128]{1,0:T(8,128)S(1)} %collective-permute-done.5.refs_1_), custom_call_target="tpu_custom_call" | custom-call | flops 10000000 | bytes 1003520 | tf_op jit(solution)/shard_map/pallas_call | solution.py:417
  57.5 8.7 %all-to-all-done.2.in_ref = f32[32,1,3200]{2,1,0:T(1,128)S(1)} async-done(((f32[32,1,3200]{2,1,0:T(1,128)}), f32[32,1,3200]{2,1,0:T(1,128)S(1)}, u32[]{:S(2)}, u32[]{:S(2)}) %all-to-all-start.2) | async-done | bytes 409632 | tf_op jit(solution)/shard_map/all_to_all | solution.py:448
  66.3 0.5 shard_map.113
  66.8 0.1 collective-permute-start.6
  66.9 0.5 collective-permute-start.7
  67.4 0.6 shard_map.112
  67.9 0.6 collective-permute-done.6.refs_2_
  68.5 0.5 collective-permute-done.7.refs_3_
  69.0 0.9 %shard_map.114 = (bf16[1232,128]{1,0:T(8,128)(2,1)}, bf16[1232,128]{1,0:T(8,128)(2,1)}) custom-call(bf16[672,128]{1,0:T(8,128)(2,1)S(1)} %get-tuple-element.72.refs_0_, bf16[672,128]{1,0:T(8,128)(2,1)S(1)} %get-tuple-element.73.refs_1_, f32[672,128]{1,0:T(8,128)S(1)} %collective-permute-done.6.refs_2_, f32[672,128]{1,0:T(8,128)S(1)} %collective-permute-done.7.refs_3_), custom_call_target="tpu_custom_call" | custom-call | flops 10000000 | bytes 1662976 | tf_op jit(solution)/shard_map/pallas_call | solution.py:417
  (16 shorter events, 0.1 us)
Async XLA Ops:
  0.6 1.0 %copy-start = (bf16[128,1232]{0,1:T(8,128)(2,1)S(1)}, bf16[128,1232]{0,1:T(8,128)(2,1)}, u32[]{:S(2)}) copy-start(bf16[128,1232]{0,1:T(8,128)(2,1)} %param.9) | copy-start | bytes 946180
  1.6 1.0 %copy-start.2 = (bf16[128,1232]{0,1:T(8,128)(2,1)S(1)}, bf16[128,1232]{0,1:T(8,128)(2,1)}, u32[]{:S(2)}) copy-start(bf16[128,1232]{0,1:T(8,128)(2,1)} %param.10) | copy-start | bytes 946180
  3.1 1.8 %collective-permute-start = (f32[680,128]{1,0:T(8,128)S(1)}, f32[680,128]{1,0:T(8,128)S(1)}, u32[]{:S(2)}, u32[]{:S(2)}) collective-permute-start(f32[680,128]{1,0:T(8,128)S(1)} %get-tuple-element.43), channel_id=1, source_target_pairs={{0,1},{1,0},{2,3},{3,2},{4,5},{5,4},{6,7},{7,6},{8,9},{9,8},{10,11... | collective-permute-start | bytes 1044488 | tf_op jit(solution)/shard_map/ppermute | solution.py:108
  5.8 7.2 %copy-start.4 = (bf16[128,1232]{0,1:T(8,128)(2,1)S(1)}, bf16[128,1232]{0,1:T(8,128)(2,1)}, u32[]{:S(2)}) copy-start(bf16[128,1232]{0,1:T(8,128)(2,1)} %param.8) | copy-start | bytes 946180
  5.8 20.8 %all-to-all-start = ((f32[32,1,3200]{2,1,0:T(1,128)}), f32[32,1,3200]{2,1,0:T(1,128)S(1)}, u32[]{:S(2)}, u32[]{:S(2)}) async-start(f32[32,1,3200]{2,1,0:T(1,128)} %shard_map.104), calls=%async_computation | async-start | bytes 819200 | tf_op jit(solution)/shard_map/all_to_all | solution.py:448
  13.0 1.0 %copy-start.1 = (bf16[128,1232]{0,1:T(8,128)(2,1)S(1)}, bf16[128,1232]{0,1:T(8,128)(2,1)}, u32[]{:S(2)}) copy-start(bf16[128,1232]{0,1:T(8,128)(2,1)} %param.9) | copy-start | bytes 946180
  14.0 1.0 %copy-start.3 = (bf16[128,1232]{0,1:T(8,128)(2,1)S(1)}, bf16[128,1232]{0,1:T(8,128)(2,1)}, u32[]{:S(2)}) copy-start(bf16[128,1232]{0,1:T(8,128)(2,1)} %param.10) | copy-start | bytes 946180
  15.0 1.0 %copy-start.5 = (bf16[128,1232]{0,1:T(8,128)(2,1)S(1)}, bf16[128,1232]{0,1:T(8,128)(2,1)}, u32[]{:S(2)}) copy-start(bf16[128,1232]{0,1:T(8,128)(2,1)} %param.11) | copy-start | bytes 946180
  16.0 1.7 %collective-permute-start.4 = (f32[672,128]{1,0:T(8,128)S(1)}, f32[672,128]{1,0:T(8,128)S(1)}, u32[]{:S(2)}, u32[]{:S(2)}) collective-permute-start(f32[672,128]{1,0:T(8,128)S(1)} %dynamic-slice_convert_fusion), channel_id=1, source_target_pairs={{0,1},{1,0},{2,3},{3,2},{4,5},{5,4},{6,7},{7,6},{8,9},{9,8},{10,11... | collective-permute-start | bytes 1032200 | tf_op jit(solution)/shard_map/ppermute | solution.py:108
  16.3 1.9 %collective-permute-start.3 = (f32[672,128]{1,0:T(8,128)S(1)}, f32[672,128]{1,0:T(8,128)S(1)}, u32[]{:S(2)}, u32[]{:S(2)}) collective-permute-start(f32[672,128]{1,0:T(8,128)S(1)} %dynamic-slice_convert_fusion.1), channel_id=1, source_target_pairs={{0,1},{1,0},{2,3},{3,2},{4,5},{5,4},{6,7},{7,6},{8,9},{9,8},{10,11... | collective-permute-start | bytes 1032200 | tf_op jit(solution)/shard_map/ppermute | solution.py:108
  16.6 2.1 %collective-permute-start.2 = (f32[672,128]{1,0:T(8,128)S(1)}, f32[672,128]{1,0:T(8,128)S(1)}, u32[]{:S(2)}, u32[]{:S(2)}) collective-permute-start(f32[672,128]{1,0:T(8,128)S(1)} %dynamic-slice_convert_fusion.2), channel_id=1, source_target_pairs={{0,1},{1,0},{2,3},{3,2},{4,5},{5,4},{6,7},{7,6},{8,9},{9,8},{10,11... | collective-permute-start | bytes 1032200 | tf_op jit(solution)/shard_map/ppermute | solution.py:108
  16.8 2.4 %collective-permute-start.1 = (f32[672,128]{1,0:T(8,128)S(1)}, f32[672,128]{1,0:T(8,128)S(1)}, u32[]{:S(2)}, u32[]{:S(2)}) collective-permute-start(f32[672,128]{1,0:T(8,128)S(1)} %dynamic-slice_convert_fusion.3), channel_id=1, source_target_pairs={{0,1},{1,0},{2,3},{3,2},{4,5},{5,4},{6,7},{7,6},{8,9},{9,8},{10,11... | collective-permute-start | bytes 1032200 | tf_op jit(solution)/shard_map/ppermute | solution.py:108
  19.2 7.4 %copy-start.12 = (f32[11,112]{1,0:T(8,128)S(1)}, f32[11,112]{1,0:T(8,128)}, u32[]{:S(2)}) copy-start(f32[11,112]{1,0:T(8,128)} %norm_in_ref.1) | copy-start | bytes 14788
  27.9 2.8 %copy-start.6 = (f32[11,112,112]{2,1,0:T(8,128)S(1)}, f32[11,112,112]{2,1,0:T(8,128)}, u32[]{:S(2)}) copy-start(f32[11,112,112]{2,1,0:T(8,128)} %state_in_ref.1) | copy-start | bytes 1655812
  27.9 20.1 %all-to-all-start.1 = ((f32[32,1,4864]{2,1,0:T(1,128)}), f32[32,1,4864]{2,1,0:T(1,128)S(1)}, u32[]{:S(2)}, u32[]{:S(2)}) async-start(f32[32,1,4864]{2,1,0:T(1,128)} %get-tuple-element.53), calls=%async_computation.1 | async-start | bytes 1245184 | tf_op jit(solution)/shard_map/all_to_all | solution.py:448
  48.7 0.8 %copy-start.8 = (f32[32,1,3200]{2,1,0:T(1,128)}, f32[32,1,3200]{2,1,0:T(1,128)S(1)}, u32[]{:S(2)}) copy-start(f32[32,1,3200]{2,1,0:T(1,128)S(1)} %get-tuple-element.59) | copy-start | bytes 1228804
  49.5 16.8 %all-to-all-start.2 = ((f32[32,1,3200]{2,1,0:T(1,128)}), f32[32,1,3200]{2,1,0:T(1,128)S(1)}, u32[]{:S(2)}, u32[]{:S(2)}) async-start(f32[32,1,3200]{2,1,0:T(1,128)} %copy-done.8), calls=%async_computation.2 | async-start | bytes 819200 | tf_op jit(solution)/shard_map/all_to_all | solution.py:448
  52.7 1.7 %copy-start.7 = (f32[11,112,112]{2,1,0:T(8,128)S(1)}, f32[11,112,112]{2,1,0:T(8,128)}, u32[]{:S(2)}) copy-start(f32[11,112,112]{2,1,0:T(8,128)} %grad_state_ref.1) | copy-start | bytes 1655812
  54.1 2.7 %collective-permute-start.5 = (f32[672,128]{1,0:T(8,128)S(1)}, f32[672,128]{1,0:T(8,128)S(1)}, u32[]{:S(2)}, u32[]{:S(2)}) collective-permute-start(f32[672,128]{1,0:T(8,128)S(1)} %get-tuple-element.64), channel_id=1, source_target_pairs={{0,1},{1,0},{2,3},{3,2},{4,5},{5,4},{6,7},{7,6},{8,9},{9,8},{10,11... | collective-permute-start | bytes 1032200 | tf_op jit(solution)/shard_map/ppermute | solution.py:108
  56.0 0.8 %copy-start.9 = (f32[6,112,128]{2,1,0:T(8,128)}, f32[6,112,128]{2,1,0:T(8,128)S(1)}, u32[]{:S(2)}) copy-start(f32[6,112,128]{2,1,0:T(8,128)S(1)} %get-tuple-element.76.value_in_ref) | copy-start | bytes 1032196
  56.8 9.5 %copy-start.10 = (f32[6,112,128]{2,1,0:T(8,128)S(1)}, f32[6,112,128]{2,1,0:T(8,128)}, u32[]{:S(2)}) copy-start(f32[6,112,128]{2,1,0:T(8,128)} %copy-done.9) | copy-start | bytes 1032196
  56.8 9.5 %copy-start.11 = (f32[11,112]{1,0:T(8,128)S(1)}, f32[11,112]{1,0:T(8,128)}, u32[]{:S(2)}) copy-start(f32[11,112]{1,0:T(8,128)} %grad_norm_ref.3) | copy-start | bytes 14788
  66.8 1.7 %collective-permute-start.6 = (f32[672,128]{1,0:T(8,128)S(1)}, f32[672,128]{1,0:T(8,128)S(1)}, u32[]{:S(2)}, u32[]{:S(2)}) collective-permute-start(f32[672,128]{1,0:T(8,128)S(1)} %get-tuple-element.77), channel_id=1, source_target_pairs={{0,1},{1,0},{2,3},{3,2},{4,5},{5,4},{6,7},{7,6},{8,9},{9,8},{10,11... | collective-permute-start | bytes 1032200 | tf_op jit(solution)/shard_map/ppermute | solution.py:108
  66.9 2.1 %collective-permute-start.7 = (f32[672,128]{1,0:T(8,128)S(1)}, f32[672,128]{1,0:T(8,128)S(1)}, u32[]{:S(2)}, u32[]{:S(2)}) collective-permute-start(f32[672,128]{1,0:T(8,128)S(1)} %get-tuple-element.78), channel_id=1, source_target_pairs={{0,1},{1,0},{2,3},{3,2},{4,5},{5,4},{6,7},{7,6},{8,9},{9,8},{10,11... | collective-permute-start | bytes 1032200 | tf_op jit(solution)/shard_map/ppermute | solution.py:108

commit v5 on v4

--- a/solution.py
+++ b/solution.py
@@ -326,7 +326,7 @@
 
 def query_grads(
     plan, a_ref, b_ref, v_ref, g_ref, inverse_ref, c_ref, z_ref, product_ref,
-    own_ref, send_ref, mixed_ref,
+    own_ref, send_ref, mixed_ref, a_out_ref, u_out_ref,
 ):
     causal = causal_mask(plan.length)
     width = plan.width
@@ -338,41 +338,37 @@
             u = (g_ref[i, h].astype(F32) * inverse).astype(BF16)
             mixed = jnp.where(causal, tn(v_ref[i, h], u) + c, 0.0).astype(BF16)
             mixed_ref[i, h] = mixed
+            a_out_ref[i, h] = a_ref[i, h]
+            u_out_ref[i, h] = u
             grad = product_ref[i, h] * inverse + columns[:width, h : h + 1] * c
             grad = jnp.where(a_ref[i, h].astype(F32) > 0, grad + nn(b_ref[i, h], mixed), 0.0)
             target = send_ref if i else own_ref
             target[rows, :] = grad
 
 
-def after_states(
-    plan, a_ref, b_ref, g_ref, inverse_ref, mixed_ref, grad_state_ref, *refs
-):
+def after_states(plan, a_ref, b_ref, u_ref, mixed_ref, grad_state_ref, *refs):
     core = my_core()
     causal = causal_mask(plan.length)
     own_first = core == 0
     early = ((1 - core).astype(F32), core.astype(F32))
     for h in range(plan.half):
-        us = []
-        for i in range(2):
-            u = (g_ref[i, h].astype(F32) * inverse_ref[i, h : h + 1, :]).astype(BF16)
-            us.append(u)
+        for i in range(2):
             low = scores_of(a_ref[i, h], b_ref[i, h], causal).astype(BF16)
-            refs[3 * i + 1][h] = nt(a_ref[i, h], mixed_ref[i, h])
-            refs[3 * i + 2][h] = nt(u, low)
+            key, value = nt(a_ref[i, h], mixed_ref[i, h]), nt(u_ref[i, h], low)
+            key = jnp.where(b_ref[i, h].astype(F32) > 0, key, 0.0)
+            rows = slice(h * plan.width, (h + 1) * plan.width)
+            refs[3 * i + 1][rows, :] = key
+            refs[3 * i + 2][rows, :] = value
         a = jnp.where(own_first, a_ref[1, h].astype(F32), a_ref[0, h].astype(F32)).astype(BF16)
-        u = jnp.where(own_first, us[1].astype(F32), us[0].astype(F32)).astype(BF16)
+        u = jnp.where(own_first, u_ref[1, h].astype(F32), u_ref[0, h].astype(F32)).astype(BF16)
         second = nt(a, u)
         for i in range(2):
             refs[3 * i][h] = grad_state_ref[core * plan.shift + h] + early[i] * second
 
 
-def key_value_grads(
-    plan, i, in_ref, after_ref, key_in_ref, value_in_ref, grad_norm_ref, m_ref, b_ref,
-    v_ref, key_ref, value_ref,
-):
+def suffix_norms(plan, in_ref, grad_norm_ref, m_ref, i):
     core, chip = my_core(), my_device() >> 1
     flag = (core if i else 1 - core).astype(F32)
-    width = plan.width
     norms = scan_norms(plan, in_ref, core, chip, True)
     zeros = plan.extra - plan.half
     norms = jnp.concatenate(
@@ -381,32 +377,73 @@
     )
     own_rows = [
         grad_norm_ref[pl.ds(core * plan.shift + h, 1), :] for h in range(plan.half)
-    ] + [jnp.zeros((zeros, width), F32)] * (zeros > 0)
-    norms = norms + wide(jnp.concatenate(own_rows, axis=0))
-    columns = (norms + flag * m_ref[1 - i]).T
+    ] + [jnp.zeros((zeros, plan.width), F32)] * (zeros > 0)
+    return norms + wide(jnp.concatenate(own_rows, axis=0)) + flag * m_ref[1 - i]
+
+
+def key_value(state, column, b, v):
+    width = state.shape[0]
+    high, low = parts(state)
+    both = nn(jnp.concatenate([high, low], axis=0), v)
+    key = both[:width] + both[width:] + column
+    return jnp.where(b.astype(F32) > 0, key, 0.0), tn(high, b) + tn(low, b)
+
+
+def other_suffix(plan, in_ref, after_ref, grad_norm_ref, m_ref, out_ref):
+    out_ref[plan.rows :, :] = suffix_norms(plan, in_ref, grad_norm_ref, m_ref, 1)
     for h in range(plan.half):
-        rows = slice(h * width, (h + 1) * width)
-        high, low = parts(load_rows(plan, in_ref, 0, h) + after_ref[h])
-        b, v = b_ref[i, h], v_ref[i, h]
-        both = nn(jnp.concatenate([high, low], axis=0), v)
-        key = both[:width] + both[width:] + columns[:width, h : h + 1] + key_in_ref[h]
-        key = jnp.where(b.astype(F32) > 0, key, 0.0)
-        value = tn(high, b) + tn(low, b) + value_in_ref[h]
-        key_ref[rows, :] = key.astype(key_ref.dtype)
-        value_ref[rows, :] = value.astype(value_ref.dtype)
-
-
-def assemble(plan, *refs):
-    core = my_core()
-    count = len(refs) // 3
+        rows = slice(h * plan.width, (h + 1) * plan.width)
+        out_ref[rows, :] = wide(load_rows(plan, in_ref, 0, h) + after_ref[h])
+
+
+def own_grads(
+    plan, in_ref, after_ref, grad_norm_ref, m_ref, b_ref, v_ref, key_in_ref, value_in_ref,
+    key_ref, value_ref,
+):
+    columns = suffix_norms(plan, in_ref, grad_norm_ref, m_ref, 0).T
+    for h in range(plan.half):
+        rows = slice(h * plan.width, (h + 1) * plan.width)
+        state = load_rows(plan, in_ref, 0, h) + after_ref[h]
+        key, value = key_value(state, columns[: plan.width, h : h + 1], b_ref[0, h], v_ref[0, h])
+        key_ref[rows, :] = (key + key_in_ref[rows, :]).astype(BF16)
+        value_ref[rows, :] = (value + value_in_ref[rows, :]).astype(BF16)
+
+
+def rest_grads(
+    plan, got_ref, k_ref, v_ref, key_in_ref, value_in_ref, own_key_ref, own_value_ref,
+    key_ref, value_ref,
+):
+    core = my_core()
+    width, count = plan.width, plan.shift
+    own = pl.multiple_of(core * (count * width), 16)
+    key_ref[pl.ds(own, plan.rows), :] = own_key_ref[...]
+    value_ref[pl.ds(own, plan.rows), :] = own_value_ref[...]
+    skip = (1 - core) * (plan.half - count)
+    norms = got_ref[pl.ds(plan.rows + skip, count), :]
+    columns = jnp.concatenate([norms, jnp.zeros((plan.extra - count, LANES), F32)], axis=0).T
+    for t in range(count):
+        source = pl.ds(pl.multiple_of((skip + t) * width, 16), width)
+        rows = pl.ds(pl.multiple_of((1 - core) * plan.rows + t * width, 16), width)
+        b, v = relu(k_ref[rows, :]), v_ref[rows, :]
+        key, value = key_value(got_ref[source, :][:, :width], columns[:width, t : t + 1], b, v)
+        key_ref[rows, :] = (key + key_in_ref[source, :]).astype(BF16)
+        value_ref[rows, :] = (value + value_in_ref[source, :]).astype(BF16)
+
+
+def assemble(plan, count, *refs):
+    core = my_core()
     start = pl.multiple_of(core * (plan.shift * plan.width), 16)
     rest = plan.shift * plan.width
     skip = plan.rows - rest
     other = pl.multiple_of((1 - core) * plan.rows, 16)
     source = pl.multiple_of((1 - core) * skip, 16)
-    for own_ref, got_ref, out_ref in zip(refs[:count], refs[count : 2 * count], refs[2 * count :]):
+    for n in range(count):
+        own_ref, out_ref = refs[n], refs[len(refs) - count + n]
         out_ref[pl.ds(start, plan.rows), :] = own_ref[...].astype(BF16)
-        out_ref[pl.ds(other, rest), :] = got_ref[pl.ds(source, rest), :].astype(BF16)
+        got = refs[count + n][pl.ds(source, rest), :]
+        for ref in refs[2 * count + n : len(refs) - count : count]:
+            got = got + ref[pl.ds(source, rest), :]
+        out_ref[pl.ds(other, rest), :] = got.astype(BF16)
 
 
 def call(body, outs, args, room=FREE, flops=10_000_000, scratch=()):
@@ -439,6 +476,7 @@
     plan = Plan(devices, length, heads, width)
     half = plan.half
     core = my_core()
+    key_rows, value_rows = key_vectors.T, value_vectors.T
     q, k, v, g = queries.T, key_vectors.T, value_vectors.T, output_grad.T
 
     def bind(body):
@@ -458,7 +496,6 @@
     states = shape((2, half, width, width))
     rows = shape((2, plan.extra, LANES))
     after = shape((half, width, width))
-    part = shape((half, width, length))
     block = shape((plan.rows + plan.extra, LANES))
     sent_single = shape((devices, 1, plan.span + half * LANES))
     sent_double = shape((devices, 1, 2 * plan.span))
@@ -473,45 +510,41 @@
         (packed, packed, packed, packed, rows, rows),
         (q, k, v, g, *(swap_columns(x) for x in (q, k, v, g))),
     )
+    before, inner = call(bind(before_states), (states, rows), (a, b, v, g, state_in))
+    got, before, inner = lax.optimization_barrier((got, before, inner))
     sent, inverse, z = call(
         bind(middle),
         (sent_double, rows, rows),
         (got, sums, a, g, norm, norm_in),
     )
     got = exchange(sent)
-    before, inner = call(
-        bind(before_states), (states, rows), (a, b, v, g, state_in)
-    )
     sent, product, c, m = call(
         bind(outputs_grad),
         (sent_single, products, rows, rows),
         (got, before, a, g, inverse, inner),
     )
     got = exchange(sent)
-    query, query_send, mixed = call(
-        bind(query_grads), (tokens, tokens, square), (a, b, v, g, inverse, c, z, product)
+    query, query_send, mixed, a, u = call(
+        bind(query_grads),
+        (tokens, tokens, square, packed, packed),
+        (a, b, v, g, inverse, c, z, product),
     )
     query_got = pair_swap(query_send)
     finals = call(
-        bind(after_states), (after, part, part) * 2, (a, b, g, inverse, mixed, grad_state)
-    )
+        bind(after_states), (after, tokens, tokens) * 2, (a, b, u, mixed, grad_state)
+    )
+    inner_got = [pair_swap(x) for x in finals[4:]]
     whole = shape((heads * width, length), BF16)
-    (query_grad,) = call(bind(assemble), (whole,), (query, query_got))
-    got, query_grad = lax.optimization_barrier((got, query_grad))
-    key_send, value_send = call(
-        functools.partial(key_value_grads, plan, 1),
-        (tokens, tokens),
-        (got, *finals[3:], grad_norm, m, b, v),
-    )
-    key_got, value_got = pair_swap(key_send), pair_swap(value_send)
-    half_tokens = shape((plan.rows, length), BF16)
+    (query_grad,) = call(functools.partial(assemble, plan, 1), (whole,), (query, query_got))
+    got, query_grad, inner_got = lax.optimization_barrier((got, query_grad, inner_got))
+    (send,) = call(bind(other_suffix), (block,), (got, finals[3], grad_norm, m))
+    rest_got = pair_swap(send)
+    own_tokens = shape((plan.rows, length), BF16)
     key, value = call(
-        functools.partial(key_value_grads, plan, 0),
-        (half_tokens, half_tokens),
-        (got, *finals[:3], grad_norm, m, b, v),
+        bind(own_grads), (own_tokens, own_tokens), (got, finals[0], grad_norm, m, b, v, *finals[1:3])
     )
     key_grad, value_grad = call(
-        bind(assemble), (whole, whole), (key, value, key_got, value_got)
+        bind(rest_grads), (whole, whole), (rest_got, key_rows, value_rows, *inner_got, key, value)
     )
     return query_grad.T, key_grad.T, value_grad.T
 

time: 70.4 us -> 68.7 us (0.976)
  blocking collectives: 0 us -> 19.8 us
  waiting for transfers between devices: 36.1 us -> 17.2 us
  starting transfers between devices: 15.7 us -> 13.1 us
    all_to_all x0 -> x1, blocking collectives: none -> 19.8 us  [exchange(): return lax.all_to_all(x, both, 0, 0, tiled=True)]
    all_to_all x3 -> x2, waiting for transfers between devices: 31.6 us -> 11.9 us  [exchange(): return lax.all_to_all(x, both, 0, 0, tiled=True)]
    all_to_all x3 -> x2, starting transfers between devices: 13.2 us -> 10.5 us  [exchange(): return lax.all_to_all(x, both, 0, 0, tiled=True)]
    ppermute x8 -> x9, waiting for transfers between devices: 4.47 us -> 5.33 us  [pair_swap(): return lax.ppermute(x, 'seq', [(i, i ^ 1) for i in range(size)])]
    unnamed x26 -> x28, local copies, waits for them, and re-layouts: 6.25 us -> 6.37 us
    ppermute x8 -> x9, starting transfers between devices: 2.53 us -> 2.61 us  [pair_swap(): return lax.ppermute(x, 'seq', [(i, i ^ 1) for i in range(size)])]
where the time goes in v5:
time: 68.7 us; the launch traced here: 68.3 us
  blocking collectives  19.8 us (29%)
  waiting for transfers between devices  17.2 us (25%)
  starting transfers between devices  13.1 us (19%)
  Pallas kernels  10.9 us (16%)
  local copies, waits for them, and re-layouts  6.37 us (9%)
  between operations  0.8 us (1%)
    all_to_all x1, blocking collectives, exchange(): return lax.all_to_all(x, both, 0, 0, tiled=True)  19.8 us
    all_to_all x2, waiting for transfers between devices, exchange(): return lax.all_to_all(x, both, 0, 0, tiled=True)  11.9 us
    pallas_call x12, Pallas kernels, call(): pl.pallas_call(body, out_shape=outs, in_specs=in_specs, out_specs=[vmem]...  10.9 us
    all_to_all x2, starting transfers between devices, exchange(): return lax.all_to_all(x, both, 0, 0, tiled=True)  10.5 us
    unnamed x28, local copies, waits for them, and re-layouts  6.37 us
    ppermute x9, waiting for transfers between devices, pair_swap(): return lax.ppermute(x, 'seq', [(i, i ^ 1) for i in range(size)])  5.33 us
    ppermute x9, starting transfers between devices, pair_swap(): return lax.ppermute(x, 'seq', [(i, i ^ 1) for i in range(size)])  2.61 us
  transfers between devices with their start and end apart: 11, of which 10 were waited for; matrix products, arithmetic and copies ran while one was open for 0% of the time, Pallas kernels for 9%

profile of v5, /device:TPU:0, one launch (start us, length us, event | category | flops | bytes accessed | tf_op | source)
XLA Modules:
  0.0 68.3 jit_solution(13301000211340902001)
XLA Ops:
  0.6 0.0 copy-start
  0.6 1.0 %copy-done = bf16[128,1232]{0,1:T(8,128)(2,1)S(1)} copy-done((bf16[128,1232]{0,1:T(8,128)(2,1)S(1)}, bf16[128,1232]{0,1:T(8,128)(2,1)}, u32[]{:S(2)}) %copy-start) | copy-done | bytes 315416
  1.6 1.0 %copy-done.2 = bf16[128,1232]{0,1:T(8,128)(2,1)S(1)} copy-done((bf16[128,1232]{0,1:T(8,128)(2,1)S(1)}, bf16[128,1232]{0,1:T(8,128)(2,1)}, u32[]{:S(2)}) %copy-start.2) | copy-done | bytes 315416
  2.6 0.5 shard_map.103
  3.1 0.6 collective-permute-start
  3.6 1.3 %collective-permute-done.got_ref = f32[680,128]{1,0:T(8,128)S(1)} collective-permute-done((f32[680,128]{1,0:T(8,128)S(1)}, f32[680,128]{1,0:T(8,128)S(1)}, u32[]{:S(2)}, u32[]{:S(2)}) %collective-permute-start) | collective-permute-done | bytes 348192 | tf_op jit(solution)/shard_map/ppermute | solution.py:108
  4.9 0.9 %shard_map.104 = f32[32,1,3200]{2,1,0:T(1,128)} custom-call(f32[680,128]{1,0:T(8,128)S(1)} %get-tuple-element.47.own_ref, f32[680,128]{1,0:T(8,128)S(1)} %collective-permute-done.got_ref), custom_call_target="tpu_custom_call" | custom-call | flops 10000000 | bytes 1105920 | tf_op jit(solution)/shard_map/pallas_call | solution.py:454
  5.8 7.2 %all-to-all-start = ((f32[32,1,3200]{2,1,0:T(1,128)}), f32[32,1,3200]{2,1,0:T(1,128)S(1)}, u32[]{:S(2)}, u32[]{:S(2)}) async-start(f32[32,1,3200]{2,1,0:T(1,128)} %shard_map.104), calls=%async_computation | async-start | bytes 819200 | tf_op jit(solution)/shard_map/all_to_all | solution.py:486
  13.1 0.0 copy-start.1
  13.1 0.9 %copy-done.1 = bf16[128,1232]{0,1:T(8,128)(2,1)S(1)} copy-done((bf16[128,1232]{0,1:T(8,128)(2,1)S(1)}, bf16[128,1232]{0,1:T(8,128)(2,1)}, u32[]{:S(2)}) %copy-start.1) | copy-done | bytes 315416
  14.1 0.9 %copy-done.3 = bf16[128,1232]{0,1:T(8,128)(2,1)S(1)} copy-done((bf16[128,1232]{0,1:T(8,128)(2,1)S(1)}, bf16[128,1232]{0,1:T(8,128)(2,1)}, u32[]{:S(2)}) %copy-start.3) | copy-done | bytes 315416
  15.0 0.9 %copy-done.5 = bf16[128,1232]{0,1:T(8,128)(2,1)S(1)} copy-done((bf16[128,1232]{0,1:T(8,128)(2,1)S(1)}, bf16[128,1232]{0,1:T(8,128)(2,1)}, u32[]{:S(2)}) %copy-start.5) | copy-done | bytes 315416
  16.0 0.0 copy-start.8
  16.0 0.3 collective-permute-start.4
  16.3 0.3 collective-permute-start.3
  16.6 0.3 collective-permute-start.2
  16.8 0.3 collective-permute-start.1
  17.1 0.6 collective-permute-done.4.g_got_ref
  17.7 0.5 collective-permute-done.3.v_got_ref
  18.2 0.5 collective-permute-done.2.k_got_ref
  18.7 0.5 collective-permute-done.1.q_got_ref
  19.2 0.5 shard_map.105
  19.8 0.0 copy-start.13
  19.8 1.3 %shard_map.106 = (f32[2,6,112,112]{3,2,1,0:T(8,128)S(1)}, f32[2,8,128]{2,1,0:T(8,128)S(1)}) custom-call(bf16[2,6,112,128]{3,2,1,0:T(8,128)(2,1)S(1)} %get-tuple-element.54.a_ref, bf16[2,6,112,128]{3,2,1,0:T(8,128)(2,1)S(1)} %get-tuple-element.55.b_ref, bf16[2,6,112,128]{3,2,1,0:T(8,128)(2,1)S(1)} %get-tuple-element.56.v_ref, ...), custom_call_target="tpu_custom_call" | custom-call | flops 10000000 | bytes 2538496 | tf_op jit(solution)/shard_map/pallas_call | solution.py:454
  21.1 0.8 %copy-done.6 = f32[2,6,112,112]{3,2,1,0:T(8,128)} copy-done((f32[2,6,112,112]{3,2,1,0:T(8,128)}, f32[2,6,112,112]{3,2,1,0:T(8,128)S(1)}, u32[]{:S(2)}) %copy-start.6) | copy-done | bytes 602136
  21.9 4.6 %all-to-all-done.in_ref = f32[32,1,3200]{2,1,0:T(1,128)S(1)} async-done(((f32[32,1,3200]{2,1,0:T(1,128)}), f32[32,1,3200]{2,1,0:T(1,128)S(1)}, u32[]{:S(2)}, u32[]{:S(2)}) %all-to-all-start) | async-done | bytes 409632 | tf_op jit(solution)/shard_map/all_to_all | solution.py:486
  26.6 0.5 shard_map.107
  27.1 19.8 %all_to_all.15.in_ref = f32[32,1,4864]{2,1,0:T(1,128)S(1)} all-to-all(f32[32,1,4864]{2,1,0:T(1,128)S(1)} %get-tuple-element.63), channel_id=1, replica_groups=mesh['grp'=4,'seq'=8] {'grp','seq'}, dimensions={0} | all-to-all | bytes 1245184 | tf_op jit(solution)/shard_map/all_to_all | solution.py:486
  46.9 1.4 %shard_map.108 = (f32[32,1,3200]{2,1,0:T(1,128)}, f32[2,6,112,128]{3,2,1,0:T(8,128)S(1)}, f32[2,8,128]{2,1,0:T(8,128)S(1)}, f32[2,8,128]{2,1,0:T(8,128)S(1)}) custom-call(f32[32,1,4864]{2,1,0:T(1,128)S(1)} %all_to_all.15.in_ref, f32[2,6,112,112]{3,2,1,0:T(8,128)S(1)} %copy-done.7, bf16[2,6,112,128]{3,2,1,0:T(8,128)(2,1)S(1)} %get-tuple-element.54.a_ref, ...), custom_call_target="tpu_custom_call" | custom-call | flops 10000000 | bytes 3043328 | tf_op jit(solution)/shard_map/pallas_call | solution.py:454
  48.3 3.3 %all-to-all-start.2 = ((f32[32,1,3200]{2,1,0:T(1,128)}), f32[32,1,3200]{2,1,0:T(1,128)S(1)}, u32[]{:S(2)}, u32[]{:S(2)}) async-start(f32[32,1,3200]{2,1,0:T(1,128)} %get-tuple-element.67), calls=%async_computation.2 | async-start | bytes 819200 | tf_op jit(solution)/shard_map/all_to_all | solution.py:486
  51.6 0.0 copy-start.9
  51.6 1.4 %shard_map.109 = (f32[672,128]{1,0:T(8,128)S(1)}, f32[672,128]{1,0:T(8,128)S(1)}, bf16[2,6,128,128]{3,2,1,0:T(8,128)(2,1)S(1)}, bf16[2,6,112,128]{3,2,1,0:T(8,128)(2,1)S(1)}, bf16[2,6,112,128]{3,2,1,0:T(8,128)(2,1)S(1)}) custom-call(bf16[2,6,112,128]{3,2,1,0:T(8,128)(2,1)S(1)} %get-tuple-element.54.a_ref, ...), custom_call_target="tpu_custom_call" | custom-call | flops 10000000 | bytes 3858432 | tf_op jit(solution)/shard_map/pallas_call | solution.py:454
  53.0 0.3 collective-permute-start.5
  53.3 1.6 %shard_map.111 = (f32[6,112,112]{2,1,0:T(8,128)S(1)}, f32[672,128]{1,0:T(8,128)S(1)}, f32[672,128]{1,0:T(8,128)S(1)}, f32[6,112,112]{2,1,0:T(8,128)S(1)}, f32[67...) custom-call(bf16[2,6,112,128]{3,2,1,0:T(8,128)(2,1)S(1)} %get-tuple-element.73.a_ref, ...), custom_call_target="tpu_custom_call" | custom-call | flops 10000000 | bytes 3955712 | tf_op jit(solution)/shard_map/pallas_call | solution.py:454
  54.9 0.3 collective-permute-start.6
  55.3 0.3 collective-permute-start.7
  55.5 0.0 collective-permute-done.5.refs_1_
  55.5 0.8 %shard_map.110 = bf16[1232,128]{1,0:T(8,128)(2,1)} custom-call(f32[672,128]{1,0:T(8,128)S(1)} %get-tuple-element.71.refs_0_, f32[672,128]{1,0:T(8,128)S(1)} %collective-permute-done.5.refs_1_), custom_call_target="tpu_custom_call" | custom-call | flops 10000000 | bytes 1003520 | tf_op jit(solution)/shard_map/pallas_call | solution.py:454
  56.3 0.4 collective-permute-done.6.key_in_ref
  56.7 0.5 collective-permute-done.7.value_in_ref
  57.2 0.7 %copy-done.10 = f32[672,128]{1,0:T(8,128)} copy-done((f32[672,128]{1,0:T(8,128)}, f32[672,128]{1,0:T(8,128)S(1)}, u32[]{:S(2)}) %copy-start.10) | copy-done | bytes 344088
  57.9 7.3 %all-to-all-done.2.in_ref = f32[32,1,3200]{2,1,0:T(1,128)S(1)} async-done(((f32[32,1,3200]{2,1,0:T(1,128)}), f32[32,1,3200]{2,1,0:T(1,128)S(1)}, u32[]{:S(2)}, u32[]{:S(2)}) %all-to-all-start.2) | async-done | bytes 409632 | tf_op jit(solution)/shard_map/all_to_all | solution.py:486
  65.2 0.2 shard_map.112
  65.3 0.1 collective-permute-start.8
  65.4 0.0 copy-start.11
  65.4 0.6 shard_map.113
  66.0 1.1 %collective-permute-done.8.got_ref = f32[680,128]{1,0:T(8,128)S(1)} collective-permute-done((f32[680,128]{1,0:T(8,128)S(1)}, f32[680,128]{1,0:T(8,128)S(1)}, u32[]{:S(2)}, u32[]{:S(2)}) %collective-permute-start.8) | collective-permute-done | bytes 348192 | tf_op jit(solution)/shard_map/ppermute | solution.py:108
  67.0 1.2 %shard_map.114 = (bf16[1232,128]{1,0:T(8,128)(2,1)}, bf16[1232,128]{1,0:T(8,128)(2,1)}) custom-call(f32[680,128]{1,0:T(8,128)S(1)} %collective-permute-done.8.got_ref, bf16[1232,128]{1,0:T(8,128)(2,1)S(1)} %bitcast.10, bf16[1232,128]{1,0:T(8,128)(2,1)S(1)} %bitcast.14, f32[672,128]{1,0:T(8,128)S(1)} %collective-permute-done.6.key_in_ref, ...), custom_call_target="tpu_custom_call" | custom-call | flops 10000000 | bytes 2641920 | tf_op jit(solution)/shard_map/pallas_call | solution.py:454
  (19 shorter events, 0.1 us)
Async XLA Ops:
  0.6 1.0 %copy-start = (bf16[128,1232]{0,1:T(8,128)(2,1)S(1)}, bf16[128,1232]{0,1:T(8,128)(2,1)}, u32[]{:S(2)}) copy-start(bf16[128,1232]{0,1:T(8,128)(2,1)} %param.9) | copy-start | bytes 946180
  1.6 1.0 %copy-start.2 = (bf16[128,1232]{0,1:T(8,128)(2,1)S(1)}, bf16[128,1232]{0,1:T(8,128)(2,1)}, u32[]{:S(2)}) copy-start(bf16[128,1232]{0,1:T(8,128)(2,1)} %param.10) | copy-start | bytes 946180
  3.1 1.8 %collective-permute-start = (f32[680,128]{1,0:T(8,128)S(1)}, f32[680,128]{1,0:T(8,128)S(1)}, u32[]{:S(2)}, u32[]{:S(2)}) collective-permute-start(f32[680,128]{1,0:T(8,128)S(1)} %get-tuple-element.48), channel_id=1, source_target_pairs={{0,1},{1,0},{2,3},{3,2},{4,5},{5,4},{6,7},{7,6},{8,9},{9,8},{10,11... | collective-permute-start | bytes 1044488 | tf_op jit(solution)/shard_map/ppermute | solution.py:108
  5.8 7.2 %copy-start.4 = (bf16[128,1232]{0,1:T(8,128)(2,1)S(1)}, bf16[128,1232]{0,1:T(8,128)(2,1)}, u32[]{:S(2)}) copy-start(bf16[128,1232]{0,1:T(8,128)(2,1)} %param.8) | copy-start | bytes 946180
  5.8 20.8 %all-to-all-start = ((f32[32,1,3200]{2,1,0:T(1,128)}), f32[32,1,3200]{2,1,0:T(1,128)S(1)}, u32[]{:S(2)}, u32[]{:S(2)}) async-start(f32[32,1,3200]{2,1,0:T(1,128)} %shard_map.104), calls=%async_computation | async-start | bytes 819200 | tf_op jit(solution)/shard_map/all_to_all | solution.py:486
  13.1 1.0 %copy-start.1 = (bf16[128,1232]{0,1:T(8,128)(2,1)S(1)}, bf16[128,1232]{0,1:T(8,128)(2,1)}, u32[]{:S(2)}) copy-start(bf16[128,1232]{0,1:T(8,128)(2,1)} %param.9) | copy-start | bytes 946180
  14.0 1.0 %copy-start.3 = (bf16[128,1232]{0,1:T(8,128)(2,1)S(1)}, bf16[128,1232]{0,1:T(8,128)(2,1)}, u32[]{:S(2)}) copy-start(bf16[128,1232]{0,1:T(8,128)(2,1)} %param.10) | copy-start | bytes 946180
  15.0 1.0 %copy-start.5 = (bf16[128,1232]{0,1:T(8,128)(2,1)S(1)}, bf16[128,1232]{0,1:T(8,128)(2,1)}, u32[]{:S(2)}) copy-start(bf16[128,1232]{0,1:T(8,128)(2,1)} %param.11) | copy-start | bytes 946180
  16.0 3.8 %copy-start.8 = (f32[11,112,112]{2,1,0:T(8,128)S(1)}, f32[11,112,112]{2,1,0:T(8,128)}, u32[]{:S(2)}) copy-start(f32[11,112,112]{2,1,0:T(8,128)} %state_in_ref.1) | copy-start | bytes 1655812
  16.0 1.7 %collective-permute-start.4 = (f32[672,128]{1,0:T(8,128)S(1)}, f32[672,128]{1,0:T(8,128)S(1)}, u32[]{:S(2)}, u32[]{:S(2)}) collective-permute-start(f32[672,128]{1,0:T(8,128)S(1)} %dynamic-slice_convert_fusion), channel_id=1, source_target_pairs={{0,1},{1,0},{2,3},{3,2},{4,5},{5,4},{6,7},{7,6},{8,9},{9,8},{10,11... | collective-permute-start | bytes 1032200 | tf_op jit(solution)/shard_map/ppermute | solution.py:108
  16.3 1.9 %collective-permute-start.3 = (f32[672,128]{1,0:T(8,128)S(1)}, f32[672,128]{1,0:T(8,128)S(1)}, u32[]{:S(2)}, u32[]{:S(2)}) collective-permute-start(f32[672,128]{1,0:T(8,128)S(1)} %dynamic-slice_convert_fusion.1), channel_id=1, source_target_pairs={{0,1},{1,0},{2,3},{3,2},{4,5},{5,4},{6,7},{7,6},{8,9},{9,8},{10,11... | collective-permute-start | bytes 1032200 | tf_op jit(solution)/shard_map/ppermute | solution.py:108
  16.6 2.1 %collective-permute-start.2 = (f32[672,128]{1,0:T(8,128)S(1)}, f32[672,128]{1,0:T(8,128)S(1)}, u32[]{:S(2)}, u32[]{:S(2)}) collective-permute-start(f32[672,128]{1,0:T(8,128)S(1)} %dynamic-slice_convert_fusion.2), channel_id=1, source_target_pairs={{0,1},{1,0},{2,3},{3,2},{4,5},{5,4},{6,7},{7,6},{8,9},{9,8},{10,11... | collective-permute-start | bytes 1032200 | tf_op jit(solution)/shard_map/ppermute | solution.py:108
  16.8 2.4 %collective-permute-start.1 = (f32[672,128]{1,0:T(8,128)S(1)}, f32[672,128]{1,0:T(8,128)S(1)}, u32[]{:S(2)}, u32[]{:S(2)}) collective-permute-start(f32[672,128]{1,0:T(8,128)S(1)} %dynamic-slice_convert_fusion.3), channel_id=1, source_target_pairs={{0,1},{1,0},{2,3},{3,2},{4,5},{5,4},{6,7},{7,6},{8,9},{9,8},{10,11... | collective-permute-start | bytes 1032200 | tf_op jit(solution)/shard_map/ppermute | solution.py:108
  19.8 6.8 %copy-start.13 = (f32[11,112]{1,0:T(8,128)S(1)}, f32[11,112]{1,0:T(8,128)}, u32[]{:S(2)}) copy-start(f32[11,112]{1,0:T(8,128)} %norm_in_ref.1) | copy-start | bytes 14788
  21.1 0.9 %copy-start.6 = (f32[2,6,112,112]{3,2,1,0:T(8,128)}, f32[2,6,112,112]{3,2,1,0:T(8,128)S(1)}, u32[]{:S(2)}) copy-start(f32[2,6,112,112]{3,2,1,0:T(8,128)S(1)} %get-tuple-element.64.before_ref) | copy-start | bytes 1806340
  27.1 19.8 %copy-start.7 = (f32[2,6,112,112]{3,2,1,0:T(8,128)S(1)}, f32[2,6,112,112]{3,2,1,0:T(8,128)}, u32[]{:S(2)}) copy-start(f32[2,6,112,112]{3,2,1,0:T(8,128)} %copy-done.6) | copy-start | bytes 1806340
  48.3 16.9 %all-to-all-start.2 = ((f32[32,1,3200]{2,1,0:T(1,128)}), f32[32,1,3200]{2,1,0:T(1,128)S(1)}, u32[]{:S(2)}, u32[]{:S(2)}) async-start(f32[32,1,3200]{2,1,0:T(1,128)} %get-tuple-element.67), calls=%async_computation.2 | async-start | bytes 819200 | tf_op jit(solution)/shard_map/all_to_all | solution.py:486
  51.6 1.7 %copy-start.9 = (f32[11,112,112]{2,1,0:T(8,128)S(1)}, f32[11,112,112]{2,1,0:T(8,128)}, u32[]{:S(2)}) copy-start(f32[11,112,112]{2,1,0:T(8,128)} %grad_state_ref.1) | copy-start | bytes 1655812
  53.0 2.5 %collective-permute-start.5 = (f32[672,128]{1,0:T(8,128)S(1)}, f32[672,128]{1,0:T(8,128)S(1)}, u32[]{:S(2)}, u32[]{:S(2)}) collective-permute-start(f32[672,128]{1,0:T(8,128)S(1)} %get-tuple-element.72), channel_id=1, source_target_pairs={{0,1},{1,0},{2,3},{3,2},{4,5},{5,4},{6,7},{7,6},{8,9},{9,8},{10,11... | collective-permute-start | bytes 1032200 | tf_op jit(solution)/shard_map/ppermute | solution.py:108
  54.9 1.7 %collective-permute-start.6 = (f32[672,128]{1,0:T(8,128)S(1)}, f32[672,128]{1,0:T(8,128)S(1)}, u32[]{:S(2)}, u32[]{:S(2)}) collective-permute-start(f32[672,128]{1,0:T(8,128)S(1)} %get-tuple-element.76), channel_id=1, source_target_pairs={{0,1},{1,0},{2,3},{3,2},{4,5},{5,4},{6,7},{7,6},{8,9},{9,8},{10,11... | collective-permute-start | bytes 1032200 | tf_op jit(solution)/shard_map/ppermute | solution.py:108
  55.3 1.9 %collective-permute-start.7 = (f32[672,128]{1,0:T(8,128)S(1)}, f32[672,128]{1,0:T(8,128)S(1)}, u32[]{:S(2)}, u32[]{:S(2)}) collective-permute-start(f32[672,128]{1,0:T(8,128)S(1)} %get-tuple-element.77), channel_id=1, source_target_pairs={{0,1},{1,0},{2,3},{3,2},{4,5},{5,4},{6,7},{7,6},{8,9},{9,8},{10,11... | collective-permute-start | bytes 1032200 | tf_op jit(solution)/shard_map/ppermute | solution.py:108
  55.5 9.6 %copy-start.12 = (f32[11,112]{1,0:T(8,128)S(1)}, f32[11,112]{1,0:T(8,128)}, u32[]{:S(2)}) copy-start(f32[11,112]{1,0:T(8,128)} %grad_norm_ref.3) | copy-start | bytes 14788
  57.2 0.8 %copy-start.10 = (f32[672,128]{1,0:T(8,128)}, f32[672,128]{1,0:T(8,128)S(1)}, u32[]{:S(2)}) copy-start(f32[672,128]{1,0:T(8,128)S(1)} %collective-permute-done.7.value_in_ref) | copy-start | bytes 1032196
  65.3 1.7 %collective-permute-start.8 = (f32[680,128]{1,0:T(8,128)S(1)}, f32[680,128]{1,0:T(8,128)S(1)}, u32[]{:S(2)}, u32[]{:S(2)}) collective-permute-start(f32[680,128]{1,0:T(8,128)S(1)} %shard_map.112), channel_id=1, source_target_pairs={{0,1},{1,0},{2,3},{3,2},{4,5},{5,4},{6,7},{7,6},{8,9},{9,8},{10,11... | collective-permute-start | bytes 1044488 | tf_op jit(solution)/shard_map/ppermute | solution.py:108
  65.4 1.6 %copy-start.11 = (f32[672,128]{1,0:T(8,128)S(1)}, f32[672,128]{1,0:T(8,128)}, u32[]{:S(2)}) copy-start(f32[672,128]{1,0:T(8,128)} %copy-done.10) | copy-start | bytes 1032196

commit v6 on v5

--- a/solution.py
+++ b/solution.py
@@ -1,4 +1,5 @@
 import functools
+from typing import NamedTuple
 
 import jax
 import jax.numpy as jnp
@@ -10,6 +11,7 @@
 F32 = jnp.float32
 BF16 = jnp.bfloat16
 LANES = 128
+HALF = LANES // 2
 SUB = 8
 VMEM_BYTES = 67_043_328
 FREE = 48 * 2**20
@@ -47,6 +49,12 @@
 
 def added(rows):
     return rows[0:1] + rows[1:2] + rows[2:3]
+
+
+class Area(NamedTuple):
+    start: int
+    half_slot: int
+    half_lane: int
 
 
 class Plan:
@@ -64,28 +72,49 @@
         self.donors = self.tiles // (self.pieces + 1) if self.pieces else 0
         self.stored = self.tiles - self.donors
         self.whole = self.stored // devices
-        self.slots = self.whole * SUB + -(-(self.stored - self.whole * devices) // self.per_slot)
-        self.span = self.slots * LANES
-
-    def put(self, ref, base, tile, value):
+        single, self.left = divmod(self.stored - self.whole * devices, self.per_slot)
+        self.single_end = self.whole * devices + single * self.per_slot
+        self.full = self.whole * SUB + single
+        self.span = (self.full + 1) * LANES
+        self.norm_slots = self.half - 1
+        fits = self.norm_slots < self.pieces <= self.norm_slots + HALF // self.spare
+        if not fits or 2 * self.left > self.per_slot:
+            raise ValueError("unsupported sizes")
+        self.single = self.span + self.norm_slots * LANES
+        self.double = (2 * self.full + 1) * LANES
+
+    def put(self, ref, area, tile, value):
+        if tile < self.single_end:
+            index, shape = self.place(area, tile)
+            ref[index] = value.reshape(shape)
+        else:
+            for side, index in enumerate(self.halves(area, tile - self.single_end)):
+                ref[index] = value[:, side * HALF : (side + 1) * HALF]
+
+    def get(self, ref, area, tile):
+        if tile < self.single_end:
+            return ref[self.place(area, tile)[0]].reshape(SUB, LANES)
+        return jnp.concatenate(
+            [ref[index] for index in self.halves(area, tile - self.single_end)], axis=1
+        )
+
+    def place(self, area, tile):
         if tile < self.whole * self.devices:
             slot, piece = divmod(tile, self.devices)
-            columns = pl.ds((base + slot * SUB) * LANES, SUB * LANES)
-            ref[piece, :, columns] = value.reshape(1, SUB * LANES)
-        else:
-            ref[self.place(base, tile)] = value
-
-    def get(self, ref, base, tile):
-        if tile < self.whole * self.devices:
-            slot, piece = divmod(tile, self.devices)
-            columns = pl.ds((base + slot * SUB) * LANES, SUB * LANES)
-            return ref[piece, :, columns].reshape(SUB, LANES)
-        return ref[self.place(base, tile)]
-
-    def place(self, base, tile):
+            columns = pl.ds((area.start + slot * SUB) * LANES, SUB * LANES)
+            return (piece, slice(None), columns), (1, SUB * LANES)
         slot, part = divmod(tile - self.whole * self.devices, self.per_slot)
-        slot += self.whole * SUB
-        return pl.ds(part * SUB, SUB), 0, pl.ds((base + slot) * LANES, LANES)
+        slot += area.start + self.whole * SUB
+        return (pl.ds(part * SUB, SUB), 0, pl.ds(slot * LANES, LANES)), (SUB, LANES)
+
+    def halves(self, area, part):
+        columns = pl.ds(area.half_slot * LANES + area.half_lane, HALF)
+        for side in range(2):
+            yield pl.ds((part + side * (self.per_slot // 2)) * SUB, SUB), 0, columns
+
+    def areas(self):
+        full = self.full
+        return Area(0, full, 0), Area(full + 1, full, HALF), Area(1, 0, HALF)
 
     def own(self, ref, core, head):
         start = pl.multiple_of(core * (self.shift * self.width) + head * self.width, 16)
@@ -115,7 +144,7 @@
     return jnp.concatenate([tile, jnp.zeros((rows, LANES - columns), tile.dtype)], axis=1)
 
 
-def store_rows(plan, ref, base, head, block, held):
+def store_rows(plan, ref, area, head, block, held):
     block = wide(block)
     lane = lax.broadcasted_iota(jnp.int32, (SUB, LANES), 1)
     for j in range(plan.head_tiles):
@@ -128,32 +157,45 @@
             donor, piece = divmod(at, plan.pieces)
             moved = pltpu.roll(held[donor], plan.width - piece * plan.spare, 1)
             tile = jnp.where(lane >= plan.width, moved, tile)
-        plan.put(ref, base, at, tile)
-
-
-def store_padding(plan, ref, base):
-    rest = (plan.slots - plan.whole * SUB) * plan.per_slot + plan.whole * plan.devices
-    for tile in range(plan.stored, rest):
-        ref[plan.place(base, tile)] = jnp.zeros((SUB, LANES), F32)
-
-
-def store_norms(plan, ref, rows):
-    rows = rows.reshape(1, plan.extra * LANES)[:, : plan.half * LANES]
+        plan.put(ref, area, at, tile)
+
+
+def store_padding(plan, ref, area):
+    for part in range(plan.left, plan.per_slot // 2):
+        for index in plan.halves(area, part):
+            ref[index] = jnp.zeros((SUB, HALF), F32)
+
+
+def store_norms(plan, ref, rows, area):
+    spare, width, last = plan.spare, plan.width, plan.half - 1
+    free = HALF - area.half_lane
+    shape = (SUB, LANES)
+    lane = lax.broadcasted_iota(jnp.int32, shape, 1)
+    row = lax.broadcasted_iota(jnp.int32, shape, 0)
+    carried = jnp.broadcast_to(rows[last : last + 1], shape)
+    packed = rows[:SUB]
+    for j in range(plan.norm_slots):
+        moved = pltpu.roll(carried, width - j * spare, 1)
+        packed = jnp.where((row == j) & (lane >= width), moved, packed)
+    packed = packed.reshape(1, SUB * LANES)[:, : plan.norm_slots * LANES]
+    extra = pltpu.roll(carried, (free - plan.norm_slots * spare) % LANES, 1)
+    extra = extra[0:1, free : free + HALF]
     for piece in range(plan.devices):
-        ref[piece, :, pl.ds(plan.span, plan.half * LANES)] = rows
-
-
-def load_rows(plan, ref, base, head):
+        ref[piece, :, pl.ds(plan.span, plan.norm_slots * LANES)] = packed
+        ref[piece, :, pl.ds(area.half_slot * LANES + free, HALF)] = extra
+
+
+def load_rows(plan, ref, area, head):
     lane = lax.broadcasted_iota(jnp.int32, (SUB, LANES), 1)
     tiles = []
     for j in range(plan.head_tiles):
         at = head * plan.head_tiles + j
         if at < plan.stored:
-            tiles.append(plan.get(ref, base, at))
+            tiles.append(plan.get(ref, area, at))
             continue
         tile = None
         for piece in range(plan.pieces):
-            part = plan.get(ref, base, (at - plan.stored) * plan.pieces + piece)
+            part = plan.get(ref, area, (at - plan.stored) * plan.pieces + piece)
             part = pltpu.roll(part, (LANES - plan.width + piece * plan.spare) % LANES, 1)
             tile = part if tile is None else jnp.where(lane >= piece * plan.spare, part, tile)
         tiles.append(tile)
@@ -185,14 +227,34 @@
     each(chips, step, (zero, zero))
 
 
-def scan_norms(plan, in_ref, core, chip, later):
-    columns = pl.ds(plan.span, plan.half * LANES)
-
-    def step(i, total):
+def scan_norms(plan, in_ref, core, chip, later, area):
+    spare, width = plan.spare, plan.width
+    free = HALF - area.half_lane
+    columns = pl.ds(plan.span, plan.norm_slots * LANES)
+    extras = pl.ds(area.half_slot * LANES, LANES)
+
+    def step(i, totals):
         take = (i > chip) if later else (i < chip)
-        return total + jnp.where(take, in_ref[2 * i + core, :, columns], 0.0)
-
-    return each(plan.devices // 2, step, jnp.zeros((1, plan.half * LANES), F32))
+        row = 2 * i + core
+        return (
+            totals[0] + jnp.where(take, in_ref[row, :, columns], 0.0),
+            totals[1] + jnp.where(take, in_ref[row, :, extras], 0.0),
+        )
+
+    zeros = (jnp.zeros((1, plan.norm_slots * LANES), F32), jnp.zeros((1, LANES), F32))
+    packed, extra = each(plan.devices // 2, step, zeros)
+    shape = (SUB, LANES)
+    lane = lax.broadcasted_iota(jnp.int32, shape, 1)
+    rows = [packed[:, j * LANES : (j + 1) * LANES] for j in range(plan.norm_slots)]
+    last = None
+    for j, row in enumerate(rows):
+        moved = jnp.broadcast_to(row, shape)
+        moved = pltpu.roll(moved, (LANES - width + j * spare) % LANES, 1)
+        last = moved if last is None else jnp.where(lane >= j * spare, moved, last)
+    at = plan.norm_slots * spare
+    moved = pltpu.roll(jnp.broadcast_to(extra, shape), (at - free) % LANES, 1)
+    last = jnp.where(lane >= at, moved, last)
+    return [row[:, :width] for row in rows] + [last[0:1, :width]]
 
 
 def causal_mask(length):
@@ -221,12 +283,13 @@
 
 
 def chip_state(plan, own_ref, got_ref, out_ref):
+    area = plan.areas()[0]
     held = {}
     for h in reversed(range(plan.half)):
         rows = slice(h * plan.width, (h + 1) * plan.width)
-        store_rows(plan, out_ref, 0, h, own_ref[rows, :] + got_ref[rows, :], held)
-    store_padding(plan, out_ref, 0)
-    store_norms(plan, out_ref, own_ref[plan.rows :, :] + got_ref[plan.rows :, :])
+        store_rows(plan, out_ref, area, h, own_ref[rows, :] + got_ref[rows, :], held)
+    store_padding(plan, out_ref, area)
+    store_norms(plan, out_ref, own_ref[plan.rows :, :] + got_ref[plan.rows :, :], area)
 
 
 def pack_tokens(
@@ -255,12 +318,13 @@
     core, chip = my_core(), my_device() >> 1
     flags = (core.astype(F32), (1 - core).astype(F32))
     width = plan.width
-    norms = scan_norms(plan, in_ref, core, chip, False)
+    first, second, _ = plan.areas()
+    norms = scan_norms(plan, in_ref, core, chip, False, first)
     scan_rows(plan, in_ref, 0, out_ref, False)
     held = {}
     for h in reversed(range(plan.half)):
         base = norm_in_ref[pl.ds(core * plan.shift + h, 1), :]
-        base = base + norms[0:1, h * LANES : h * LANES + width]
+        base = base + norms[h]
         features, grads = [], []
         for i in range(2):
             z = base + flags[i] * norm_ref[1 - i, h : h + 1, :width]
@@ -272,8 +336,8 @@
             features.append(a)
             grads.append((g_ref[i, h].astype(F32) * inverse).astype(BF16))
         state = nt(jnp.concatenate(features, axis=1), jnp.concatenate(grads, axis=1))
-        store_rows(plan, out_ref, plan.slots, h, state, held)
-    store_padding(plan, out_ref, plan.slots)
+        store_rows(plan, out_ref, second, h, state, held)
+    store_padding(plan, out_ref, second)
 
 
 def before_states(
@@ -301,10 +365,11 @@
     plan, in_ref, before_ref, a_ref, g_ref, inverse_ref, inner_ref,
     out_ref, product_ref, c_ref, m_ref,
 ):
-    scan_rows(plan, in_ref, plan.span, out_ref, True)
+    first, _, third = plan.areas()
+    scan_rows(plan, in_ref, plan.full * LANES, out_ref, True)
     totals = []
     for h in range(plan.half):
-        base = load_rows(plan, in_ref, 0, h)
+        base = load_rows(plan, in_ref, first, h)
         total = None
         for i in range(2):
             high, low = parts(base + before_ref[i, h])
@@ -321,7 +386,7 @@
             total = m if total is None else total + m
         totals.append(total)
     totals += [jnp.zeros((1, LANES), F32)] * (plan.extra - plan.half)
-    store_norms(plan, out_ref, jnp.concatenate(totals, axis=0))
+    store_norms(plan, out_ref, jnp.concatenate(totals, axis=0), third)
 
 
 def query_grads(
@@ -369,16 +434,13 @@
 def suffix_norms(plan, in_ref, grad_norm_ref, m_ref, i):
     core, chip = my_core(), my_device() >> 1
     flag = (core if i else 1 - core).astype(F32)
-    norms = scan_norms(plan, in_ref, core, chip, True)
+    norms = scan_norms(plan, in_ref, core, chip, True, plan.areas()[2])
+    rows = [
+        norm + grad_norm_ref[pl.ds(core * plan.shift + h, 1), :] for h, norm in enumerate(norms)
+    ]
     zeros = plan.extra - plan.half
-    norms = jnp.concatenate(
-        [norms[:, h * LANES : (h + 1) * LANES] for h in range(plan.half)]
-        + [jnp.zeros((zeros, LANES), F32)] * (zeros > 0), axis=0,
-    )
-    own_rows = [
-        grad_norm_ref[pl.ds(core * plan.shift + h, 1), :] for h in range(plan.half)
-    ] + [jnp.zeros((zeros, plan.width), F32)] * (zeros > 0)
-    return norms + wide(jnp.concatenate(own_rows, axis=0)) + flag * m_ref[1 - i]
+    rows += [jnp.zeros((zeros, plan.width), F32)] * (zeros > 0)
+    return wide(jnp.concatenate(rows, axis=0)) + flag * m_ref[1 - i]
 
 
 def key_value(state, column, b, v):
@@ -393,7 +455,7 @@
     out_ref[plan.rows :, :] = suffix_norms(plan, in_ref, grad_norm_ref, m_ref, 1)
     for h in range(plan.half):
         rows = slice(h * plan.width, (h + 1) * plan.width)
-        out_ref[rows, :] = wide(load_rows(plan, in_ref, 0, h) + after_ref[h])
+        out_ref[rows, :] = wide(load_rows(plan, in_ref, plan.areas()[2], h) + after_ref[h])
 
 
 def own_grads(
@@ -403,7 +465,7 @@
     columns = suffix_norms(plan, in_ref, grad_norm_ref, m_ref, 0).T
     for h in range(plan.half):
         rows = slice(h * plan.width, (h + 1) * plan.width)
-        state = load_rows(plan, in_ref, 0, h) + after_ref[h]
+        state = load_rows(plan, in_ref, plan.areas()[2], h) + after_ref[h]
         key, value = key_value(state, columns[: plan.width, h : h + 1], b_ref[0, h], v_ref[0, h])
         key_ref[rows, :] = (key + key_in_ref[rows, :]).astype(BF16)
         value_ref[rows, :] = (value + value_in_ref[rows, :]).astype(BF16)
@@ -497,8 +559,8 @@
     rows = shape((2, plan.extra, LANES))
     after = shape((half, width, width))
     block = shape((plan.rows + plan.extra, LANES))
-    sent_single = shape((devices, 1, plan.span + half * LANES))
-    sent_double = shape((devices, 1, 2 * plan.span))
+    sent_single = shape((devices, 1, plan.single))
+    sent_double = shape((devices, 1, plan.double))
 
     send, block_own = call(bind(block_states), (block, block), (k, v))
     block_got = pair_swap(send)

time: 68.7 us -> 67.9 us (0.988)
  waiting for transfers between devices: 17.2 us -> 16.5 us
where the time goes in v6:
time: 67.9 us; the launch traced here: 67.5 us
  blocking collectives  19.4 us (29%)
  waiting for transfers between devices  16.5 us (24%)
  starting transfers between devices  13.1 us (19%)
  Pallas kernels  11.2 us (16%)
  local copies, waits for them, and re-layouts  6.36 us (9%)
  between operations  0.81 us (1%)
    all_to_all x1, blocking collectives, exchange(): return lax.all_to_all(x, both, 0, 0, tiled=True)  19.4 us
    all_to_all x2, waiting for transfers between devices, exchange(): return lax.all_to_all(x, both, 0, 0, tiled=True)  11.3 us
    pallas_call x12, Pallas kernels, call(): pl.pallas_call(body, out_shape=outs, in_specs=in_specs, out_specs=[vmem]...  11.2 us
    all_to_all x2, starting transfers between devices, exchange(): return lax.all_to_all(x, both, 0, 0, tiled=True)  10.5 us
    unnamed x28, local copies, waits for them, and re-layouts  6.36 us
    ppermute x9, waiting for transfers between devices, pair_swap(): return lax.ppermute(x, 'seq', [(i, i ^ 1) for i in range(size)])  5.21 us
    ppermute x9, starting transfers between devices, pair_swap(): return lax.ppermute(x, 'seq', [(i, i ^ 1) for i in range(size)])  2.61 us
  transfers between devices with their start and end apart: 11, of which 10 were waited for; matrix products, arithmetic and copies ran while one was open for 0% of the time, Pallas kernels for 9%

profile of v6, /device:TPU:0, one launch (start us, length us, event | category | flops | bytes accessed | tf_op | source)
XLA Modules:
  0.0 67.5 jit_solution(16467934740638335984)
XLA Ops:
  0.6 0.0 copy-start
  0.6 1.0 %copy-done = bf16[128,1232]{0,1:T(8,128)(2,1)S(1)} copy-done((bf16[128,1232]{0,1:T(8,128)(2,1)S(1)}, bf16[128,1232]{0,1:T(8,128)(2,1)}, u32[]{:S(2)}) %copy-start) | copy-done | bytes 315416
  1.6 1.0 %copy-done.2 = bf16[128,1232]{0,1:T(8,128)(2,1)S(1)} copy-done((bf16[128,1232]{0,1:T(8,128)(2,1)S(1)}, bf16[128,1232]{0,1:T(8,128)(2,1)}, u32[]{:S(2)}) %copy-start.2) | copy-done | bytes 315416
  2.6 0.5 shard_map.103
  3.1 0.6 collective-permute-start
  3.6 1.3 %collective-permute-done.got_ref = f32[680,128]{1,0:T(8,128)S(1)} collective-permute-done((f32[680,128]{1,0:T(8,128)S(1)}, f32[680,128]{1,0:T(8,128)S(1)}, u32[]{:S(2)}, u32[]{:S(2)}) %collective-permute-start) | collective-permute-done | bytes 348192 | tf_op jit(solution)/shard_map/ppermute | solution.py:137
  4.9 0.9 %shard_map.104 = f32[32,1,3072]{2,1,0:T(1,128)} custom-call(f32[680,128]{1,0:T(8,128)S(1)} %get-tuple-element.47.own_ref, f32[680,128]{1,0:T(8,128)S(1)} %collective-permute-done.got_ref), custom_call_target="tpu_custom_call" | custom-call | flops 10000000 | bytes 1089536 | tf_op jit(solution)/shard_map/pallas_call | solution.py:516
  5.9 7.2 %all-to-all-start = ((f32[32,1,3072]{2,1,0:T(1,128)}), f32[32,1,3072]{2,1,0:T(1,128)S(1)}, u32[]{:S(2)}, u32[]{:S(2)}) async-start(f32[32,1,3072]{2,1,0:T(1,128)} %shard_map.104), calls=%async_computation | async-start | bytes 786432 | tf_op jit(solution)/shard_map/all_to_all | solution.py:548
  13.1 0.0 copy-done.4
  13.1 0.0 copy-start.1
  13.1 0.9 %copy-done.1 = bf16[128,1232]{0,1:T(8,128)(2,1)S(1)} copy-done((bf16[128,1232]{0,1:T(8,128)(2,1)S(1)}, bf16[128,1232]{0,1:T(8,128)(2,1)}, u32[]{:S(2)}) %copy-start.1) | copy-done | bytes 315416
  14.1 0.9 %copy-done.3 = bf16[128,1232]{0,1:T(8,128)(2,1)S(1)} copy-done((bf16[128,1232]{0,1:T(8,128)(2,1)S(1)}, bf16[128,1232]{0,1:T(8,128)(2,1)}, u32[]{:S(2)}) %copy-start.3) | copy-done | bytes 315416
  15.1 0.9 %copy-done.5 = bf16[128,1232]{0,1:T(8,128)(2,1)S(1)} copy-done((bf16[128,1232]{0,1:T(8,128)(2,1)S(1)}, bf16[128,1232]{0,1:T(8,128)(2,1)}, u32[]{:S(2)}) %copy-start.5) | copy-done | bytes 315416
  16.0 0.0 copy-start.8
  16.0 0.3 collective-permute-start.4
  16.3 0.3 collective-permute-start.3
  16.6 0.3 collective-permute-start.2
  16.9 0.3 collective-permute-start.1
  17.1 0.6 collective-permute-done.4.g_got_ref
  17.7 0.5 collective-permute-done.3.v_got_ref
  18.2 0.5 collective-permute-done.2.k_got_ref
  18.7 0.5 collective-permute-done.1.q_got_ref
  19.2 0.5 shard_map.105
  19.8 0.0 copy-start.13
  19.8 1.3 %shard_map.106 = (f32[2,6,112,112]{3,2,1,0:T(8,128)S(1)}, f32[2,8,128]{2,1,0:T(8,128)S(1)}) custom-call(bf16[2,6,112,128]{3,2,1,0:T(8,128)(2,1)S(1)} %get-tuple-element.54.a_ref, bf16[2,6,112,128]{3,2,1,0:T(8,128)(2,1)S(1)} %get-tuple-element.55.b_ref, bf16[2,6,112,128]{3,2,1,0:T(8,128)(2,1)S(1)} %get-tuple-element.56.v_ref, ...), custom_call_target="tpu_custom_call" | custom-call | flops 10000000 | bytes 2538496 | tf_op jit(solution)/shard_map/pallas_call | solution.py:516
  21.1 0.8 %copy-done.6 = f32[2,6,112,112]{3,2,1,0:T(8,128)} copy-done((f32[2,6,112,112]{3,2,1,0:T(8,128)}, f32[2,6,112,112]{3,2,1,0:T(8,128)S(1)}, u32[]{:S(2)}) %copy-start.6) | copy-done | bytes 602136
  22.0 4.3 %all-to-all-done.in_ref = f32[32,1,3072]{2,1,0:T(1,128)S(1)} async-done(((f32[32,1,3072]{2,1,0:T(1,128)}), f32[32,1,3072]{2,1,0:T(1,128)S(1)}, u32[]{:S(2)}, u32[]{:S(2)}) %all-to-all-start) | async-done | bytes 393248 | tf_op jit(solution)/shard_map/all_to_all | solution.py:548
  26.3 0.6 shard_map.107
  26.9 19.4 %all_to_all.15.in_ref = f32[32,1,4736]{2,1,0:T(1,128)S(1)} all-to-all(f32[32,1,4736]{2,1,0:T(1,128)S(1)} %get-tuple-element.63), channel_id=1, replica_groups=mesh['grp'=4,'seq'=8] {'grp','seq'}, dimensions={0} | all-to-all | bytes 1212416 | tf_op jit(solution)/shard_map/all_to_all | solution.py:548
  46.4 1.5 %shard_map.108 = (f32[32,1,3072]{2,1,0:T(1,128)}, f32[2,6,112,128]{3,2,1,0:T(8,128)S(1)}, f32[2,8,128]{2,1,0:T(8,128)S(1)}, f32[2,8,128]{2,1,0:T(8,128)S(1)}) custom-call(f32[32,1,4736]{2,1,0:T(1,128)S(1)} %all_to_all.15.in_ref, f32[2,6,112,112]{3,2,1,0:T(8,128)S(1)} %copy-done.7, bf16[2,6,112,128]{3,2,1,0:T(8,128)(2,1)S(1)} %get-tuple-element.54.a_ref, ...), custom_call_target="tpu_custom_call" | custom-call | flops 10000000 | bytes 3010560 | tf_op jit(solution)/shard_map/pallas_call | solution.py:516
  47.8 3.2 %all-to-all-start.2 = ((f32[32,1,3072]{2,1,0:T(1,128)}), f32[32,1,3072]{2,1,0:T(1,128)S(1)}, u32[]{:S(2)}, u32[]{:S(2)}) async-start(f32[32,1,3072]{2,1,0:T(1,128)} %get-tuple-element.67), calls=%async_computation.2 | async-start | bytes 786432 | tf_op jit(solution)/shard_map/all_to_all | solution.py:548
  51.1 0.0 copy-start.9
  51.1 1.4 %shard_map.109 = (f32[672,128]{1,0:T(8,128)S(1)}, f32[672,128]{1,0:T(8,128)S(1)}, bf16[2,6,128,128]{3,2,1,0:T(8,128)(2,1)S(1)}, bf16[2,6,112,128]{3,2,1,0:T(8,128)(2,1)S(1)}, bf16[2,6,112,128]{3,2,1,0:T(8,128)(2,1)S(1)}) custom-call(bf16[2,6,112,128]{3,2,1,0:T(8,128)(2,1)S(1)} %get-tuple-element.54.a_ref, ...), custom_call_target="tpu_custom_call" | custom-call | flops 10000000 | bytes 3858432 | tf_op jit(solution)/shard_map/pallas_call | solution.py:516
  52.5 0.3 collective-permute-start.5
  52.8 1.6 %shard_map.111 = (f32[6,112,112]{2,1,0:T(8,128)S(1)}, f32[672,128]{1,0:T(8,128)S(1)}, f32[672,128]{1,0:T(8,128)S(1)}, f32[6,112,112]{2,1,0:T(8,128)S(1)}, f32[67...) custom-call(bf16[2,6,112,128]{3,2,1,0:T(8,128)(2,1)S(1)} %get-tuple-element.73.a_ref, ...), custom_call_target="tpu_custom_call" | custom-call | flops 10000000 | bytes 3955712 | tf_op jit(solution)/shard_map/pallas_call | solution.py:516
  54.4 0.3 collective-permute-start.6
  54.7 0.3 collective-permute-start.7
  55.0 0.0 collective-permute-done.5.refs_1_
  55.0 0.8 %shard_map.110 = bf16[1232,128]{1,0:T(8,128)(2,1)} custom-call(f32[672,128]{1,0:T(8,128)S(1)} %get-tuple-element.71.refs_0_, f32[672,128]{1,0:T(8,128)S(1)} %collective-permute-done.5.refs_1_), custom_call_target="tpu_custom_call" | custom-call | flops 10000000 | bytes 1003520 | tf_op jit(solution)/shard_map/pallas_call | solution.py:516
  55.7 0.4 collective-permute-done.6.key_in_ref
  56.1 0.5 collective-permute-done.7.value_in_ref
  56.6 0.7 %copy-done.10 = f32[672,128]{1,0:T(8,128)} copy-done((f32[672,128]{1,0:T(8,128)}, f32[672,128]{1,0:T(8,128)S(1)}, u32[]{:S(2)}) %copy-start.10) | copy-done | bytes 344088
  57.4 7.0 %all-to-all-done.2.in_ref = f32[32,1,3072]{2,1,0:T(1,128)S(1)} async-done(((f32[32,1,3072]{2,1,0:T(1,128)}), f32[32,1,3072]{2,1,0:T(1,128)S(1)}, u32[]{:S(2)}, u32[]{:S(2)}) %all-to-all-start.2) | async-done | bytes 393248 | tf_op jit(solution)/shard_map/all_to_all | solution.py:548
  64.3 0.2 shard_map.112
  64.5 0.1 collective-permute-start.8
  64.6 0.7 %shard_map.113 = (bf16[672,128]{1,0:T(8,128)(2,1)S(1)}, bf16[672,128]{1,0:T(8,128)(2,1)S(1)}) custom-call(f32[32,1,3072]{2,1,0:T(1,128)S(1)} %all-to-all-done.2.in_ref, f32[6,112,112]{2,1,0:T(8,128)S(1)} %get-tuple-element.84.after_ref, f32[11,112]{1,0:T(8,128)S(1)} %copy-done.12, f32[2,8,128]{2,1,0:T(8,128)S(1)} %get-tuple-element.81.m_ref, ...), custom_call_target="tpu_custom_call" | custom-call | flops 10000000 | bytes 2427712 | tf_op jit(solution)/shard_map/pallas_call | solution.py:516
  65.3 0.9 %collective-permute-done.8.got_ref = f32[680,128]{1,0:T(8,128)S(1)} collective-permute-done((f32[680,128]{1,0:T(8,128)S(1)}, f32[680,128]{1,0:T(8,128)S(1)}, u32[]{:S(2)}, u32[]{:S(2)}) %collective-permute-start.8) | collective-permute-done | bytes 348192 | tf_op jit(solution)/shard_map/ppermute | solution.py:137
  66.2 1.2 %shard_map.114 = (bf16[1232,128]{1,0:T(8,128)(2,1)}, bf16[1232,128]{1,0:T(8,128)(2,1)}) custom-call(f32[680,128]{1,0:T(8,128)S(1)} %collective-permute-done.8.got_ref, bf16[1232,128]{1,0:T(8,128)(2,1)S(1)} %bitcast.10, bf16[1232,128]{1,0:T(8,128)(2,1)S(1)} %bitcast.14, f32[672,128]{1,0:T(8,128)S(1)} %collective-permute-done.6.key_in_ref, ...), custom_call_target="tpu_custom_call" | custom-call | flops 10000000 | bytes 2641920 | tf_op jit(solution)/shard_map/pallas_call | solution.py:516
  (19 shorter events, 0.1 us)
Async XLA Ops:
  0.6 1.0 %copy-start = (bf16[128,1232]{0,1:T(8,128)(2,1)S(1)}, bf16[128,1232]{0,1:T(8,128)(2,1)}, u32[]{:S(2)}) copy-start(bf16[128,1232]{0,1:T(8,128)(2,1)} %param.9) | copy-start | bytes 946180
  1.6 1.0 %copy-start.2 = (bf16[128,1232]{0,1:T(8,128)(2,1)S(1)}, bf16[128,1232]{0,1:T(8,128)(2,1)}, u32[]{:S(2)}) copy-start(bf16[128,1232]{0,1:T(8,128)(2,1)} %param.10) | copy-start | bytes 946180
  3.1 1.8 %collective-permute-start = (f32[680,128]{1,0:T(8,128)S(1)}, f32[680,128]{1,0:T(8,128)S(1)}, u32[]{:S(2)}, u32[]{:S(2)}) collective-permute-start(f32[680,128]{1,0:T(8,128)S(1)} %get-tuple-element.48), channel_id=1, source_target_pairs={{0,1},{1,0},{2,3},{3,2},{4,5},{5,4},{6,7},{7,6},{8,9},{9,8},{10,11... | collective-permute-start | bytes 1044488 | tf_op jit(solution)/shard_map/ppermute | solution.py:137
  5.9 7.2 %copy-start.4 = (bf16[128,1232]{0,1:T(8,128)(2,1)S(1)}, bf16[128,1232]{0,1:T(8,128)(2,1)}, u32[]{:S(2)}) copy-start(bf16[128,1232]{0,1:T(8,128)(2,1)} %param.8) | copy-start | bytes 946180
  5.9 20.5 %all-to-all-start = ((f32[32,1,3072]{2,1,0:T(1,128)}), f32[32,1,3072]{2,1,0:T(1,128)S(1)}, u32[]{:S(2)}, u32[]{:S(2)}) async-start(f32[32,1,3072]{2,1,0:T(1,128)} %shard_map.104), calls=%async_computation | async-start | bytes 786432 | tf_op jit(solution)/shard_map/all_to_all | solution.py:548
  13.1 1.0 %copy-start.1 = (bf16[128,1232]{0,1:T(8,128)(2,1)S(1)}, bf16[128,1232]{0,1:T(8,128)(2,1)}, u32[]{:S(2)}) copy-start(bf16[128,1232]{0,1:T(8,128)(2,1)} %param.9) | copy-start | bytes 946180
  14.1 1.0 %copy-start.3 = (bf16[128,1232]{0,1:T(8,128)(2,1)S(1)}, bf16[128,1232]{0,1:T(8,128)(2,1)}, u32[]{:S(2)}) copy-start(bf16[128,1232]{0,1:T(8,128)(2,1)} %param.10) | copy-start | bytes 946180
  15.0 1.0 %copy-start.5 = (bf16[128,1232]{0,1:T(8,128)(2,1)S(1)}, bf16[128,1232]{0,1:T(8,128)(2,1)}, u32[]{:S(2)}) copy-start(bf16[128,1232]{0,1:T(8,128)(2,1)} %param.11) | copy-start | bytes 946180
  16.0 3.8 %copy-start.8 = (f32[11,112,112]{2,1,0:T(8,128)S(1)}, f32[11,112,112]{2,1,0:T(8,128)}, u32[]{:S(2)}) copy-start(f32[11,112,112]{2,1,0:T(8,128)} %state_in_ref.1) | copy-start | bytes 1655812
  16.0 1.7 %collective-permute-start.4 = (f32[672,128]{1,0:T(8,128)S(1)}, f32[672,128]{1,0:T(8,128)S(1)}, u32[]{:S(2)}, u32[]{:S(2)}) collective-permute-start(f32[672,128]{1,0:T(8,128)S(1)} %dynamic-slice_convert_fusion), channel_id=1, source_target_pairs={{0,1},{1,0},{2,3},{3,2},{4,5},{5,4},{6,7},{7,6},{8,9},{9,8},{10,11... | collective-permute-start | bytes 1032200 | tf_op jit(solution)/shard_map/ppermute | solution.py:137
  16.3 1.9 %collective-permute-start.3 = (f32[672,128]{1,0:T(8,128)S(1)}, f32[672,128]{1,0:T(8,128)S(1)}, u32[]{:S(2)}, u32[]{:S(2)}) collective-permute-start(f32[672,128]{1,0:T(8,128)S(1)} %dynamic-slice_convert_fusion.1), channel_id=1, source_target_pairs={{0,1},{1,0},{2,3},{3,2},{4,5},{5,4},{6,7},{7,6},{8,9},{9,8},{10,11... | collective-permute-start | bytes 1032200 | tf_op jit(solution)/shard_map/ppermute | solution.py:137
  16.6 2.1 %collective-permute-start.2 = (f32[672,128]{1,0:T(8,128)S(1)}, f32[672,128]{1,0:T(8,128)S(1)}, u32[]{:S(2)}, u32[]{:S(2)}) collective-permute-start(f32[672,128]{1,0:T(8,128)S(1)} %dynamic-slice_convert_fusion.2), channel_id=1, source_target_pairs={{0,1},{1,0},{2,3},{3,2},{4,5},{5,4},{6,7},{7,6},{8,9},{9,8},{10,11... | collective-permute-start | bytes 1032200 | tf_op jit(solution)/shard_map/ppermute | solution.py:137
  16.9 2.4 %collective-permute-start.1 = (f32[672,128]{1,0:T(8,128)S(1)}, f32[672,128]{1,0:T(8,128)S(1)}, u32[]{:S(2)}, u32[]{:S(2)}) collective-permute-start(f32[672,128]{1,0:T(8,128)S(1)} %dynamic-slice_convert_fusion.3), channel_id=1, source_target_pairs={{0,1},{1,0},{2,3},{3,2},{4,5},{5,4},{6,7},{7,6},{8,9},{9,8},{10,11... | collective-permute-start | bytes 1032200 | tf_op jit(solution)/shard_map/ppermute | solution.py:137
  19.8 6.5 %copy-start.13 = (f32[11,112]{1,0:T(8,128)S(1)}, f32[11,112]{1,0:T(8,128)}, u32[]{:S(2)}) copy-start(f32[11,112]{1,0:T(8,128)} %norm_in_ref.1) | copy-start | bytes 14788
  21.1 0.9 %copy-start.6 = (f32[2,6,112,112]{3,2,1,0:T(8,128)}, f32[2,6,112,112]{3,2,1,0:T(8,128)S(1)}, u32[]{:S(2)}) copy-start(f32[2,6,112,112]{3,2,1,0:T(8,128)S(1)} %get-tuple-element.64.before_ref) | copy-start | bytes 1806340
  26.9 19.5 %copy-start.7 = (f32[2,6,112,112]{3,2,1,0:T(8,128)S(1)}, f32[2,6,112,112]{3,2,1,0:T(8,128)}, u32[]{:S(2)}) copy-start(f32[2,6,112,112]{3,2,1,0:T(8,128)} %copy-done.6) | copy-start | bytes 1806340
  47.8 16.5 %all-to-all-start.2 = ((f32[32,1,3072]{2,1,0:T(1,128)}), f32[32,1,3072]{2,1,0:T(1,128)S(1)}, u32[]{:S(2)}, u32[]{:S(2)}) async-start(f32[32,1,3072]{2,1,0:T(1,128)} %get-tuple-element.67), calls=%async_computation.2 | async-start | bytes 786432 | tf_op jit(solution)/shard_map/all_to_all | solution.py:548
  51.1 1.7 %copy-start.9 = (f32[11,112,112]{2,1,0:T(8,128)S(1)}, f32[11,112,112]{2,1,0:T(8,128)}, u32[]{:S(2)}) copy-start(f32[11,112,112]{2,1,0:T(8,128)} %grad_state_ref.1) | copy-start | bytes 1655812
  52.5 2.5 %collective-permute-start.5 = (f32[672,128]{1,0:T(8,128)S(1)}, f32[672,128]{1,0:T(8,128)S(1)}, u32[]{:S(2)}, u32[]{:S(2)}) collective-permute-start(f32[672,128]{1,0:T(8,128)S(1)} %get-tuple-element.72), channel_id=1, source_target_pairs={{0,1},{1,0},{2,3},{3,2},{4,5},{5,4},{6,7},{7,6},{8,9},{9,8},{10,11... | collective-permute-start | bytes 1032200 | tf_op jit(solution)/shard_map/ppermute | solution.py:137
  54.4 1.7 %collective-permute-start.6 = (f32[672,128]{1,0:T(8,128)S(1)}, f32[672,128]{1,0:T(8,128)S(1)}, u32[]{:S(2)}, u32[]{:S(2)}) collective-permute-start(f32[672,128]{1,0:T(8,128)S(1)} %get-tuple-element.76), channel_id=1, source_target_pairs={{0,1},{1,0},{2,3},{3,2},{4,5},{5,4},{6,7},{7,6},{8,9},{9,8},{10,11... | collective-permute-start | bytes 1032200 | tf_op jit(solution)/shard_map/ppermute | solution.py:137
  54.7 1.9 %collective-permute-start.7 = (f32[672,128]{1,0:T(8,128)S(1)}, f32[672,128]{1,0:T(8,128)S(1)}, u32[]{:S(2)}, u32[]{:S(2)}) collective-permute-start(f32[672,128]{1,0:T(8,128)S(1)} %get-tuple-element.77), channel_id=1, source_target_pairs={{0,1},{1,0},{2,3},{3,2},{4,5},{5,4},{6,7},{7,6},{8,9},{9,8},{10,11... | collective-permute-start | bytes 1032200 | tf_op jit(solution)/shard_map/ppermute | solution.py:137
  55.0 9.3 %copy-start.12 = (f32[11,112]{1,0:T(8,128)S(1)}, f32[11,112]{1,0:T(8,128)}, u32[]{:S(2)}) copy-start(f32[11,112]{1,0:T(8,128)} %grad_norm_ref.3) | copy-start | bytes 14788
  56.6 0.7 %copy-start.10 = (f32[672,128]{1,0:T(8,128)}, f32[672,128]{1,0:T(8,128)S(1)}, u32[]{:S(2)}) copy-start(f32[672,128]{1,0:T(8,128)S(1)} %collective-permute-done.7.value_in_ref) | copy-start | bytes 1032196
  64.5 1.7 %collective-permute-start.8 = (f32[680,128]{1,0:T(8,128)S(1)}, f32[680,128]{1,0:T(8,128)S(1)}, u32[]{:S(2)}, u32[]{:S(2)}) collective-permute-start(f32[680,128]{1,0:T(8,128)S(1)} %shard_map.112), channel_id=1, source_target_pairs={{0,1},{1,0},{2,3},{3,2},{4,5},{5,4},{6,7},{7,6},{8,9},{9,8},{10,11... | collective-permute-start | bytes 1044488 | tf_op jit(solution)/shard_map/ppermute | solution.py:137
  64.6 1.6 %copy-start.11 = (f32[672,128]{1,0:T(8,128)S(1)}, f32[672,128]{1,0:T(8,128)}, u32[]{:S(2)}) copy-start(f32[672,128]{1,0:T(8,128)} %copy-done.10) | copy-start | bytes 1032196

commit v7 on v6

--- a/solution.py
+++ b/solution.py
@@ -271,15 +271,17 @@
     return jnp.maximum(x, 0)
 
 
-def block_states(plan, k_ref, v_ref, send_ref, own_ref):
+def block_state(plan, other, kv_ref, out_ref):
     core = my_core()
+    side = 1 - core if other else core
+    size = plan.heads * plan.width
+    k_ref, v_ref = kv_ref.at[:size, :], kv_ref.at[size:, :]
     ones = jnp.ones((SUB, plan.length), BF16)
-    for side, out_ref in ((1 - core, send_ref), (core, own_ref)):
-        out_ref[plan.rows :, :] = jnp.zeros((plan.extra, LANES), F32)
-        for h in range(plan.half):
-            b, v = relu(plan.own(k_ref, side, h)), plan.own(v_ref, side, h)
-            out_ref[h * plan.width : (h + 1) * plan.width, :] = wide(nt(b, v))
-            out_ref[plan.rows + h : plan.rows + h + 1, :] = wide(nt(ones, b))[0:1]
+    out_ref[plan.rows :, :] = jnp.zeros((plan.extra, LANES), F32)
+    for h in range(plan.half):
+        b, v = relu(plan.own(k_ref, side, h)), plan.own(v_ref, side, h)
+        out_ref[h * plan.width : (h + 1) * plan.width, :] = wide(nt(b, v))
+        out_ref[plan.rows + h : plan.rows + h + 1, :] = wide(nt(ones, b))[0:1]
 
 
 def chip_state(plan, own_ref, got_ref, out_ref):
@@ -562,8 +564,10 @@
     sent_single = shape((devices, 1, plan.single))
     sent_double = shape((devices, 1, plan.double))
 
-    send, block_own = call(bind(block_states), (block, block), (k, v))
+    keys_values = jnp.concatenate([k, v], axis=0)
+    (send,) = call(functools.partial(block_state, plan, True), (block,), (keys_values,))
     block_got = pair_swap(send)
+    (block_own,) = call(functools.partial(block_state, plan, False), (block,), (keys_values,))
     (sent,) = call(bind(chip_state), (sent_single,), (block_own, block_got))
     sent, k, v, q, g = lax.optimization_barrier((sent, k, v, q, g))
     got = exchange(sent)

time: 67.9 us -> 66.8 us (0.984)
  local copies, waits for them, and re-layouts: 6.36 us -> 2.55 us
  waiting for transfers between devices: 16.5 us -> 18 us
  other arithmetic: 0.11 us -> 1.22 us
    unnamed x28 -> x24, local copies, waits for them, and re-layouts: 6.36 us -> 2.55 us
    all_to_all x2, waiting for transfers between devices: 11.3 us -> 13.2 us  [exchange(): return lax.all_to_all(x, both, 0, 0, tiled=True)]
    concatenate x0 -> x1, other arithmetic: none -> 1.11 us  [per_device(): keys_values = jnp.concatenate([k, v], axis=0)]
    pallas_call x12 -> x13, Pallas kernels: 11.2 us -> 11.3 us  [call(): pl.pallas_call(body, out_shape=outs, in_specs=in_specs, out_specs=[vmem]...]
  transfers between devices with their start and end apart: 11 -> 11, of which waited for: 10 -> 10; matrix products, arithmetic and copies ran while one was open for 0% -> 0% of each run, Pallas kernels for 9% -> 10%
where the time goes in v7:
time: 66.8 us; the launch traced here: 66.5 us
  blocking collectives  19.4 us (29%)
  waiting for transfers between devices  18 us (27%)
  starting transfers between devices  13.1 us (20%)
  Pallas kernels  11.3 us (17%)
  local copies, waits for them, and re-layouts  2.55 us (4%)
  other arithmetic  1.22 us (2%)
  between operations  0.84 us (1%)
    all_to_all x1, blocking collectives, exchange(): return lax.all_to_all(x, both, 0, 0, tiled=True)  19.4 us
    all_to_all x2, waiting for transfers between devices, exchange(): return lax.all_to_all(x, both, 0, 0, tiled=True)  13.2 us
    pallas_call x13, Pallas kernels, call(): pl.pallas_call(body, out_shape=outs, in_specs=in_specs, out_specs=[vmem]...  11.3 us
    all_to_all x2, starting transfers between devices, exchange(): return lax.all_to_all(x, both, 0, 0, tiled=True)  10.5 us
    ppermute x9, waiting for transfers between devices, pair_swap(): return lax.ppermute(x, 'seq', [(i, i ^ 1) for i in range(size)])  4.88 us
    ppermute x9, starting transfers between devices, pair_swap(): return lax.ppermute(x, 'seq', [(i, i ^ 1) for i in range(size)])  2.61 us
    unnamed x24, local copies, waits for them, and re-layouts  2.55 us
  transfers between devices with their start and end apart: 11, of which 10 were waited for; matrix products, arithmetic and copies ran while one was open for 0% of the time, Pallas kernels for 10%

profile of v7, /device:TPU:0, one launch (start us, length us, event | category | flops | bytes accessed | tf_op | source)
XLA Modules:
  0.0 66.5 jit_solution(8202615212323030556)
XLA Ops:
  0.6 1.1 %pad_maximum_fusion.kv_ref = bf16[2464,128]{1,0:T(8,128)(2,1)S(1)} fusion(bf16[1232,128]{1,0:T(8,128)(2,1)} %bitcast.11, bf16[1232,128]{1,0:T(8,128)(2,1)} %bitcast.7), kind=kLoop, calls=%fused_computation | loop fusion | flops 1261568 | bytes 1261568 | tf_op jit(solution)/shard_map/concatenate | solution.py:567
  1.7 0.3 shard_map.104
  2.1 0.6 collective-permute-start
  2.6 0.3 shard_map.103.own_ref
  3.0 0.0 copy-start.2
  3.0 0.9 %collective-permute-done.got_ref = f32[680,128]{1,0:T(8,128)S(1)} collective-permute-done((f32[680,128]{1,0:T(8,128)S(1)}, f32[680,128]{1,0:T(8,128)S(1)}, u32[]{:S(2)}, u32[]{:S(2)}) %collective-permute-start) | collective-permute-done | bytes 348192 | tf_op jit(solution)/shard_map/ppermute | solution.py:137
  3.9 0.9 %shard_map.105 = f32[32,1,3072]{2,1,0:T(1,128)} custom-call(f32[680,128]{1,0:T(8,128)S(1)} %shard_map.103.own_ref, f32[680,128]{1,0:T(8,128)S(1)} %collective-permute-done.got_ref), custom_call_target="tpu_custom_call" | custom-call | flops 10000000 | bytes 1089536 | tf_op jit(solution)/shard_map/pallas_call | solution.py:518
  4.9 7.2 %all-to-all-start = ((f32[32,1,3072]{2,1,0:T(1,128)}), f32[32,1,3072]{2,1,0:T(1,128)S(1)}, u32[]{:S(2)}, u32[]{:S(2)}) async-start(f32[32,1,3072]{2,1,0:T(1,128)} %shard_map.105), calls=%async_computation | async-start | bytes 786432 | tf_op jit(solution)/shard_map/all_to_all | solution.py:550
  12.1 0.0 copy-start.1
  12.1 0.0 copy-start.3
  12.2 0.9 %copy-done.1 = bf16[128,1232]{0,1:T(8,128)(2,1)S(1)} copy-done((bf16[128,1232]{0,1:T(8,128)(2,1)S(1)}, bf16[128,1232]{0,1:T(8,128)(2,1)}, u32[]{:S(2)}) %copy-start.1) | copy-done | bytes 315416
  13.1 0.1 copy-done.3
  13.2 0.0 copy-start.6
  13.2 0.3 collective-permute-start.4
  13.5 0.3 collective-permute-start.3
  13.8 0.3 collective-permute-start.2
  14.0 0.3 collective-permute-start.1
  14.3 0.6 collective-permute-done.4.g_got_ref
  14.9 0.5 collective-permute-done.3.v_got_ref
  15.4 0.5 collective-permute-done.2.k_got_ref
  15.9 0.5 collective-permute-done.1.q_got_ref
  16.4 0.5 shard_map.106
  16.9 0.0 copy-start.11
  16.9 1.3 %shard_map.107 = (f32[2,6,112,112]{3,2,1,0:T(8,128)S(1)}, f32[2,8,128]{2,1,0:T(8,128)S(1)}) custom-call(bf16[2,6,112,128]{3,2,1,0:T(8,128)(2,1)S(1)} %get-tuple-element.50.a_ref, bf16[2,6,112,128]{3,2,1,0:T(8,128)(2,1)S(1)} %get-tuple-element.51.b_ref, bf16[2,6,112,128]{3,2,1,0:T(8,128)(2,1)S(1)} %get-tuple-element.52.v_ref, ...), custom_call_target="tpu_custom_call" | custom-call | flops 10000000 | bytes 2538496 | tf_op jit(solution)/shard_map/pallas_call | solution.py:518
  18.3 0.8 %copy-done.4 = f32[2,6,112,112]{3,2,1,0:T(8,128)} copy-done((f32[2,6,112,112]{3,2,1,0:T(8,128)}, f32[2,6,112,112]{3,2,1,0:T(8,128)S(1)}, u32[]{:S(2)}) %copy-start.4) | copy-done | bytes 602136
  19.1 6.2 %all-to-all-done.in_ref = f32[32,1,3072]{2,1,0:T(1,128)S(1)} async-done(((f32[32,1,3072]{2,1,0:T(1,128)}), f32[32,1,3072]{2,1,0:T(1,128)S(1)}, u32[]{:S(2)}, u32[]{:S(2)}) %all-to-all-start) | async-done | bytes 393248 | tf_op jit(solution)/shard_map/all_to_all | solution.py:550
  25.3 0.6 shard_map.108
  25.9 19.4 %all_to_all.15.in_ref = f32[32,1,4736]{2,1,0:T(1,128)S(1)} all-to-all(f32[32,1,4736]{2,1,0:T(1,128)S(1)} %get-tuple-element.59), channel_id=1, replica_groups=mesh['grp'=4,'seq'=8] {'grp','seq'}, dimensions={0} | all-to-all | bytes 1212416 | tf_op jit(solution)/shard_map/all_to_all | solution.py:550
  45.4 1.5 %shard_map.109 = (f32[32,1,3072]{2,1,0:T(1,128)}, f32[2,6,112,128]{3,2,1,0:T(8,128)S(1)}, f32[2,8,128]{2,1,0:T(8,128)S(1)}, f32[2,8,128]{2,1,0:T(8,128)S(1)}) custom-call(f32[32,1,4736]{2,1,0:T(1,128)S(1)} %all_to_all.15.in_ref, f32[2,6,112,112]{3,2,1,0:T(8,128)S(1)} %copy-done.5, bf16[2,6,112,128]{3,2,1,0:T(8,128)(2,1)S(1)} %get-tuple-element.50.a_ref, ...), custom_call_target="tpu_custom_call" | custom-call | flops 10000000 | bytes 3010560 | tf_op jit(solution)/shard_map/pallas_call | solution.py:518
  46.8 3.2 %all-to-all-start.2 = ((f32[32,1,3072]{2,1,0:T(1,128)}), f32[32,1,3072]{2,1,0:T(1,128)S(1)}, u32[]{:S(2)}, u32[]{:S(2)}) async-start(f32[32,1,3072]{2,1,0:T(1,128)} %get-tuple-element.63), calls=%async_computation.2 | async-start | bytes 786432 | tf_op jit(solution)/shard_map/all_to_all | solution.py:550
  50.1 0.0 copy-start.7
  50.1 1.4 %shard_map.110 = (f32[672,128]{1,0:T(8,128)S(1)}, f32[672,128]{1,0:T(8,128)S(1)}, bf16[2,6,128,128]{3,2,1,0:T(8,128)(2,1)S(1)}, bf16[2,6,112,128]{3,2,1,0:T(8,128)(2,1)S(1)}, bf16[2,6,112,128]{3,2,1,0:T(8,128)(2,1)S(1)}) custom-call(bf16[2,6,112,128]{3,2,1,0:T(8,128)(2,1)S(1)} %get-tuple-element.50.a_ref, ...), custom_call_target="tpu_custom_call" | custom-call | flops 10000000 | bytes 3858432 | tf_op jit(solution)/shard_map/pallas_call | solution.py:518
  51.5 0.3 collective-permute-start.5
  51.8 1.6 %shard_map.112 = (f32[6,112,112]{2,1,0:T(8,128)S(1)}, f32[672,128]{1,0:T(8,128)S(1)}, f32[672,128]{1,0:T(8,128)S(1)}, f32[6,112,112]{2,1,0:T(8,128)S(1)}, f32[67...) custom-call(bf16[2,6,112,128]{3,2,1,0:T(8,128)(2,1)S(1)} %get-tuple-element.69.a_ref, ...), custom_call_target="tpu_custom_call" | custom-call | flops 10000000 | bytes 3955712 | tf_op jit(solution)/shard_map/pallas_call | solution.py:518
  53.4 0.0 copy-start.10
  53.4 0.3 collective-permute-start.6
  53.8 0.2 collective-permute-start.7
  54.0 0.0 collective-permute-done.5.refs_1_
  54.0 0.8 %shard_map.111 = bf16[1232,128]{1,0:T(8,128)(2,1)} custom-call(f32[672,128]{1,0:T(8,128)S(1)} %get-tuple-element.67.refs_0_, f32[672,128]{1,0:T(8,128)S(1)} %collective-permute-done.5.refs_1_), custom_call_target="tpu_custom_call" | custom-call | flops 10000000 | bytes 1003520 | tf_op jit(solution)/shard_map/pallas_call | solution.py:518
  54.8 0.4 collective-permute-done.6.key_in_ref
  55.2 0.5 collective-permute-done.7.value_in_ref
  55.6 0.7 %copy-done.8 = f32[672,128]{1,0:T(8,128)} copy-done((f32[672,128]{1,0:T(8,128)}, f32[672,128]{1,0:T(8,128)S(1)}, u32[]{:S(2)}) %copy-start.8) | copy-done | bytes 344088
  56.4 7.0 %all-to-all-done.2.in_ref = f32[32,1,3072]{2,1,0:T(1,128)S(1)} async-done(((f32[32,1,3072]{2,1,0:T(1,128)}), f32[32,1,3072]{2,1,0:T(1,128)S(1)}, u32[]{:S(2)}, u32[]{:S(2)}) %all-to-all-start.2) | async-done | bytes 393248 | tf_op jit(solution)/shard_map/all_to_all | solution.py:550
  63.3 0.2 shard_map.113
  63.5 0.1 collective-permute-start.8
  63.6 0.7 %shard_map.114 = (bf16[672,128]{1,0:T(8,128)(2,1)S(1)}, bf16[672,128]{1,0:T(8,128)(2,1)S(1)}) custom-call(f32[32,1,3072]{2,1,0:T(1,128)S(1)} %all-to-all-done.2.in_ref, f32[6,112,112]{2,1,0:T(8,128)S(1)} %get-tuple-element.80.after_ref, f32[11,112]{1,0:T(8,128)S(1)} %copy-done.10, f32[2,8,128]{2,1,0:T(8,128)S(1)} %get-tuple-element.77.m_ref, ...), custom_call_target="tpu_custom_call" | custom-call | flops 10000000 | bytes 2427712 | tf_op jit(solution)/shard_map/pallas_call | solution.py:518
  64.3 0.9 %collective-permute-done.8.got_ref = f32[680,128]{1,0:T(8,128)S(1)} collective-permute-done((f32[680,128]{1,0:T(8,128)S(1)}, f32[680,128]{1,0:T(8,128)S(1)}, u32[]{:S(2)}, u32[]{:S(2)}) %collective-permute-start.8) | collective-permute-done | bytes 348192 | tf_op jit(solution)/shard_map/ppermute | solution.py:137
  65.2 1.2 %shard_map.115 = (bf16[1232,128]{1,0:T(8,128)(2,1)}, bf16[1232,128]{1,0:T(8,128)(2,1)}) custom-call(f32[680,128]{1,0:T(8,128)S(1)} %collective-permute-done.8.got_ref, bf16[1232,128]{1,0:T(8,128)(2,1)S(1)} %bitcast.10, bf16[1232,128]{1,0:T(8,128)(2,1)S(1)} %bitcast.14, f32[672,128]{1,0:T(8,128)S(1)} %collective-permute-done.6.key_in_ref, ...), custom_call_target="tpu_custom_call" | custom-call | flops 10000000 | bytes 2641920 | tf_op jit(solution)/shard_map/pallas_call | solution.py:518
  (17 shorter events, 0.1 us)
Async XLA Ops:
  2.1 1.8 %collective-permute-start = (f32[680,128]{1,0:T(8,128)S(1)}, f32[680,128]{1,0:T(8,128)S(1)}, u32[]{:S(2)}, u32[]{:S(2)}) collective-permute-start(f32[680,128]{1,0:T(8,128)S(1)} %shard_map.104), channel_id=1, source_target_pairs={{0,1},{1,0},{2,3},{3,2},{4,5},{5,4},{6,7},{7,6},{8,9},{9,8},{10,11... | collective-permute-start | bytes 1044488 | tf_op jit(solution)/shard_map/ppermute | solution.py:137
  3.0 9.1 %copy-start.2 = (bf16[128,1232]{0,1:T(8,128)(2,1)S(1)}, bf16[128,1232]{0,1:T(8,128)(2,1)}, u32[]{:S(2)}) copy-start(bf16[128,1232]{0,1:T(8,128)(2,1)} %param.8) | copy-start | bytes 946180
  4.9 7.3 %copy-start = (bf16[128,1232]{0,1:T(8,128)(2,1)S(1)}, bf16[128,1232]{0,1:T(8,128)(2,1)}, u32[]{:S(2)}) copy-start(bf16[128,1232]{0,1:T(8,128)(2,1)} %param.9) | copy-start | bytes 946180
  4.9 20.5 %all-to-all-start = ((f32[32,1,3072]{2,1,0:T(1,128)}), f32[32,1,3072]{2,1,0:T(1,128)S(1)}, u32[]{:S(2)}, u32[]{:S(2)}) async-start(f32[32,1,3072]{2,1,0:T(1,128)} %shard_map.105), calls=%async_computation | async-start | bytes 786432 | tf_op jit(solution)/shard_map/all_to_all | solution.py:550
  12.1 1.0 %copy-start.1 = (bf16[128,1232]{0,1:T(8,128)(2,1)S(1)}, bf16[128,1232]{0,1:T(8,128)(2,1)}, u32[]{:S(2)}) copy-start(bf16[128,1232]{0,1:T(8,128)(2,1)} %param.10) | copy-start | bytes 946180
  12.1 1.1 %copy-start.3 = (bf16[128,1232]{0,1:T(8,128)(2,1)S(1)}, bf16[128,1232]{0,1:T(8,128)(2,1)}, u32[]{:S(2)}) copy-start(bf16[128,1232]{0,1:T(8,128)(2,1)} %param.11) | copy-start | bytes 946180
  13.2 3.8 %copy-start.6 = (f32[11,112,112]{2,1,0:T(8,128)S(1)}, f32[11,112,112]{2,1,0:T(8,128)}, u32[]{:S(2)}) copy-start(f32[11,112,112]{2,1,0:T(8,128)} %state_in_ref.1) | copy-start | bytes 1655812
  13.2 1.7 %collective-permute-start.4 = (f32[672,128]{1,0:T(8,128)S(1)}, f32[672,128]{1,0:T(8,128)S(1)}, u32[]{:S(2)}, u32[]{:S(2)}) collective-permute-start(f32[672,128]{1,0:T(8,128)S(1)} %dynamic-slice_convert_fusion), channel_id=1, source_target_pairs={{0,1},{1,0},{2,3},{3,2},{4,5},{5,4},{6,7},{7,6},{8,9},{9,8},{10,11... | collective-permute-start | bytes 1032200 | tf_op jit(solution)/shard_map/ppermute | solution.py:137
  13.5 1.9 %collective-permute-start.3 = (f32[672,128]{1,0:T(8,128)S(1)}, f32[672,128]{1,0:T(8,128)S(1)}, u32[]{:S(2)}, u32[]{:S(2)}) collective-permute-start(f32[672,128]{1,0:T(8,128)S(1)} %dynamic-slice_convert_fusion.1), channel_id=1, source_target_pairs={{0,1},{1,0},{2,3},{3,2},{4,5},{5,4},{6,7},{7,6},{8,9},{9,8},{10,11... | collective-permute-start | bytes 1032200 | tf_op jit(solution)/shard_map/ppermute | solution.py:137
  13.8 2.1 %collective-permute-start.2 = (f32[672,128]{1,0:T(8,128)S(1)}, f32[672,128]{1,0:T(8,128)S(1)}, u32[]{:S(2)}, u32[]{:S(2)}) collective-permute-start(f32[672,128]{1,0:T(8,128)S(1)} %dynamic-slice_convert_fusion.2), channel_id=1, source_target_pairs={{0,1},{1,0},{2,3},{3,2},{4,5},{5,4},{6,7},{7,6},{8,9},{9,8},{10,11... | collective-permute-start | bytes 1032200 | tf_op jit(solution)/shard_map/ppermute | solution.py:137
  14.0 2.4 %collective-permute-start.1 = (f32[672,128]{1,0:T(8,128)S(1)}, f32[672,128]{1,0:T(8,128)S(1)}, u32[]{:S(2)}, u32[]{:S(2)}) collective-permute-start(f32[672,128]{1,0:T(8,128)S(1)} %dynamic-slice_convert_fusion.3), channel_id=1, source_target_pairs={{0,1},{1,0},{2,3},{3,2},{4,5},{5,4},{6,7},{7,6},{8,9},{9,8},{10,11... | collective-permute-start | bytes 1032200 | tf_op jit(solution)/shard_map/ppermute | solution.py:137
  16.9 8.4 %copy-start.11 = (f32[11,112]{1,0:T(8,128)S(1)}, f32[11,112]{1,0:T(8,128)}, u32[]{:S(2)}) copy-start(f32[11,112]{1,0:T(8,128)} %norm_in_ref.1) | copy-start | bytes 14788
  18.3 0.8 %copy-start.4 = (f32[2,6,112,112]{3,2,1,0:T(8,128)}, f32[2,6,112,112]{3,2,1,0:T(8,128)S(1)}, u32[]{:S(2)}) copy-start(f32[2,6,112,112]{3,2,1,0:T(8,128)S(1)} %get-tuple-element.60.before_ref) | copy-start | bytes 1806340
  25.9 19.5 %copy-start.5 = (f32[2,6,112,112]{3,2,1,0:T(8,128)S(1)}, f32[2,6,112,112]{3,2,1,0:T(8,128)}, u32[]{:S(2)}) copy-start(f32[2,6,112,112]{3,2,1,0:T(8,128)} %copy-done.4) | copy-start | bytes 1806340
  46.8 16.5 %all-to-all-start.2 = ((f32[32,1,3072]{2,1,0:T(1,128)}), f32[32,1,3072]{2,1,0:T(1,128)S(1)}, u32[]{:S(2)}, u32[]{:S(2)}) async-start(f32[32,1,3072]{2,1,0:T(1,128)} %get-tuple-element.63), calls=%async_computation.2 | async-start | bytes 786432 | tf_op jit(solution)/shard_map/all_to_all | solution.py:550
  50.1 1.7 %copy-start.7 = (f32[11,112,112]{2,1,0:T(8,128)S(1)}, f32[11,112,112]{2,1,0:T(8,128)}, u32[]{:S(2)}) copy-start(f32[11,112,112]{2,1,0:T(8,128)} %grad_state_ref.1) | copy-start | bytes 1655812
  51.5 2.5 %collective-permute-start.5 = (f32[672,128]{1,0:T(8,128)S(1)}, f32[672,128]{1,0:T(8,128)S(1)}, u32[]{:S(2)}, u32[]{:S(2)}) collective-permute-start(f32[672,128]{1,0:T(8,128)S(1)} %get-tuple-element.68), channel_id=1, source_target_pairs={{0,1},{1,0},{2,3},{3,2},{4,5},{5,4},{6,7},{7,6},{8,9},{9,8},{10,11... | collective-permute-start | bytes 1032200 | tf_op jit(solution)/shard_map/ppermute | solution.py:137
  53.4 9.9 %copy-start.10 = (f32[11,112]{1,0:T(8,128)S(1)}, f32[11,112]{1,0:T(8,128)}, u32[]{:S(2)}) copy-start(f32[11,112]{1,0:T(8,128)} %grad_norm_ref.3) | copy-start | bytes 14788
  53.4 1.7 %collective-permute-start.6 = (f32[672,128]{1,0:T(8,128)S(1)}, f32[672,128]{1,0:T(8,128)S(1)}, u32[]{:S(2)}, u32[]{:S(2)}) collective-permute-start(f32[672,128]{1,0:T(8,128)S(1)} %get-tuple-element.72), channel_id=1, source_target_pairs={{0,1},{1,0},{2,3},{3,2},{4,5},{5,4},{6,7},{7,6},{8,9},{9,8},{10,11... | collective-permute-start | bytes 1032200 | tf_op jit(solution)/shard_map/ppermute | solution.py:137
  53.8 1.9 %collective-permute-start.7 = (f32[672,128]{1,0:T(8,128)S(1)}, f32[672,128]{1,0:T(8,128)S(1)}, u32[]{:S(2)}, u32[]{:S(2)}) collective-permute-start(f32[672,128]{1,0:T(8,128)S(1)} %get-tuple-element.73), channel_id=1, source_target_pairs={{0,1},{1,0},{2,3},{3,2},{4,5},{5,4},{6,7},{7,6},{8,9},{9,8},{10,11... | collective-permute-start | bytes 1032200 | tf_op jit(solution)/shard_map/ppermute | solution.py:137
  55.6 0.7 %copy-start.8 = (f32[672,128]{1,0:T(8,128)}, f32[672,128]{1,0:T(8,128)S(1)}, u32[]{:S(2)}) copy-start(f32[672,128]{1,0:T(8,128)S(1)} %collective-permute-done.7.value_in_ref) | copy-start | bytes 1032196
  63.5 1.7 %collective-permute-start.8 = (f32[680,128]{1,0:T(8,128)S(1)}, f32[680,128]{1,0:T(8,128)S(1)}, u32[]{:S(2)}, u32[]{:S(2)}) collective-permute-start(f32[680,128]{1,0:T(8,128)S(1)} %shard_map.113), channel_id=1, source_target_pairs={{0,1},{1,0},{2,3},{3,2},{4,5},{5,4},{6,7},{7,6},{8,9},{9,8},{10,11... | collective-permute-start | bytes 1044488 | tf_op jit(solution)/shard_map/ppermute | solution.py:137
  63.6 1.6 %copy-start.9 = (f32[672,128]{1,0:T(8,128)S(1)}, f32[672,128]{1,0:T(8,128)}, u32[]{:S(2)}) copy-start(f32[672,128]{1,0:T(8,128)} %copy-done.8) | copy-start | bytes 1032196

commit v8 on v7

--- a/solution.py
+++ b/solution.py
@@ -58,7 +58,8 @@
 
 
 class Plan:
-    def __init__(self, devices, length, heads, width):
+    def __init__(self, groups, members, length, heads, width):
+        self.groups, self.members, devices = groups, members, groups * members
         self.devices, self.length, self.heads, self.width = devices, length, heads, width
         self.half = -(-heads // 2)
         self.shift = heads - self.half
@@ -116,6 +117,14 @@
         full = self.full
         return Area(0, full, 0), Area(full + 1, full, HALF), Area(1, 0, HALF)
 
+    def row(self, chip, core):
+        first, members = 2 * chip, self.members
+        if isinstance(chip, int):
+            group, member = divmod(first, members)
+        else:
+            group, member = lax.div(first, members), lax.rem(first, members)
+        return (member + core) * self.groups + group
+
     def own(self, ref, core, head):
         start = pl.multiple_of(core * (self.shift * self.width) + head * self.width, 16)
         return ref[pl.ds(start, self.width), :]
@@ -218,7 +227,7 @@
         chip = chips - 1 - i if later else i
         grown = []
         for core in range(2):
-            row = 2 * chip + core
+            row = plan.row(chip, core)
             out_ref[row, :, : plan.span] = sums[core]
             grown.append(sums[core] + in_ref[row, :, columns])
         return tuple(grown)
@@ -235,7 +244,7 @@
 
     def step(i, totals):
         take = (i > chip) if later else (i < chip)
-        row = 2 * i + core
+        row = plan.row(i, core)
         return (
             totals[0] + jnp.where(take, in_ref[row, :, columns], 0.0),
             totals[1] + jnp.where(take, in_ref[row, :, extras], 0.0),
@@ -533,11 +542,11 @@
 def per_device(
     queries, key_vectors, value_vectors, output_grad, state_in, norm_in, grad_state, grad_norm
 ):
-    both = ("grp", "seq")
+    both = ("seq", "grp")
     length = queries.shape[0]
     heads, width = norm_in.shape
-    devices = lax.axis_size("grp") * lax.axis_size("seq")
-    plan = Plan(devices, length, heads, width)
+    plan = Plan(lax.axis_size("grp"), lax.axis_size("seq"), length, heads, width)
+    devices = plan.devices
     half = plan.half
     core = my_core()
     key_rows, value_rows = key_vectors.T, value_vectors.T

time: 66.8 us -> 66 us (0.988)
  waiting for transfers between devices: 18 us -> 14.9 us
  starting transfers between devices: 13.1 us -> 15.3 us
    all_to_all x2, waiting for transfers between devices: 13.2 us -> 10.4 us  [exchange(): return lax.all_to_all(x, both, 0, 0, tiled=True)]
    ppermute x9, starting transfers between devices: 2.61 us -> 3.82 us  [pair_swap(): return lax.ppermute(x, 'seq', [(i, i ^ 1) for i in range(size)])]
    all_to_all x2, starting transfers between devices: 10.5 us -> 11.5 us  [exchange(): return lax.all_to_all(x, both, 0, 0, tiled=True)]
where the time goes in v8:
time: 66 us; the launch traced here: 65.6 us
  blocking collectives  19.4 us (29%)
  starting transfers between devices  15.3 us (23%)
  waiting for transfers between devices  14.9 us (23%)
  Pallas kernels  11.3 us (17%)
  local copies, waits for them, and re-layouts  2.55 us (4%)
  other arithmetic  1.22 us (2%)
  between operations  0.82 us (1%)
    all_to_all x1, blocking collectives, exchange(): return lax.all_to_all(x, both, 0, 0, tiled=True)  19.4 us
    all_to_all x2, starting transfers between devices, exchange(): return lax.all_to_all(x, both, 0, 0, tiled=True)  11.5 us
    pallas_call x13, Pallas kernels, call(): pl.pallas_call(body, out_shape=outs, in_specs=in_specs, out_specs=[vmem]...  11.3 us
    all_to_all x2, waiting for transfers between devices, exchange(): return lax.all_to_all(x, both, 0, 0, tiled=True)  10.4 us
    ppermute x9, waiting for transfers between devices, pair_swap(): return lax.ppermute(x, 'seq', [(i, i ^ 1) for i in range(size)])  4.53 us
    ppermute x9, starting transfers between devices, pair_swap(): return lax.ppermute(x, 'seq', [(i, i ^ 1) for i in range(size)])  3.82 us
    unnamed x24, local copies, waits for them, and re-layouts  2.55 us
  transfers between devices with their start and end apart: 11, of which 10 were waited for; matrix products, arithmetic and copies ran while one was open for 0% of the time, Pallas kernels for 10%

profile of v8, /device:TPU:0, one launch (start us, length us, event | category | flops | bytes accessed | tf_op | source)
XLA Modules:
  0.0 65.6 jit_solution(12662301662405315736)
XLA Ops:
  0.6 1.1 %pad_maximum_fusion.kv_ref = bf16[2464,128]{1,0:T(8,128)(2,1)S(1)} fusion(bf16[1232,128]{1,0:T(8,128)(2,1)} %bitcast.11, bf16[1232,128]{1,0:T(8,128)(2,1)} %bitcast.7), kind=kLoop, calls=%fused_computation | loop fusion | flops 1261568 | bytes 1261568 | tf_op jit(solution)/shard_map/concatenate | solution.py:576
  1.7 0.3 shard_map.104
  2.1 0.6 collective-permute-start
  2.6 0.3 shard_map.103.own_ref
  3.0 0.0 copy-start.2
  3.0 0.9 %collective-permute-done.got_ref = f32[680,128]{1,0:T(8,128)S(1)} collective-permute-done((f32[680,128]{1,0:T(8,128)S(1)}, f32[680,128]{1,0:T(8,128)S(1)}, u32[]{:S(2)}, u32[]{:S(2)}) %collective-permute-start) | collective-permute-done | bytes 348192 | tf_op jit(solution)/shard_map/ppermute | solution.py:146
  3.9 0.9 %shard_map.105 = f32[32,1,3072]{2,1,0:T(1,128)} custom-call(f32[680,128]{1,0:T(8,128)S(1)} %shard_map.103.own_ref, f32[680,128]{1,0:T(8,128)S(1)} %collective-permute-done.got_ref), custom_call_target="tpu_custom_call" | custom-call | flops 10000000 | bytes 1089536 | tf_op jit(solution)/shard_map/pallas_call | solution.py:527
  4.9 7.2 %all-to-all-start = ((f32[32,1,3072]{2,1,0:T(1,128)}), f32[32,1,3072]{2,1,0:T(1,128)S(1)}, u32[]{:S(2)}, u32[]{:S(2)}) async-start(f32[32,1,3072]{2,1,0:T(1,128)} %shard_map.105), calls=%async_computation | async-start | bytes 786432 | tf_op jit(solution)/shard_map/all_to_all | solution.py:559
  12.1 0.0 copy-start.1
  12.1 0.0 copy-start.3
  12.2 0.9 %copy-done.1 = bf16[128,1232]{0,1:T(8,128)(2,1)S(1)} copy-done((bf16[128,1232]{0,1:T(8,128)(2,1)S(1)}, bf16[128,1232]{0,1:T(8,128)(2,1)}, u32[]{:S(2)}) %copy-start.1) | copy-done | bytes 315416
  13.1 0.1 copy-done.3
  13.2 0.0 copy-start.6
  13.2 0.3 collective-permute-start.4
  13.5 0.3 collective-permute-start.3
  13.8 0.3 collective-permute-start.2
  14.0 0.3 collective-permute-start.1
  14.3 0.6 collective-permute-done.4.g_got_ref
  14.9 0.5 collective-permute-done.3.v_got_ref
  15.4 0.5 collective-permute-done.2.k_got_ref
  15.9 0.5 collective-permute-done.1.q_got_ref
  16.4 0.5 shard_map.106
  16.9 0.0 copy-start.11
  16.9 1.3 %shard_map.107 = (f32[2,6,112,112]{3,2,1,0:T(8,128)S(1)}, f32[2,8,128]{2,1,0:T(8,128)S(1)}) custom-call(bf16[2,6,112,128]{3,2,1,0:T(8,128)(2,1)S(1)} %get-tuple-element.50.a_ref, bf16[2,6,112,128]{3,2,1,0:T(8,128)(2,1)S(1)} %get-tuple-element.51.b_ref, bf16[2,6,112,128]{3,2,1,0:T(8,128)(2,1)S(1)} %get-tuple-element.52.v_ref, ...), custom_call_target="tpu_custom_call" | custom-call | flops 10000000 | bytes 2538496 | tf_op jit(solution)/shard_map/pallas_call | solution.py:527
  18.3 0.8 %copy-done.4 = f32[2,6,112,112]{3,2,1,0:T(8,128)} copy-done((f32[2,6,112,112]{3,2,1,0:T(8,128)}, f32[2,6,112,112]{3,2,1,0:T(8,128)S(1)}, u32[]{:S(2)}) %copy-start.4) | copy-done | bytes 602136
  19.1 4.8 %all-to-all-done.in_ref = f32[32,1,3072]{2,1,0:T(1,128)S(1)} async-done(((f32[32,1,3072]{2,1,0:T(1,128)}), f32[32,1,3072]{2,1,0:T(1,128)S(1)}, u32[]{:S(2)}, u32[]{:S(2)}) %all-to-all-start) | async-done | bytes 393248 | tf_op jit(solution)/shard_map/all_to_all | solution.py:559
  23.9 0.6 shard_map.108
  24.5 19.4 %all_to_all.15.in_ref = f32[32,1,4736]{2,1,0:T(1,128)S(1)} all-to-all(f32[32,1,4736]{2,1,0:T(1,128)S(1)} %get-tuple-element.59), channel_id=1, replica_groups=mesh['grp'=4,'seq'=8] {'seq','grp'}, dimensions={0} | all-to-all | bytes 1212416 | tf_op jit(solution)/shard_map/all_to_all | solution.py:559
  44.0 1.5 %shard_map.109 = (f32[32,1,3072]{2,1,0:T(1,128)}, f32[2,6,112,128]{3,2,1,0:T(8,128)S(1)}, f32[2,8,128]{2,1,0:T(8,128)S(1)}, f32[2,8,128]{2,1,0:T(8,128)S(1)}) custom-call(f32[32,1,4736]{2,1,0:T(1,128)S(1)} %all_to_all.15.in_ref, f32[2,6,112,112]{3,2,1,0:T(8,128)S(1)} %copy-done.5, bf16[2,6,112,128]{3,2,1,0:T(8,128)(2,1)S(1)} %get-tuple-element.50.a_ref, ...), custom_call_target="tpu_custom_call" | custom-call | flops 10000000 | bytes 3010560 | tf_op jit(solution)/shard_map/pallas_call | solution.py:527
  45.5 4.3 %all-to-all-start.2 = ((f32[32,1,3072]{2,1,0:T(1,128)}), f32[32,1,3072]{2,1,0:T(1,128)S(1)}, u32[]{:S(2)}, u32[]{:S(2)}) async-start(f32[32,1,3072]{2,1,0:T(1,128)} %get-tuple-element.63), calls=%async_computation.2 | async-start | bytes 786432 | tf_op jit(solution)/shard_map/all_to_all | solution.py:559
  49.8 0.0 copy-start.7
  49.8 1.4 %shard_map.110 = (f32[672,128]{1,0:T(8,128)S(1)}, f32[672,128]{1,0:T(8,128)S(1)}, bf16[2,6,128,128]{3,2,1,0:T(8,128)(2,1)S(1)}, bf16[2,6,112,128]{3,2,1,0:T(8,128)(2,1)S(1)}, bf16[2,6,112,128]{3,2,1,0:T(8,128)(2,1)S(1)}) custom-call(bf16[2,6,112,128]{3,2,1,0:T(8,128)(2,1)S(1)} %get-tuple-element.50.a_ref, ...), custom_call_target="tpu_custom_call" | custom-call | flops 10000000 | bytes 3858432 | tf_op jit(solution)/shard_map/pallas_call | solution.py:527
  51.2 0.3 collective-permute-start.5
  51.5 1.6 %shard_map.112 = (f32[6,112,112]{2,1,0:T(8,128)S(1)}, f32[672,128]{1,0:T(8,128)S(1)}, f32[672,128]{1,0:T(8,128)S(1)}, f32[6,112,112]{2,1,0:T(8,128)S(1)}, f32[67...) custom-call(bf16[2,6,112,128]{3,2,1,0:T(8,128)(2,1)S(1)} %get-tuple-element.69.a_ref, ...), custom_call_target="tpu_custom_call" | custom-call | flops 10000000 | bytes 3955712 | tf_op jit(solution)/shard_map/pallas_call | solution.py:527
  53.1 0.0 copy-start.10
  53.1 0.3 collective-permute-start.6
  53.4 0.2 collective-permute-start.7
  53.7 0.0 collective-permute-done.5.refs_1_
  53.7 0.8 %shard_map.111 = bf16[1232,128]{1,0:T(8,128)(2,1)} custom-call(f32[672,128]{1,0:T(8,128)S(1)} %get-tuple-element.67.refs_0_, f32[672,128]{1,0:T(8,128)S(1)} %collective-permute-done.5.refs_1_), custom_call_target="tpu_custom_call" | custom-call | flops 10000000 | bytes 1003520 | tf_op jit(solution)/shard_map/pallas_call | solution.py:527
  54.4 0.4 collective-permute-done.6.key_in_ref
  54.8 0.5 collective-permute-done.7.value_in_ref
  55.3 0.7 %copy-done.8 = f32[672,128]{1,0:T(8,128)} copy-done((f32[672,128]{1,0:T(8,128)}, f32[672,128]{1,0:T(8,128)S(1)}, u32[]{:S(2)}) %copy-start.8) | copy-done | bytes 344088
  56.1 5.6 %all-to-all-done.2.in_ref = f32[32,1,3072]{2,1,0:T(1,128)S(1)} async-done(((f32[32,1,3072]{2,1,0:T(1,128)}), f32[32,1,3072]{2,1,0:T(1,128)S(1)}, u32[]{:S(2)}, u32[]{:S(2)}) %all-to-all-start.2) | async-done | bytes 393248 | tf_op jit(solution)/shard_map/all_to_all | solution.py:559
  61.6 0.2 shard_map.113
  61.8 1.3 %collective-permute-start.8 = (f32[680,128]{1,0:T(8,128)S(1)}, f32[680,128]{1,0:T(8,128)S(1)}, u32[]{:S(2)}, u32[]{:S(2)}) collective-permute-start(f32[680,128]{1,0:T(8,128)S(1)} %shard_map.113), channel_id=1, source_target_pairs={{0,1},{1,0},{2,3},{3,2},{4,5},{5,4},{6,7},{7,6},{8,9},{9,8},{10,11... | collective-permute-start | bytes 1044488 | tf_op jit(solution)/shard_map/ppermute | solution.py:146
  63.1 0.7 %shard_map.114 = (bf16[672,128]{1,0:T(8,128)(2,1)S(1)}, bf16[672,128]{1,0:T(8,128)(2,1)S(1)}) custom-call(f32[32,1,3072]{2,1,0:T(1,128)S(1)} %all-to-all-done.2.in_ref, f32[6,112,112]{2,1,0:T(8,128)S(1)} %get-tuple-element.80.after_ref, f32[11,112]{1,0:T(8,128)S(1)} %copy-done.10, f32[2,8,128]{2,1,0:T(8,128)S(1)} %get-tuple-element.77.m_ref, ...), custom_call_target="tpu_custom_call" | custom-call | flops 10000000 | bytes 2427712 | tf_op jit(solution)/shard_map/pallas_call | solution.py:527
  63.8 0.6 collective-permute-done.8.got_ref
  64.4 1.2 %shard_map.115 = (bf16[1232,128]{1,0:T(8,128)(2,1)}, bf16[1232,128]{1,0:T(8,128)(2,1)}) custom-call(f32[680,128]{1,0:T(8,128)S(1)} %collective-permute-done.8.got_ref, bf16[1232,128]{1,0:T(8,128)(2,1)S(1)} %bitcast.10, bf16[1232,128]{1,0:T(8,128)(2,1)S(1)} %bitcast.14, f32[672,128]{1,0:T(8,128)S(1)} %collective-permute-done.6.key_in_ref, ...), custom_call_target="tpu_custom_call" | custom-call | flops 10000000 | bytes 2641920 | tf_op jit(solution)/shard_map/pallas_call | solution.py:527
  (17 shorter events, 0.1 us)
Async XLA Ops:
  2.1 1.8 %collective-permute-start = (f32[680,128]{1,0:T(8,128)S(1)}, f32[680,128]{1,0:T(8,128)S(1)}, u32[]{:S(2)}, u32[]{:S(2)}) collective-permute-start(f32[680,128]{1,0:T(8,128)S(1)} %shard_map.104), channel_id=1, source_target_pairs={{0,1},{1,0},{2,3},{3,2},{4,5},{5,4},{6,7},{7,6},{8,9},{9,8},{10,11... | collective-permute-start | bytes 1044488 | tf_op jit(solution)/shard_map/ppermute | solution.py:146
  3.0 9.1 %copy-start.2 = (bf16[128,1232]{0,1:T(8,128)(2,1)S(1)}, bf16[128,1232]{0,1:T(8,128)(2,1)}, u32[]{:S(2)}) copy-start(bf16[128,1232]{0,1:T(8,128)(2,1)} %param.8) | copy-start | bytes 946180
  4.9 7.3 %copy-start = (bf16[128,1232]{0,1:T(8,128)(2,1)S(1)}, bf16[128,1232]{0,1:T(8,128)(2,1)}, u32[]{:S(2)}) copy-start(bf16[128,1232]{0,1:T(8,128)(2,1)} %param.9) | copy-start | bytes 946180
  4.9 19.1 %all-to-all-start = ((f32[32,1,3072]{2,1,0:T(1,128)}), f32[32,1,3072]{2,1,0:T(1,128)S(1)}, u32[]{:S(2)}, u32[]{:S(2)}) async-start(f32[32,1,3072]{2,1,0:T(1,128)} %shard_map.105), calls=%async_computation | async-start | bytes 786432 | tf_op jit(solution)/shard_map/all_to_all | solution.py:559
  12.1 1.0 %copy-start.1 = (bf16[128,1232]{0,1:T(8,128)(2,1)S(1)}, bf16[128,1232]{0,1:T(8,128)(2,1)}, u32[]{:S(2)}) copy-start(bf16[128,1232]{0,1:T(8,128)(2,1)} %param.10) | copy-start | bytes 946180
  12.1 1.1 %copy-start.3 = (bf16[128,1232]{0,1:T(8,128)(2,1)S(1)}, bf16[128,1232]{0,1:T(8,128)(2,1)}, u32[]{:S(2)}) copy-start(bf16[128,1232]{0,1:T(8,128)(2,1)} %param.11) | copy-start | bytes 946180
  13.2 3.8 %copy-start.6 = (f32[11,112,112]{2,1,0:T(8,128)S(1)}, f32[11,112,112]{2,1,0:T(8,128)}, u32[]{:S(2)}) copy-start(f32[11,112,112]{2,1,0:T(8,128)} %state_in_ref.1) | copy-start | bytes 1655812
  13.2 1.7 %collective-permute-start.4 = (f32[672,128]{1,0:T(8,128)S(1)}, f32[672,128]{1,0:T(8,128)S(1)}, u32[]{:S(2)}, u32[]{:S(2)}) collective-permute-start(f32[672,128]{1,0:T(8,128)S(1)} %dynamic-slice_convert_fusion), channel_id=1, source_target_pairs={{0,1},{1,0},{2,3},{3,2},{4,5},{5,4},{6,7},{7,6},{8,9},{9,8},{10,11... | collective-permute-start | bytes 1032200 | tf_op jit(solution)/shard_map/ppermute | solution.py:146
  13.5 1.9 %collective-permute-start.3 = (f32[672,128]{1,0:T(8,128)S(1)}, f32[672,128]{1,0:T(8,128)S(1)}, u32[]{:S(2)}, u32[]{:S(2)}) collective-permute-start(f32[672,128]{1,0:T(8,128)S(1)} %dynamic-slice_convert_fusion.1), channel_id=1, source_target_pairs={{0,1},{1,0},{2,3},{3,2},{4,5},{5,4},{6,7},{7,6},{8,9},{9,8},{10,11... | collective-permute-start | bytes 1032200 | tf_op jit(solution)/shard_map/ppermute | solution.py:146
  13.8 2.1 %collective-permute-start.2 = (f32[672,128]{1,0:T(8,128)S(1)}, f32[672,128]{1,0:T(8,128)S(1)}, u32[]{:S(2)}, u32[]{:S(2)}) collective-permute-start(f32[672,128]{1,0:T(8,128)S(1)} %dynamic-slice_convert_fusion.2), channel_id=1, source_target_pairs={{0,1},{1,0},{2,3},{3,2},{4,5},{5,4},{6,7},{7,6},{8,9},{9,8},{10,11... | collective-permute-start | bytes 1032200 | tf_op jit(solution)/shard_map/ppermute | solution.py:146
  14.0 2.4 %collective-permute-start.1 = (f32[672,128]{1,0:T(8,128)S(1)}, f32[672,128]{1,0:T(8,128)S(1)}, u32[]{:S(2)}, u32[]{:S(2)}) collective-permute-start(f32[672,128]{1,0:T(8,128)S(1)} %dynamic-slice_convert_fusion.3), channel_id=1, source_target_pairs={{0,1},{1,0},{2,3},{3,2},{4,5},{5,4},{6,7},{7,6},{8,9},{9,8},{10,11... | collective-permute-start | bytes 1032200 | tf_op jit(solution)/shard_map/ppermute | solution.py:146
  16.9 7.0 %copy-start.11 = (f32[11,112]{1,0:T(8,128)S(1)}, f32[11,112]{1,0:T(8,128)}, u32[]{:S(2)}) copy-start(f32[11,112]{1,0:T(8,128)} %norm_in_ref.1) | copy-start | bytes 14788
  18.3 0.8 %copy-start.4 = (f32[2,6,112,112]{3,2,1,0:T(8,128)}, f32[2,6,112,112]{3,2,1,0:T(8,128)S(1)}, u32[]{:S(2)}) copy-start(f32[2,6,112,112]{3,2,1,0:T(8,128)S(1)} %get-tuple-element.60.before_ref) | copy-start | bytes 1806340
  24.5 19.5 %copy-start.5 = (f32[2,6,112,112]{3,2,1,0:T(8,128)S(1)}, f32[2,6,112,112]{3,2,1,0:T(8,128)}, u32[]{:S(2)}) copy-start(f32[2,6,112,112]{3,2,1,0:T(8,128)} %copy-done.4) | copy-start | bytes 1806340
  45.5 16.2 %all-to-all-start.2 = ((f32[32,1,3072]{2,1,0:T(1,128)}), f32[32,1,3072]{2,1,0:T(1,128)S(1)}, u32[]{:S(2)}, u32[]{:S(2)}) async-start(f32[32,1,3072]{2,1,0:T(1,128)} %get-tuple-element.63), calls=%async_computation.2 | async-start | bytes 786432 | tf_op jit(solution)/shard_map/all_to_all | solution.py:559
  49.8 1.7 %copy-start.7 = (f32[11,112,112]{2,1,0:T(8,128)S(1)}, f32[11,112,112]{2,1,0:T(8,128)}, u32[]{:S(2)}) copy-start(f32[11,112,112]{2,1,0:T(8,128)} %grad_state_ref.1) | copy-start | bytes 1655812
  51.2 2.5 %collective-permute-start.5 = (f32[672,128]{1,0:T(8,128)S(1)}, f32[672,128]{1,0:T(8,128)S(1)}, u32[]{:S(2)}, u32[]{:S(2)}) collective-permute-start(f32[672,128]{1,0:T(8,128)S(1)} %get-tuple-element.68), channel_id=1, source_target_pairs={{0,1},{1,0},{2,3},{3,2},{4,5},{5,4},{6,7},{7,6},{8,9},{9,8},{10,11... | collective-permute-start | bytes 1032200 | tf_op jit(solution)/shard_map/ppermute | solution.py:146
  53.1 8.5 %copy-start.10 = (f32[11,112]{1,0:T(8,128)S(1)}, f32[11,112]{1,0:T(8,128)}, u32[]{:S(2)}) copy-start(f32[11,112]{1,0:T(8,128)} %grad_norm_ref.3) | copy-start | bytes 14788
  53.1 1.7 %collective-permute-start.6 = (f32[672,128]{1,0:T(8,128)S(1)}, f32[672,128]{1,0:T(8,128)S(1)}, u32[]{:S(2)}, u32[]{:S(2)}) collective-permute-start(f32[672,128]{1,0:T(8,128)S(1)} %get-tuple-element.72), channel_id=1, source_target_pairs={{0,1},{1,0},{2,3},{3,2},{4,5},{5,4},{6,7},{7,6},{8,9},{9,8},{10,11... | collective-permute-start | bytes 1032200 | tf_op jit(solution)/shard_map/ppermute | solution.py:146
  53.4 1.9 %collective-permute-start.7 = (f32[672,128]{1,0:T(8,128)S(1)}, f32[672,128]{1,0:T(8,128)S(1)}, u32[]{:S(2)}, u32[]{:S(2)}) collective-permute-start(f32[672,128]{1,0:T(8,128)S(1)} %get-tuple-element.73), channel_id=1, source_target_pairs={{0,1},{1,0},{2,3},{3,2},{4,5},{5,4},{6,7},{7,6},{8,9},{9,8},{10,11... | collective-permute-start | bytes 1032200 | tf_op jit(solution)/shard_map/ppermute | solution.py:146
  55.3 0.7 %copy-start.8 = (f32[672,128]{1,0:T(8,128)}, f32[672,128]{1,0:T(8,128)S(1)}, u32[]{:S(2)}) copy-start(f32[672,128]{1,0:T(8,128)S(1)} %collective-permute-done.7.value_in_ref) | copy-start | bytes 1032196
  61.8 2.6 %collective-permute-start.8 = (f32[680,128]{1,0:T(8,128)S(1)}, f32[680,128]{1,0:T(8,128)S(1)}, u32[]{:S(2)}, u32[]{:S(2)}) collective-permute-start(f32[680,128]{1,0:T(8,128)S(1)} %shard_map.113), channel_id=1, source_target_pairs={{0,1},{1,0},{2,3},{3,2},{4,5},{5,4},{6,7},{7,6},{8,9},{9,8},{10,11... | collective-permute-start | bytes 1044488 | tf_op jit(solution)/shard_map/ppermute | solution.py:146
  63.1 1.3 %copy-start.9 = (f32[672,128]{1,0:T(8,128)S(1)}, f32[672,128]{1,0:T(8,128)}, u32[]{:S(2)}) copy-start(f32[672,128]{1,0:T(8,128)} %copy-done.8) | copy-start | bytes 1032196

commit v9 on v8

--- a/solution.py
+++ b/solution.py
@@ -373,11 +373,12 @@
 
 
 def outputs_grad(
-    plan, in_ref, before_ref, a_ref, g_ref, inverse_ref, inner_ref,
+    plan, sends, in_ref, before_ref, a_ref, g_ref, inverse_ref, inner_ref,
     out_ref, product_ref, c_ref, m_ref,
 ):
     first, _, third = plan.areas()
     scan_rows(plan, in_ref, plan.full * LANES, out_ref, True)
+    sends.flush(LANES, plan.span - LANES)
     totals = []
     for h in range(plan.half):
         base = load_rows(plan, in_ref, first, h)
@@ -398,6 +399,8 @@
         totals.append(total)
     totals += [jnp.zeros((1, LANES), F32)] * (plan.extra - plan.half)
     store_norms(plan, out_ref, jnp.concatenate(totals, axis=0), third)
+    sends.flush(0, LANES)
+    sends.flush(plan.span, plan.norm_slots * LANES)
 
 
 def query_grads(
@@ -463,10 +466,20 @@
 
 
 def other_suffix(plan, in_ref, after_ref, grad_norm_ref, m_ref, out_ref):
-    out_ref[plan.rows :, :] = suffix_norms(plan, in_ref, grad_norm_ref, m_ref, 1)
+    core, count, width = my_core(), plan.shift, plan.width
+    out_ref[count * width :, :] = suffix_norms(plan, in_ref, grad_norm_ref, m_ref, 1)
     for h in range(plan.half):
-        rows = slice(h * plan.width, (h + 1) * plan.width)
-        out_ref[rows, :] = wide(load_rows(plan, in_ref, plan.areas()[2], h) + after_ref[h])
+        state = wide(load_rows(plan, in_ref, plan.areas()[2], h) + after_ref[h])
+        at = h - core * (plan.half - count)
+
+        def store():
+            start = pl.multiple_of(jnp.clip(at, 0, count - 1) * width, 16)
+            out_ref[pl.ds(start, width), :] = state
+
+        if plan.half - count <= h < count:
+            store()
+        else:
+            pl.when((at >= 0) & (at < count))(store)
 
 
 def own_grads(
@@ -492,13 +505,14 @@
     key_ref[pl.ds(own, plan.rows), :] = own_key_ref[...]
     value_ref[pl.ds(own, plan.rows), :] = own_value_ref[...]
     skip = (1 - core) * (plan.half - count)
-    norms = got_ref[pl.ds(plan.rows + skip, count), :]
+    norms = got_ref[pl.ds(count * width + skip, count), :]
     columns = jnp.concatenate([norms, jnp.zeros((plan.extra - count, LANES), F32)], axis=0).T
     for t in range(count):
         source = pl.ds(pl.multiple_of((skip + t) * width, 16), width)
         rows = pl.ds(pl.multiple_of((1 - core) * plan.rows + t * width, 16), width)
         b, v = relu(k_ref[rows, :]), v_ref[rows, :]
-        key, value = key_value(got_ref[source, :][:, :width], columns[:width, t : t + 1], b, v)
+        state = got_ref[t * width : (t + 1) * width, :][:, :width]
+        key, value = key_value(state, columns[:width, t : t + 1], b, v)
         key_ref[rows, :] = (key + key_in_ref[source, :]).astype(BF16)
         value_ref[rows, :] = (value + value_in_ref[source, :]).astype(BF16)
 
@@ -519,17 +533,50 @@
         out_ref[pl.ds(other, rest), :] = got.astype(BF16)
 
 
-def call(body, outs, args, room=FREE, flops=10_000_000, scratch=()):
-    smem = pl.BlockSpec(memory_space=pltpu.SMEM)
+class Sends:
+    def __init__(self, buffer, target, sems):
+        self.buffer, self.target, self.sems, self.copies = buffer, target, sems, []
+
+    def flush(self, start, count):
+        at = slice(None), slice(None), pl.ds(start, count)
+        sem = self.sems.at[len(self.copies)]
+        copy = pltpu.make_async_copy(self.buffer.at[at], self.target.at[at], sem)
+        copy.start()
+        self.copies.append(copy)
+
+    def finish(self):
+        for copy in self.copies:
+            copy.wait()
+
+
+def call(body, outs, args, room=FREE, flops=10_000_000, send=False, reuse=None):
     vmem = pl.BlockSpec(memory_space=pltpu.VMEM)
-    in_specs = [smem if x.ndim == 1 else vmem for x in args]
+    anywhere = pl.BlockSpec(memory_space=pl.ANY)
     moved = sum(x.size * x.dtype.itemsize for x in (*args, *outs))
+    in_specs, out_specs, scratch, kernel = [vmem] * len(args), [vmem] * len(outs), [], body
+    aliases = {}
+    count = len(args)
+    if send:
+        out_specs[0] = anywhere
+        scratch = [pltpu.VMEM(outs[0].shape, outs[0].dtype), pltpu.SemaphoreType.DMA((4,))]
+        if reuse is not None:
+            args, in_specs = (*args, reuse), [*in_specs, anywhere]
+            aliases = {count: 0}
+
+        def kernel(*refs):
+            ins, refs = refs[:count], refs[len(args) :]
+            out_refs, (buffer, sems) = refs[: len(outs)], refs[len(outs) :]
+            sends = Sends(buffer, out_refs[0], sems)
+            body(sends, *ins, buffer, *out_refs[1:])
+            sends.finish()
+
     return pl.pallas_call(
-        body,
+        kernel,
         out_shape=outs,
         in_specs=in_specs,
-        out_specs=[vmem] * len(outs),
-        scratch_shapes=list(scratch),
+        out_specs=out_specs,
+        scratch_shapes=scratch,
+        input_output_aliases=aliases,
         compiler_params=pltpu.CompilerParams(vmem_limit_bytes=VMEM_BYTES - room),
         cost_estimate=pl.CostEstimate(flops=flops, bytes_accessed=moved, transcendentals=0),
     )(*args)
@@ -578,6 +625,7 @@
     block_got = pair_swap(send)
     (block_own,) = call(functools.partial(block_state, plan, False), (block,), (keys_values,))
     (sent,) = call(bind(chip_state), (sent_single,), (block_own, block_got))
+    first_sent = sent
     sent, k, v, q, g = lax.optimization_barrier((sent, k, v, q, g))
     got = exchange(sent)
     a, b, v, g, sums, norm = call(
@@ -597,6 +645,8 @@
         bind(outputs_grad),
         (sent_single, products, rows, rows),
         (got, before, a, g, inverse, inner),
+        send=True,
+        reuse=first_sent,
     )
     got = exchange(sent)
     query, query_send, mixed, a, u = call(
@@ -612,7 +662,8 @@
     whole = shape((heads * width, length), BF16)
     (query_grad,) = call(functools.partial(assemble, plan, 1), (whole,), (query, query_got))
     got, query_grad, inner_got = lax.optimization_barrier((got, query_grad, inner_got))
-    (send,) = call(bind(other_suffix), (block,), (got, finals[3], grad_norm, m))
+    rest = shape((plan.shift * width + plan.extra, LANES))
+    (send,) = call(bind(other_suffix), (rest,), (got, finals[3], grad_norm, m))
     rest_got = pair_swap(send)
     own_tokens = shape((plan.rows, length), BF16)
     key, value = call(

time: 66 us -> 65.9 us (level)
  no operation moved by 1% of the time
where the time goes in v9:
time: 65.9 us; the launch traced here: 65.6 us
  blocking collectives  19.4 us (29%)
  starting transfers between devices  15.3 us (23%)
  waiting for transfers between devices  14.8 us (22%)
  Pallas kernels  11.4 us (17%)
  local copies, waits for them, and re-layouts  2.54 us (4%)
  other arithmetic  1.22 us (2%)
  between operations  0.83 us (1%)
    all_to_all x1, blocking collectives, exchange(): return lax.all_to_all(x, both, 0, 0, tiled=True)  19.4 us
    all_to_all x2, starting transfers between devices, exchange(): return lax.all_to_all(x, both, 0, 0, tiled=True)  11.5 us
    pallas_call x13, Pallas kernels, call(): pl.pallas_call(kernel, out_shape=outs, in_specs=in_specs, out_specs=out_s...  11.4 us
    all_to_all x2, waiting for transfers between devices, exchange(): return lax.all_to_all(x, both, 0, 0, tiled=True)  10.4 us
    ppermute x9, waiting for transfers between devices, pair_swap(): return lax.ppermute(x, 'seq', [(i, i ^ 1) for i in range(size)])  4.45 us
    ppermute x9, starting transfers between devices, pair_swap(): return lax.ppermute(x, 'seq', [(i, i ^ 1) for i in range(size)])  3.82 us
    unnamed x24, local copies, waits for them, and re-layouts  2.54 us
  transfers between devices with their start and end apart: 11, of which 10 were waited for; matrix products, arithmetic and copies ran while one was open for 0% of the time, Pallas kernels for 10%

profile of v9, /device:TPU:0, one launch (start us, length us, event | category | flops | bytes accessed | tf_op | source)
XLA Modules:
  0.0 65.6 jit_solution(4443680435967128738)
XLA Ops:
  0.6 1.1 %pad_maximum_fusion.kv_ref = bf16[2464,128]{1,0:T(8,128)(2,1)S(1)} fusion(bf16[1232,128]{1,0:T(8,128)(2,1)} %bitcast.11, bf16[1232,128]{1,0:T(8,128)(2,1)} %bitcast.7), kind=kLoop, calls=%fused_computation | loop fusion | flops 1261568 | bytes 1261568 | tf_op jit(solution)/shard_map/concatenate | solution.py:623
  1.7 0.3 shard_map.104
  2.1 0.6 collective-permute-start
  2.6 0.3 shard_map.103.own_ref
  3.0 0.0 copy-start.2
  3.0 0.9 %collective-permute-done.got_ref = f32[680,128]{1,0:T(8,128)S(1)} collective-permute-done((f32[680,128]{1,0:T(8,128)S(1)}, f32[680,128]{1,0:T(8,128)S(1)}, u32[]{:S(2)}, u32[]{:S(2)}) %collective-permute-start) | collective-permute-done | bytes 348192 | tf_op jit(solution)/shard_map/ppermute | solution.py:146
  3.9 0.9 %shard_map.105.refs_6_ = f32[32,1,3072]{2,1,0:T(1,128)} custom-call(f32[680,128]{1,0:T(8,128)S(1)} %shard_map.103.own_ref, f32[680,128]{1,0:T(8,128)S(1)} %collective-permute-done.got_ref), custom_call_target="tpu_custom_call" | custom-call | flops 10000000 | bytes 1089536 | tf_op jit(solution)/shard_map/pallas_call | solution.py:573
  4.9 7.2 %all-to-all-start = ((f32[32,1,3072]{2,1,0:T(1,128)}), f32[32,1,3072]{2,1,0:T(1,128)S(1)}, u32[]{:S(2)}, u32[]{:S(2)}) async-start(f32[32,1,3072]{2,1,0:T(1,128)} %shard_map.105.refs_6_), calls=%async_computation | async-start | bytes 786432 | tf_op jit(solution)/shard_map/all_to_all | solution.py:606
  12.1 0.0 copy-start.1
  12.1 0.0 copy-start.3
  12.2 0.9 %copy-done.1 = bf16[128,1232]{0,1:T(8,128)(2,1)S(1)} copy-done((bf16[128,1232]{0,1:T(8,128)(2,1)S(1)}, bf16[128,1232]{0,1:T(8,128)(2,1)}, u32[]{:S(2)}) %copy-start.1) | copy-done | bytes 315416
  13.1 0.1 copy-done.3
  13.2 0.0 copy-start.6
  13.2 0.3 collective-permute-start.4
  13.5 0.3 collective-permute-start.3
  13.8 0.3 collective-permute-start.2
  14.0 0.3 collective-permute-start.1
  14.3 0.6 collective-permute-done.4.g_got_ref
  14.9 0.5 collective-permute-done.3.v_got_ref
  15.4 0.5 collective-permute-done.2.k_got_ref
  15.9 0.5 collective-permute-done.1.q_got_ref
  16.4 0.5 shard_map.106
  16.9 0.0 copy-start.11
  16.9 1.3 %shard_map.107 = (f32[2,6,112,112]{3,2,1,0:T(8,128)S(1)}, f32[2,8,128]{2,1,0:T(8,128)S(1)}) custom-call(bf16[2,6,112,128]{3,2,1,0:T(8,128)(2,1)S(1)} %get-tuple-element.50.a_ref.refs_2_, bf16[2,6,112,128]{3,2,1,0:T(8,128)(2,1)S(1)} %get-tuple-element.51.b_ref, bf16[2,6,112,128]{3,2,1,0:T(8,128)(2,1)S(1)} %get-tuple-element.52.v_ref, ...), custom_call_target="tpu_custom_call" | custom-call | flops 10000000 | bytes 2538496 | tf_op jit(solution)/shard_map/pallas_call | solution.py:573
  18.3 0.8 %copy-done.4 = f32[2,6,112,112]{3,2,1,0:T(8,128)} copy-done((f32[2,6,112,112]{3,2,1,0:T(8,128)}, f32[2,6,112,112]{3,2,1,0:T(8,128)S(1)}, u32[]{:S(2)}) %copy-start.4) | copy-done | bytes 602136
  19.1 4.8 %all-to-all-done.in_ref = f32[32,1,3072]{2,1,0:T(1,128)S(1)} async-done(((f32[32,1,3072]{2,1,0:T(1,128)}), f32[32,1,3072]{2,1,0:T(1,128)S(1)}, u32[]{:S(2)}, u32[]{:S(2)}) %all-to-all-start) | async-done | bytes 393248 | tf_op jit(solution)/shard_map/all_to_all | solution.py:606
  23.9 0.6 shard_map.108
  24.5 19.4 %all_to_all.15.refs_0_ = f32[32,1,4736]{2,1,0:T(1,128)S(1)} all-to-all(f32[32,1,4736]{2,1,0:T(1,128)S(1)} %get-tuple-element.59), channel_id=1, replica_groups=mesh['grp'=4,'seq'=8] {'seq','grp'}, dimensions={0} | all-to-all | bytes 1212416 | tf_op jit(solution)/shard_map/all_to_all | solution.py:606
  44.0 1.5 %shard_map.109 = (f32[32,1,3072]{2,1,0:T(1,128)}, f32[2,6,112,128]{3,2,1,0:T(8,128)S(1)}, f32[2,8,128]{2,1,0:T(8,128)S(1)}, f32[2,8,128]{2,1,0:T(8,128)S(1)}) custom-call(f32[32,1,4736]{2,1,0:T(1,128)S(1)} %all_to_all.15.refs_0_, f32[2,6,112,112]{3,2,1,0:T(8,128)S(1)} %copy-done.5, ...), custom_call_target="tpu_custom_call", output_to_operand_aliasing={{0}: (6, {})} | custom-call | flops 10000000 | bytes 3010560 | tf_op jit(solution)/shard_map/pallas_call | solution.py:573
  45.4 4.3 %all-to-all-start.2 = ((f32[32,1,3072]{2,1,0:T(1,128)}), f32[32,1,3072]{2,1,0:T(1,128)S(1)}, u32[]{:S(2)}, u32[]{:S(2)}) async-start(f32[32,1,3072]{2,1,0:T(1,128)} %get-tuple-element.63), calls=%async_computation.2 | async-start | bytes 786432 | tf_op jit(solution)/shard_map/all_to_all | solution.py:606
  49.8 0.0 copy-start.7
  49.8 1.4 %shard_map.110 = (f32[672,128]{1,0:T(8,128)S(1)}, f32[672,128]{1,0:T(8,128)S(1)}, bf16[2,6,128,128]{3,2,1,0:T(8,128)(2,1)S(1)}, bf16[2,6,112,128]{3,2,1,0:T(8,128)(2,1)S(1)}, bf16[2,6,112,128]{3,2,1,0:T(8,128)(2,1)S(1)}) custom-call(bf16[2,6,112,128]{3,2,1,0:T(8,128)(2,1)S(1)} %get-tuple-element.50.a_ref.refs_2_, ...), custom_call_target="tpu_custom_call" | custom-call | flops 10000000 | bytes 3858432 | tf_op jit(solution)/shard_map/pallas_call | solution.py:573
  51.2 0.3 collective-permute-start.5
  51.5 1.6 %shard_map.112 = (f32[6,112,112]{2,1,0:T(8,128)S(1)}, f32[672,128]{1,0:T(8,128)S(1)}, f32[672,128]{1,0:T(8,128)S(1)}, f32[6,112,112]{2,1,0:T(8,128)S(1)}, f32[67...) custom-call(bf16[2,6,112,128]{3,2,1,0:T(8,128)(2,1)S(1)} %get-tuple-element.69.a_ref, ...), custom_call_target="tpu_custom_call" | custom-call | flops 10000000 | bytes 3955712 | tf_op jit(solution)/shard_map/pallas_call | solution.py:573
  53.1 0.0 copy-start.10
  53.1 0.3 collective-permute-start.6
  53.4 0.3 collective-permute-start.7
  53.7 0.0 collective-permute-done.5.refs_1_
  53.7 0.8 %shard_map.111 = bf16[1232,128]{1,0:T(8,128)(2,1)} custom-call(f32[672,128]{1,0:T(8,128)S(1)} %get-tuple-element.67.refs_0_, f32[672,128]{1,0:T(8,128)S(1)} %collective-permute-done.5.refs_1_), custom_call_target="tpu_custom_call" | custom-call | flops 10000000 | bytes 1003520 | tf_op jit(solution)/shard_map/pallas_call | solution.py:573
  54.4 0.4 collective-permute-done.6.key_in_ref
  54.8 0.5 collective-permute-done.7.value_in_ref
  55.3 0.7 %copy-done.8 = f32[672,128]{1,0:T(8,128)} copy-done((f32[672,128]{1,0:T(8,128)}, f32[672,128]{1,0:T(8,128)S(1)}, u32[]{:S(2)}) %copy-start.8) | copy-done | bytes 344088
  56.0 5.6 %all-to-all-done.2.in_ref = f32[32,1,3072]{2,1,0:T(1,128)S(1)} async-done(((f32[32,1,3072]{2,1,0:T(1,128)}), f32[32,1,3072]{2,1,0:T(1,128)S(1)}, u32[]{:S(2)}, u32[]{:S(2)}) %all-to-all-start.2) | async-done | bytes 393248 | tf_op jit(solution)/shard_map/all_to_all | solution.py:606
  61.6 0.3 shard_map.113
  61.9 1.3 %collective-permute-start.8 = (f32[568,128]{1,0:T(8,128)S(1)}, f32[568,128]{1,0:T(8,128)S(1)}, u32[]{:S(2)}, u32[]{:S(2)}) collective-permute-start(f32[568,128]{1,0:T(8,128)S(1)} %shard_map.113), channel_id=1, source_target_pairs={{0,1},{1,0},{2,3},{3,2},{4,5},{5,4},{6,7},{7,6},{8,9},{9,8},{10,11... | collective-permute-start | bytes 872456 | tf_op jit(solution)/shard_map/ppermute | solution.py:146
  63.2 0.7 %shard_map.114 = (bf16[672,128]{1,0:T(8,128)(2,1)S(1)}, bf16[672,128]{1,0:T(8,128)(2,1)S(1)}) custom-call(f32[32,1,3072]{2,1,0:T(1,128)S(1)} %all-to-all-done.2.in_ref, f32[6,112,112]{2,1,0:T(8,128)S(1)} %get-tuple-element.80.after_ref, f32[11,112]{1,0:T(8,128)S(1)} %copy-done.10, f32[2,8,128]{2,1,0:T(8,128)S(1)} %get-tuple-element.77.m_ref, ...), custom_call_target="tpu_custom_call" | custom-call | flops 10000000 | bytes 2427712 | tf_op jit(solution)/shard_map/pallas_call | solution.py:573
  63.8 0.5 collective-permute-done.8.got_ref
  64.4 1.2 %shard_map.115 = (bf16[1232,128]{1,0:T(8,128)(2,1)}, bf16[1232,128]{1,0:T(8,128)(2,1)}) custom-call(f32[568,128]{1,0:T(8,128)S(1)} %collective-permute-done.8.got_ref, bf16[1232,128]{1,0:T(8,128)(2,1)S(1)} %bitcast.10, bf16[1232,128]{1,0:T(8,128)(2,1)S(1)} %bitcast.14, f32[672,128]{1,0:T(8,128)S(1)} %collective-permute-done.6.key_in_ref, ...), custom_call_target="tpu_custom_call" | custom-call | flops 10000000 | bytes 2584576 | tf_op jit(solution)/shard_map/pallas_call | solution.py:573
  (17 shorter events, 0.1 us)
Async XLA Ops:
  2.1 1.8 %collective-permute-start = (f32[680,128]{1,0:T(8,128)S(1)}, f32[680,128]{1,0:T(8,128)S(1)}, u32[]{:S(2)}, u32[]{:S(2)}) collective-permute-start(f32[680,128]{1,0:T(8,128)S(1)} %shard_map.104), channel_id=1, source_target_pairs={{0,1},{1,0},{2,3},{3,2},{4,5},{5,4},{6,7},{7,6},{8,9},{9,8},{10,11... | collective-permute-start | bytes 1044488 | tf_op jit(solution)/shard_map/ppermute | solution.py:146
  3.0 9.1 %copy-start.2 = (bf16[128,1232]{0,1:T(8,128)(2,1)S(1)}, bf16[128,1232]{0,1:T(8,128)(2,1)}, u32[]{:S(2)}) copy-start(bf16[128,1232]{0,1:T(8,128)(2,1)} %param.8) | copy-start | bytes 946180
  4.9 7.3 %copy-start = (bf16[128,1232]{0,1:T(8,128)(2,1)S(1)}, bf16[128,1232]{0,1:T(8,128)(2,1)}, u32[]{:S(2)}) copy-start(bf16[128,1232]{0,1:T(8,128)(2,1)} %param.9) | copy-start | bytes 946180
  4.9 19.1 %all-to-all-start = ((f32[32,1,3072]{2,1,0:T(1,128)}), f32[32,1,3072]{2,1,0:T(1,128)S(1)}, u32[]{:S(2)}, u32[]{:S(2)}) async-start(f32[32,1,3072]{2,1,0:T(1,128)} %shard_map.105.refs_6_), calls=%async_computation | async-start | bytes 786432 | tf_op jit(solution)/shard_map/all_to_all | solution.py:606
  12.1 1.0 %copy-start.1 = (bf16[128,1232]{0,1:T(8,128)(2,1)S(1)}, bf16[128,1232]{0,1:T(8,128)(2,1)}, u32[]{:S(2)}) copy-start(bf16[128,1232]{0,1:T(8,128)(2,1)} %param.10) | copy-start | bytes 946180
  12.1 1.1 %copy-start.3 = (bf16[128,1232]{0,1:T(8,128)(2,1)S(1)}, bf16[128,1232]{0,1:T(8,128)(2,1)}, u32[]{:S(2)}) copy-start(bf16[128,1232]{0,1:T(8,128)(2,1)} %param.11) | copy-start | bytes 946180
  13.2 3.8 %copy-start.6 = (f32[11,112,112]{2,1,0:T(8,128)S(1)}, f32[11,112,112]{2,1,0:T(8,128)}, u32[]{:S(2)}) copy-start(f32[11,112,112]{2,1,0:T(8,128)} %state_in_ref.1) | copy-start | bytes 1655812
  13.2 1.7 %collective-permute-start.4 = (f32[672,128]{1,0:T(8,128)S(1)}, f32[672,128]{1,0:T(8,128)S(1)}, u32[]{:S(2)}, u32[]{:S(2)}) collective-permute-start(f32[672,128]{1,0:T(8,128)S(1)} %dynamic-slice_convert_fusion), channel_id=1, source_target_pairs={{0,1},{1,0},{2,3},{3,2},{4,5},{5,4},{6,7},{7,6},{8,9},{9,8},{10,11... | collective-permute-start | bytes 1032200 | tf_op jit(solution)/shard_map/ppermute | solution.py:146
  13.5 1.9 %collective-permute-start.3 = (f32[672,128]{1,0:T(8,128)S(1)}, f32[672,128]{1,0:T(8,128)S(1)}, u32[]{:S(2)}, u32[]{:S(2)}) collective-permute-start(f32[672,128]{1,0:T(8,128)S(1)} %dynamic-slice_convert_fusion.1), channel_id=1, source_target_pairs={{0,1},{1,0},{2,3},{3,2},{4,5},{5,4},{6,7},{7,6},{8,9},{9,8},{10,11... | collective-permute-start | bytes 1032200 | tf_op jit(solution)/shard_map/ppermute | solution.py:146
  13.8 2.1 %collective-permute-start.2 = (f32[672,128]{1,0:T(8,128)S(1)}, f32[672,128]{1,0:T(8,128)S(1)}, u32[]{:S(2)}, u32[]{:S(2)}) collective-permute-start(f32[672,128]{1,0:T(8,128)S(1)} %dynamic-slice_convert_fusion.2), channel_id=1, source_target_pairs={{0,1},{1,0},{2,3},{3,2},{4,5},{5,4},{6,7},{7,6},{8,9},{9,8},{10,11... | collective-permute-start | bytes 1032200 | tf_op jit(solution)/shard_map/ppermute | solution.py:146
  14.0 2.4 %collective-permute-start.1 = (f32[672,128]{1,0:T(8,128)S(1)}, f32[672,128]{1,0:T(8,128)S(1)}, u32[]{:S(2)}, u32[]{:S(2)}) collective-permute-start(f32[672,128]{1,0:T(8,128)S(1)} %dynamic-slice_convert_fusion.3), channel_id=1, source_target_pairs={{0,1},{1,0},{2,3},{3,2},{4,5},{5,4},{6,7},{7,6},{8,9},{9,8},{10,11... | collective-permute-start | bytes 1032200 | tf_op jit(solution)/shard_map/ppermute | solution.py:146
  16.9 7.0 %copy-start.11 = (f32[11,112]{1,0:T(8,128)S(1)}, f32[11,112]{1,0:T(8,128)}, u32[]{:S(2)}) copy-start(f32[11,112]{1,0:T(8,128)} %norm_in_ref.1) | copy-start | bytes 14788
  18.3 0.8 %copy-start.4 = (f32[2,6,112,112]{3,2,1,0:T(8,128)}, f32[2,6,112,112]{3,2,1,0:T(8,128)S(1)}, u32[]{:S(2)}) copy-start(f32[2,6,112,112]{3,2,1,0:T(8,128)S(1)} %get-tuple-element.60.refs_1_) | copy-start | bytes 1806340
  24.5 19.5 %copy-start.5 = (f32[2,6,112,112]{3,2,1,0:T(8,128)S(1)}, f32[2,6,112,112]{3,2,1,0:T(8,128)}, u32[]{:S(2)}) copy-start(f32[2,6,112,112]{3,2,1,0:T(8,128)} %copy-done.4) | copy-start | bytes 1806340
  45.4 16.2 %all-to-all-start.2 = ((f32[32,1,3072]{2,1,0:T(1,128)}), f32[32,1,3072]{2,1,0:T(1,128)S(1)}, u32[]{:S(2)}, u32[]{:S(2)}) async-start(f32[32,1,3072]{2,1,0:T(1,128)} %get-tuple-element.63), calls=%async_computation.2 | async-start | bytes 786432 | tf_op jit(solution)/shard_map/all_to_all | solution.py:606
  49.8 1.7 %copy-start.7 = (f32[11,112,112]{2,1,0:T(8,128)S(1)}, f32[11,112,112]{2,1,0:T(8,128)}, u32[]{:S(2)}) copy-start(f32[11,112,112]{2,1,0:T(8,128)} %grad_state_ref.1) | copy-start | bytes 1655812
  51.2 2.5 %collective-permute-start.5 = (f32[672,128]{1,0:T(8,128)S(1)}, f32[672,128]{1,0:T(8,128)S(1)}, u32[]{:S(2)}, u32[]{:S(2)}) collective-permute-start(f32[672,128]{1,0:T(8,128)S(1)} %get-tuple-element.68), channel_id=1, source_target_pairs={{0,1},{1,0},{2,3},{3,2},{4,5},{5,4},{6,7},{7,6},{8,9},{9,8},{10,11... | collective-permute-start | bytes 1032200 | tf_op jit(solution)/shard_map/ppermute | solution.py:146
  53.1 8.5 %copy-start.10 = (f32[11,112]{1,0:T(8,128)S(1)}, f32[11,112]{1,0:T(8,128)}, u32[]{:S(2)}) copy-start(f32[11,112]{1,0:T(8,128)} %grad_norm_ref.3) | copy-start | bytes 14788
  53.1 1.7 %collective-permute-start.6 = (f32[672,128]{1,0:T(8,128)S(1)}, f32[672,128]{1,0:T(8,128)S(1)}, u32[]{:S(2)}, u32[]{:S(2)}) collective-permute-start(f32[672,128]{1,0:T(8,128)S(1)} %get-tuple-element.72), channel_id=1, source_target_pairs={{0,1},{1,0},{2,3},{3,2},{4,5},{5,4},{6,7},{7,6},{8,9},{9,8},{10,11... | collective-permute-start | bytes 1032200 | tf_op jit(solution)/shard_map/ppermute | solution.py:146
  53.4 1.9 %collective-permute-start.7 = (f32[672,128]{1,0:T(8,128)S(1)}, f32[672,128]{1,0:T(8,128)S(1)}, u32[]{:S(2)}, u32[]{:S(2)}) collective-permute-start(f32[672,128]{1,0:T(8,128)S(1)} %get-tuple-element.73), channel_id=1, source_target_pairs={{0,1},{1,0},{2,3},{3,2},{4,5},{5,4},{6,7},{7,6},{8,9},{9,8},{10,11... | collective-permute-start | bytes 1032200 | tf_op jit(solution)/shard_map/ppermute | solution.py:146
  55.3 0.7 %copy-start.8 = (f32[672,128]{1,0:T(8,128)}, f32[672,128]{1,0:T(8,128)S(1)}, u32[]{:S(2)}) copy-start(f32[672,128]{1,0:T(8,128)S(1)} %collective-permute-done.7.value_in_ref) | copy-start | bytes 1032196
  61.9 2.5 %collective-permute-start.8 = (f32[568,128]{1,0:T(8,128)S(1)}, f32[568,128]{1,0:T(8,128)S(1)}, u32[]{:S(2)}, u32[]{:S(2)}) collective-permute-start(f32[568,128]{1,0:T(8,128)S(1)} %shard_map.113), channel_id=1, source_target_pairs={{0,1},{1,0},{2,3},{3,2},{4,5},{5,4},{6,7},{7,6},{8,9},{9,8},{10,11... | collective-permute-start | bytes 872456 | tf_op jit(solution)/shard_map/ppermute | solution.py:146
  63.2 1.2 %copy-start.9 = (f32[672,128]{1,0:T(8,128)S(1)}, f32[672,128]{1,0:T(8,128)}, u32[]{:S(2)}) copy-start(f32[672,128]{1,0:T(8,128)} %copy-done.8) | copy-start | bytes 1032196
